TPU v7x, 512 devices: a whole 4x8x8 slice. The times are simulated.
512 devices in a mesh: grp: 16 (over y, core), tbl: 32 (over x, z).
Axes of the slice: x: 4, y: 8, z: 8, core: 2. Of those that a mesh axis runs over, the one named last changes fastest.
Arguments:
- dense_feats: bfloat16 [16384, 13], P(('grp', 'tbl')), may hold values from -6 to 6
- sparse_ids: int32 [26, 16384, 8], P(None, 'grp'), may hold values from 0 to 2047
- lengths: int32 [26, 16384], P(None, 'grp'), may hold values from 1 to 8
- table_map: int32 [26], replicated, may hold values from 0 to 63, as said below
- row_perm: int32 [16384], P(('grp', 'tbl')), may hold values from 0 to 16383, as said below
- tables: bfloat16 [64, 2048, 128], P('tbl'), may hold values from -2 to 2
- bottom_one: bfloat16 [13, 512], replicated, may hold values from -1.75 to 1.75
- bottom_two: bfloat16 [512, 256], replicated, may hold values from -0.25 to 0.25
- bottom_three: bfloat16 [256, 128], replicated, may hold values from -0.375 to 0.375
- top_one: bfloat16 [480, 4096], P(None, 'grp'), may hold values from -0.25 to 0.25
- top_two: bfloat16 [4096, 2048], P('grp'), may hold values from -0.09375 to 0.09375
- top_out: bfloat16 [2048], replicated, may hold values from -0.125 to 0.125
Outputs:
- probs: float32 [2, 16384], P(None, ('grp', 'tbl'))
Inputs may be any that keep to these rules, and one draw needn't show every extreme that they name: `table_map`: distinct slots; no device of tbl holds more than 2 of the features' tables, and one holds exactly 2. A permutation of the rows; b and row_perm[b] have the same value of (b // 32) % 32.
All inputs are finite; a program needn't handle non-finite values.
Results may differ from a plain program's by a relative error of at most 0.0065.
Values may be sent and summed in bfloat16 or wider, within the bound.
No kernel may reach another device: no remote copies, remote signals or barrier semaphores. Data moves between devices by JAX's collectives and lax.ppermute only.
A program may use at most 64 MiB of HBM per device.

v0:
```python
import jax
import jax.numpy as jnp
from jax import lax
from jax.sharding import PartitionSpec as P

NPERM = 4


def dense_layer(inputs, weights):
    return jnp.maximum(jnp.dot(inputs, weights, preferred_element_type=jnp.float32), 0.0).astype(
        jnp.bfloat16
    )


def second_layer(source, top_two):
    return jnp.dot(source, top_two, preferred_element_type=jnp.float32)


def lower_pairs(gram):
    vec_count = gram.shape[1]
    return jnp.concatenate([gram[:, level, :level] for level in range(1, vec_count)], axis=1)


def make_codes(vectors, lead_cols, zero_col):
    gram = jnp.einsum("ird,jrd->rij", vectors, vectors, preferred_element_type=jnp.float32)
    return jnp.concatenate([lead_cols, lower_pairs(gram), zero_col], axis=1).astype(jnp.bfloat16)


def local(
    dense_feats,
    sparse_ids,
    lengths,
    table_map,
    row_perm,
    tables,
    bottom_one,
    bottom_two,
    bottom_three,
    top_one,
    top_two,
    top_out,
):
    groups = lax.axis_size("grp")
    owners = lax.axis_size("tbl")
    owner_idx = lax.axis_index("tbl")
    slot_count = tables.shape[0]
    vocab_size = tables.shape[1]
    row_count = dense_feats.shape[0]
    bag_len = sparse_ids.shape[2]
    slot_index = owner_idx * slot_count + jnp.arange(slot_count, dtype=jnp.int32)
    owned_slots = (table_map[None, :] == slot_index[:, None]).astype(jnp.int32)
    slot_ids = jnp.sum(owned_slots[:, :, None, None] * sparse_ids[None], axis=1)
    slot_len = jnp.sum(owned_slots[:, :, None] * lengths[None], axis=1)
    bag_pos = jnp.arange(bag_len, dtype=jnp.int32)
    vocab_pos = jnp.arange(vocab_size, dtype=jnp.int32)
    pooled_list = []
    for slot_pos in range(slot_count):
        bag_mask = (bag_pos[None, :] < slot_len[slot_pos][:, None]).astype(jnp.float32)
        hits = (slot_ids[slot_pos][:, :, None] == vocab_pos[None, None, :]).astype(jnp.float32)
        counts = jnp.sum(hits * bag_mask[:, :, None], axis=1).astype(jnp.bfloat16)
        pooled_list.append(
            jnp.dot(counts, tables[slot_pos], preferred_element_type=jnp.float32).astype(
                jnp.bfloat16
            )
        )
    pooled = jnp.stack(pooled_list, axis=0)
    arrived = lax.all_to_all(pooled, "tbl", split_axis=1, concat_axis=0, tiled=True)
    slot_total = arrived.shape[0]
    pick_slot = (table_map[:, None] == jnp.arange(slot_total, dtype=jnp.int32)[None, :]).astype(
        jnp.bfloat16
    )
    embedded = jnp.einsum(
        "fs,srd->frd", pick_slot, arrived, preferred_element_type=jnp.float32
    ).astype(jnp.bfloat16)
    bottom_out = dense_layer(
        dense_layer(dense_layer(dense_feats, bottom_one), bottom_two), bottom_three
    )
    lead_cols = bottom_out.astype(jnp.float32)
    zero_col = jnp.zeros((row_count, 1), jnp.float32)
    vectors = jnp.concatenate([bottom_out[None], embedded], axis=0)
    code_base = make_codes(vectors, lead_cols, zero_col)
    gathered = lax.all_gather(embedded[:NPERM], "grp", axis=1, tiled=True)
    source = row_perm // (owners * row_count) * row_count + row_perm % row_count
    pick_row = (source[:, None] == jnp.arange(gathered.shape[1], dtype=jnp.int32)[None, :]).astype(
        jnp.bfloat16
    )
    shuffled = jnp.einsum(
        "rs,psd->prd", pick_row, gathered, preferred_element_type=jnp.float32
    ).astype(jnp.bfloat16)
    swapped = jnp.concatenate([bottom_out[None], shuffled, embedded[NPERM:]], axis=0)
    code_perm = make_codes(swapped, lead_cols, zero_col)
    hidden_local = top_one.shape[1]
    stacked_codes = jnp.concatenate([code_base, code_perm], axis=0)
    pre_all = jnp.dot(
        lax.all_gather(stacked_codes, "grp", axis=0, tiled=True),
        top_one,
        preferred_element_type=jnp.float32,
    )
    pre_all = pre_all.reshape(groups, 2, row_count, hidden_local)
    pre_base = pre_all[:, 0].reshape(groups * row_count, hidden_local)
    pre_perm = pre_all[:, 1].reshape(groups * row_count, hidden_local)
    hidden_base = jnp.maximum(pre_base, 0.0).astype(jnp.bfloat16)
    hidden_perm = jnp.maximum(pre_perm, 0.0).astype(jnp.bfloat16)
    hidden = jnp.concatenate(
        [
            hidden_base.reshape(groups, row_count, hidden_local),
            hidden_perm.reshape(groups, row_count, hidden_local),
        ],
        axis=1,
    ).reshape(groups * 2 * row_count, hidden_local)
    summed = lax.psum_scatter(
        second_layer(hidden, top_two).astype(jnp.bfloat16), "grp", scatter_dimension=0, tiled=True
    ).astype(jnp.float32)
    summed = summed.reshape(2, row_count, -1)
    logits = jnp.dot(
        jnp.maximum(summed, 0.0), top_out.astype(jnp.float32), precision=lax.Precision.HIGHEST
    )
    return jax.nn.sigmoid(logits)


def solution(mesh):
    placed = (
        P(("grp", "tbl"), None),
        P(None, "grp", None),
        P(None, "grp"),
        P(),
        P(("grp", "tbl")),
        P("tbl", None, None),
        P(),
        P(),
        P(),
        P(None, "grp"),
        P("grp", None),
        P(),
    )
    return jax.shard_map(
        local, mesh=mesh, in_specs=placed, out_specs=P(None, ("grp", "tbl")), check_vma=False
    )
```

profile of v0, /device:TPU:1, one launch (start us, length us, event | category | flops | bytes accessed | tf_op | source)
XLA Modules:
  0.0 209.8 jit_solution(5805964670611610993)
XLA Ops:
  6.5 0.0 copy-start
  6.5 0.8 compare_convert_fusion
  7.4 0.1 copy.83
  7.5 1.3 multiply_reduce_fusion
  8.8 0.2 copy.84
  9.0 1.1 multiply_reduce_fusion.1
  10.1 0.2 fusion.30
  10.3 0.2 copy.82
  10.5 0.2 fusion.29
  10.7 24.3 %select_reduce_fusion = bf16[1024,2048]{1,0:T(8,128)(2,1)} fusion(f32[1024,8]{1,0:T(8,128)S(1)} %fusion.30, s32[1024,8]{1,0:T(8,128)S(1)} %copy.84), kind=kLoop, calls=%fused_computation | loop fusion | flops 48234496 | bytes 4259840 | tf_op jit(solution)/shard_map/reduce_sum | solution.py:60
  35.0 3.5 %fusion.10 = bf16[1,1024,128]{2,1,0:T(8,128)(2,1)S(1)} fusion(bf16[1024,2048]{1,0:T(8,128)(2,1)} %select_reduce_fusion, bf16[2,2048,128]{2,1,0:T(8,128)(2,1)} %param.17), kind=kOutput, calls=%fused_computation.13 | convolution fusion | flops 537001984 | bytes 4980736 | tf_op jit(solution)/shard_map/dot_general | solution.py:62
  38.6 24.3 %select_reduce_fusion.1 = bf16[1024,2048]{1,0:T(8,128)(2,1)} fusion(f32[1024,8]{1,0:T(8,128)S(1)} %fusion.29, s32[1024,8]{1,0:T(8,128)S(1)} %copy.82), kind=kLoop, calls=%fused_computation.2 | loop fusion | flops 48234496 | bytes 4259840 | tf_op jit(solution)/shard_map/reduce_sum | solution.py:60
  62.9 0.0 copy-start.1
  62.9 0.0 copy-start.4
  62.9 0.0 copy-start.5
  62.9 0.0 copy-start.3
  62.9 0.0 copy-start.8
  62.9 0.0 copy-start.7
  62.9 3.6 %fusion.13 = bf16[1,1024,128]{2,1,0:T(8,128)(2,1)S(1)} fusion(bf16[1024,2048]{1,0:T(8,128)(2,1)} %select_reduce_fusion.1, bf16[2,2048,128]{2,1,0:T(8,128)(2,1)} %param.17), kind=kOutput, calls=%fused_computation.14 | convolution fusion | flops 537001984 | bytes 4980736 | tf_op jit(solution)/shard_map/dot_general | solution.py:62
  66.5 0.1 pad_maximum_fusion
  66.5 1.3 copy.85
  67.9 13.7 %all-to-all-start = ((bf16[2,1024,128]{2,0,1:T(2,128)(2,1)}), bf16[2,1024,128]{2,0,1:T(2,128)(2,1)S(1)}, u32[]{:S(2)}, u32[]{:S(2)}) async-start(bf16[2,1024,128]{2,0,1:T(2,128)(2,1)} %copy.85), calls=%async_computation | async-start | bytes 1048576 | tf_op jit(solution)/shard_map/all_to_all | solution.py:67
  81.6 0.0 reduce-scatter.2.cloned.1.call-start
  81.6 0.0 copy-done.1
  81.6 0.0 copy-done.4
  81.7 0.0 copy-done.5
  81.7 0.3 fusion.19
  81.9 0.0 copy-done.3
  82.0 0.1 fusion.20
  82.1 0.0 copy-done.8
  82.2 13.7 %all-to-all-done = bf16[2,1024,128]{2,0,1:T(2,128)(2,1)S(1)} async-done(((bf16[2,1024,128]{2,0,1:T(2,128)(2,1)}), bf16[2,1024,128]{2,0,1:T(2,128)(2,1)S(1)}, u32[]{:S(2)}, u32[]{:S(2)}) %all-to-all-start) | async-done | bytes 524320 | tf_op jit(solution)/shard_map/all_to_all | solution.py:67
  95.9 0.0 copy-start.2
  95.9 0.5 copy.86
  96.4 0.0 copy-done.7
  96.5 0.3 convolution_convert_fusion.1
  96.7 0.3 fusion.31
  97.0 0.1 copy.124
  97.4 0.1 slice.331
  97.5 22.4 %all_gather.6 = bf16[4,512,128]{2,0,1:T(4,128)(2,1)S(1)} all-gather(bf16[4,32,128]{2,0,1:T(4,128)(2,1)S(1)} %slice.330), channel_id=1, replica_groups=mesh['grp'=16,'tbl'=32] {'grp'}, dimensions={1}, use_global_device_ids=true | all-gather | bytes 557056 | tf_op jit(solution)/shard_map/all_gather | solution.py:82
  119.8 0.2 convolution_convert_fusion.2
  120.1 0.3 fusion.33
  120.4 0.1 copy.123
  120.7 0.2 concatenate.21
  120.9 0.2 concatenate.23
  121.1 18.1 %all_gather.7 = bf16[1024,480]{1,0:T(8,128)(2,1)S(1)} all-gather(bf16[64,480]{1,0:T(8,128)(2,1)S(1)} %pad_maximum_fusion.5), channel_id=1, replica_groups=mesh['grp'=16,'tbl'=32] {'grp'}, dimensions={0}, use_global_device_ids=true | all-gather | bytes 1044480 | tf_op jit(solution)/shard_map/all_gather | solution.py:95
  139.2 0.0 copy-done.2
  139.2 0.4 fusion.52
  139.6 0.1 fusion.35
  139.7 0.1 fusion.36
  139.8 0.0 copy-done
  139.8 0.0 copy-start.6
  139.8 3.2 %convolution_convert_fusion = bf16[1024,2048]{1,0:T(8,128)(2,1)} fusion(bf16[1024,256]{1,0:T(8,128)(2,1)S(1)} %bitcast.169, bf16[256,2048]{1,0:T(8,128)(2,1)S(1)} %copy-done), kind=kOutput, calls=%fused_computation.8 | convolution fusion | flops 1075838976 | bytes 5767168 | tf_op jit(solution)/shard_map/dot_general | solution.py:16
  143.0 0.0 reduce-scatter.2.cloned.1.call-update
  143.0 0.0 copy-done.6
  143.0 57.7 %reduce-scatter.2.cloned.1.call-done = bf16[64,2048]{1,0:T(8,128)(2,1)} async-done(((bf16[1024,2048]{1,0:T(8,128)(2,1)}), bf16[64,2048]{1,0:T(8,128)(2,1)}) %reduce-scatter.2.cloned.1.call-update) | async-done | bytes 262160 | tf_op jit(solution)/shard_map/reduce_scatter | solution.py:111
  200.7 1.0 convert_maximum_fusion
  201.7 0.6 fusion.53
  202.3 0.6 add_divide_fusion
  (63 shorter events, 0.3 us)
Async XLA Ops:
  6.5 133.2 %copy-start = (bf16[256,2048]{1,0:T(8,128)(2,1)S(1)}, bf16[256,2048]{1,0:T(8,128)(2,1)}, u32[]{:S(2)}) copy-start(bf16[256,2048]{1,0:T(8,128)(2,1)} %param.22) | copy-start | bytes 3145732
  62.9 18.8 %copy-start.1 = (bf16[512,256]{1,0:T(8,128)(2,1)S(1)}, bf16[512,256]{1,0:T(8,128)(2,1)}, u32[]{:S(2)}) copy-start(bf16[512,256]{1,0:T(8,128)(2,1)} %param.19) | copy-start | bytes 786436
  62.9 18.8 %copy-start.4 = (bf16[13,512]{1,0:T(8,128)(2,1)S(1)}, bf16[13,512]{1,0:T(8,128)(2,1)}, u32[]{:S(2)}) copy-start(bf16[13,512]{1,0:T(8,128)(2,1)} %param.18) | copy-start | bytes 39940
  62.9 18.8 %copy-start.5 = (bf16[32,13]{0,1:T(8,128)(2,1)S(1)}, bf16[32,13]{0,1:T(8,128)(2,1)}, u32[]{:S(2)}) copy-start(bf16[32,13]{0,1:T(8,128)(2,1)} %param.12) | copy-start | bytes 2500
  62.9 19.1 %copy-start.3 = (bf16[256,128]{1,0:T(8,128)(2,1)S(1)}, bf16[256,128]{1,0:T(8,128)(2,1)}, u32[]{:S(2)}) copy-start(bf16[256,128]{1,0:T(8,128)(2,1)} %param.20) | copy-start | bytes 196612
  62.9 19.3 %copy-start.8 = (s32[32]{0:T(128)S(1)}, s32[32]{0:T(128)}, u32[]{:S(2)}) copy-start(s32[32]{0:T(128)} %param.16) | copy-start | bytes 388
  62.9 33.6 %copy-start.7 = (s32[26]{0:T(128)S(1)}, s32[26]{0:T(128)}, u32[]{:S(2)}) copy-start(s32[26]{0:T(128)} %param.15) | copy-start | bytes 316
  67.9 28.0 %all-to-all-start = ((bf16[2,1024,128]{2,0,1:T(2,128)(2,1)}), bf16[2,1024,128]{2,0,1:T(2,128)(2,1)S(1)}, u32[]{:S(2)}, u32[]{:S(2)}) async-start(bf16[2,1024,128]{2,0,1:T(2,128)(2,1)} %copy.85), calls=%async_computation | async-start | bytes 1048576 | tf_op jit(solution)/shard_map/all_to_all | solution.py:67
  81.6 119.1 %reduce-scatter.2.cloned.1.call-start = ((), (), s32[]{:S(2)}) async-start(), calls=%async_computation.2 | async-start | bytes 4456448 | tf_op jit(solution)/shard_map/reduce_scatter | solution.py:111
  95.9 43.3 %copy-start.2 = (bf16[480,256]{1,0:T(8,128)(2,1)S(1)}, bf16[480,256]{1,0:T(8,128)(2,1)}, u32[]{:S(2)}) copy-start(bf16[480,256]{1,0:T(8,128)(2,1)} %param.21) | copy-start | bytes 737284
  139.8 3.2 %copy-start.6 = (bf16[2048]{0:T(1024)(128)(2,1)S(1)}, bf16[2048]{0:T(1024)(128)(2,1)}, u32[]{:S(2)}) copy-start(bf16[2048]{0:T(1024)(128)(2,1)} %param.23) | copy-start | bytes 12292
Sparse Core Ops, SparseCore 0:
  143.1 57.5 reduce-scatter.1
where the time goes:
time: 211 us; the launch traced here: 210 us
  waiting for transfers between devices  71.5 us (34%)
  other arithmetic  54 us (26%)
  blocking collectives  40.5 us (19%)
  between operations  14.1 us (7%)
  starting transfers between devices  13.8 us (7%)
  matrix products  12.8 us (6%)
  local copies, waits for them, and re-layouts  3.17 us (2%)
    reduce_scatter x1, waiting for transfers between devices, local(): lax.psum_scatter(second_layer(hidden, top_two).astype(jnp.bfloat16), 'grp...  57.7 us
    reduce_sum x2, other arithmetic, local(): counts = jnp.sum(hits * bag_mask[:, :, None], axis=1).astype(jnp.bfloat16)  48.6 us
    all_gather x1, blocking collectives, local(): gathered = lax.all_gather(embedded[:NPERM], 'grp', axis=1, tiled=True)  22.4 us
    all_gather x1, blocking collectives, local(): lax.all_gather(stacked_codes, 'grp', axis=0, tiled=True)  18.1 us
    all_to_all x1, waiting for transfers between devices, local(): lax.all_to_all(pooled, 'tbl', split_axis=1, concat_axis=0, tiled=True)  13.7 us
    all_to_all x1, starting transfers between devices, local(): lax.all_to_all(pooled, 'tbl', split_axis=1, concat_axis=0, tiled=True)  13.7 us
    dot_general x2, matrix products, local(): jnp.dot(counts, tables[slot_pos], preferred_element_type=jnp.float32)  7.14 us
  transfers between devices with their start and end apart: 2, of which 2 were waited for; matrix products, arithmetic and copies ran while one was open for 0% of the time, Pallas kernels for 0%

commit v1 on v0

v1 whole, which is shorter than its diff:
```python
import jax
import jax.numpy as jnp
import numpy as np
from jax import lax
from jax.experimental import pallas as pl
from jax.experimental.pallas import tpu as pltpu
from jax.sharding import PartitionSpec as P

NPERM = 4
LO = 256
ROWBLK = 16
TILE = 256


def dense_layer(inputs, weights):
    return jnp.maximum(jnp.dot(inputs, weights, preferred_element_type=jnp.float32), 0.0).astype(
        jnp.bfloat16
    )


def spread_bags(ids):
    sub = lax.broadcasted_iota(jnp.int32, ids.shape, 0)
    grp = lax.broadcasted_iota(jnp.int32, ids.shape, 1) // ROWBLK
    for step in (1, 2, 4):
        down = pltpu.roll(pltpu.roll(ids, 8 - step, 0), ROWBLK * step, 1)
        up = pltpu.roll(pltpu.roll(ids, step, 0), 128 - ROWBLK * step, 1)
        sub_bit = (sub & step) != 0
        grp_bit = (grp & step) != 0
        ids = jnp.where(sub_bit == grp_bit, ids, jnp.where(sub_bit, up, down))
    return ids


def pool_kernel(map_ref, owner_ref, ids_ref, len_ref, table_ref, out_ref, cnt_ref):
    vocab = table_ref.shape[1]
    hi_count = vocab // LO
    feat = find_feature(pl.program_id(0), map_ref, owner_ref)
    row_id = lax.broadcasted_iota(jnp.int32, (hi_count * ROWBLK, 128), 0)
    col_id = lax.broadcasted_iota(jnp.int32, (hi_count * ROWBLK, 128), 1)
    target = jnp.where(row_id % ROWBLK == col_id % ROWBLK, row_id // ROWBLK, -1)
    target = target.astype(jnp.float32).astype(jnp.bfloat16)
    lo_id = lax.broadcasted_iota(jnp.int32, (LO, 128), 0).astype(jnp.float32).astype(jnp.bfloat16)
    one = jnp.ones((), jnp.bfloat16)
    zero = jnp.zeros((), jnp.bfloat16)

    def tile(tile_idx, carry):
        for part in range(TILE // 128):
            start = pl.multiple_of(tile_idx * TILE + part * 128, 128)
            ids = ids_ref[0, :, pl.ds(start, 128)]
            lens = len_ref[:, pl.ds(start, 128)]
            feat_pos = lax.broadcasted_iota(jnp.int32, lens.shape, 0)
            lens = jnp.sum(jnp.where(feat_pos == feat, lens, 0), axis=0, keepdims=True)
            bag_pos = lax.broadcasted_iota(jnp.int32, ids.shape, 0)
            ids = spread_bags(jnp.where(bag_pos < lens, ids, vocab))
            high = (ids // LO).astype(jnp.float32)
            low = (ids % LO).astype(jnp.float32)
            for blk in range(8):
                high_row = jnp.broadcast_to(high[blk : blk + 1], target.shape).astype(jnp.bfloat16)
                low_row = jnp.broadcast_to(low[blk : blk + 1], lo_id.shape).astype(jnp.bfloat16)
                lhs = jnp.where(high_row == target, one, zero)
                rhs = jnp.where(low_row == lo_id, one, zero)
                counts = lax.dot_general(
                    lhs, rhs, (((1,), (1,)), ((), ())), preferred_element_type=jnp.float32
                ).astype(jnp.bfloat16)
                row = part * 128 + blk * ROWBLK
                for hi in range(hi_count):
                    cnt_ref[row : row + ROWBLK, hi * LO : (hi + 1) * LO] = counts[
                        hi * ROWBLK : (hi + 1) * ROWBLK
                    ]
        pooled = jnp.dot(cnt_ref[...], table_ref[0], preferred_element_type=jnp.float32)
        owners = TILE // out_ref.shape[2]
        out_ref[pl.ds(tile_idx * owners, owners), 0] = pooled.astype(jnp.bfloat16).reshape(
            owners, out_ref.shape[2], out_ref.shape[3]
        )
        return carry

    lax.fori_loop(0, ids_ref.shape[2] // TILE, tile, 0)


def find_feature(slot, map_ref, owner_ref):
    wanted = owner_ref[0] + slot
    feat = jnp.int32(0)
    for idx in range(map_ref.shape[0]):
        feat = jnp.where(map_ref[idx] == wanted, idx, feat)
    return feat


def pool_slots(table_map, first_slot, ids_t, lengths, tables, owners, row_count):
    slot_count, vocab, dim = tables.shape
    feats, bag, span = ids_t.shape
    return pl.pallas_call(
        pool_kernel,
        grid_spec=pltpu.PrefetchScalarGridSpec(
            num_scalar_prefetch=2,
            grid=(slot_count,),
            in_specs=[
                pl.BlockSpec(
                    (1, bag, span), lambda s, m, o: (find_feature(s, m, o), 0, 0)
                ),
                pl.BlockSpec((feats, span), lambda s, m, o: (0, 0)),
                pl.BlockSpec((1, vocab, dim), lambda s, m, o: (s, 0, 0)),
            ],
            out_specs=pl.BlockSpec(
                (owners, 1, row_count, dim), lambda s, m, o: (0, s, 0, 0)
            ),
            scratch_shapes=[pltpu.VMEM((TILE, vocab), jnp.bfloat16)],
        ),
        out_shape=jax.ShapeDtypeStruct((owners, slot_count, row_count, dim), jnp.bfloat16),
    )(table_map, first_slot, ids_t, lengths, tables)


def code_order(feats, dim, width):
    order = [0, *range(NPERM + 1, feats + 1), *range(1, NPERM + 1)]
    fixed = feats + 1 - NPERM

    def column(i, j):
        a, b = max(order[i], order[j]), min(order[i], order[j])
        return dim + a * (a - 1) // 2 + b

    cols = list(range(dim))
    cols += [column(i, j) for i in range(1, fixed) for j in range(i)]
    cols += [width - 1]
    cols += [-1] * (-len(cols) % 128)
    fixed_width = len(cols)
    cols += [column(i, j) for i in range(fixed, feats + 1) for j in range(i)]
    cols += [-1] * (-len(cols) % 128)
    return np.array(cols, np.int32), fixed_width


def fixed_codes(vectors, lead, fixed_width):
    gram = jnp.einsum("ird,jrd->rij", vectors, vectors, preferred_element_type=jnp.float32)
    pairs = [gram[:, level, :level] for level in range(1, vectors.shape[0])]
    out = jnp.concatenate([lead.astype(jnp.float32), *pairs], axis=1)
    return jnp.pad(out, ((0, 0), (0, fixed_width - out.shape[1]))).astype(jnp.bfloat16)


def moved_codes(moved, fixed, moved_width):
    every = jnp.concatenate([fixed, moved], axis=0)
    gram = jnp.einsum("ird,jrd->rij", moved, every, preferred_element_type=jnp.float32)
    pairs = [gram[:, i, : fixed.shape[0] + i] for i in range(moved.shape[0])]
    out = jnp.concatenate(pairs, axis=1)
    return jnp.pad(out, ((0, 0), (0, moved_width - out.shape[1]))).astype(jnp.bfloat16)


def top_kernel(core_ref, codes_ref, one_ref, own_ref, far_ref, out_w_ref, out_ref, acc_ref):
    step = pl.program_id(0)
    core = core_ref[0]
    width = codes_ref.shape[3]
    rows = codes_ref.shape[0] * codes_ref.shape[2]
    in_width = one_ref.shape[2]
    moved_width = width - in_width
    fixed_width = in_width - moved_width
    codes = jnp.concatenate([codes_ref[y, 0] for y in range(codes_ref.shape[0])], axis=0)
    fixed = codes[:, :fixed_width]
    moved = jnp.concatenate([codes[:, fixed_width:in_width], codes[:, in_width:]], axis=0)

    @pl.when(step == 0)
    def _():
        acc_ref[...] = jnp.zeros_like(acc_ref)

    total = acc_ref[...]
    for blk in range(own_ref.shape[0]):
        for side, second in ((core, own_ref), (1 - core, far_ref)):
            first = one_ref[blk, side]
            base = jnp.dot(fixed, first[:fixed_width], preferred_element_type=jnp.float32)
            delta = jnp.dot(moved, first[fixed_width:], preferred_element_type=jnp.float32)
            hidden = jnp.concatenate([base, base], axis=0) + delta
            hidden = jnp.maximum(hidden, 0.0).astype(jnp.bfloat16)
            total += jnp.dot(hidden, second[blk], preferred_element_type=jnp.float32)
    acc_ref[...] = total

    @pl.when(step == pl.num_programs(0) - 1)
    def _():
        scaled = jnp.maximum(total, 0.0) * out_w_ref[...]
        folded = scaled[:, :128]
        for lane in range(128, scaled.shape[1], 128):
            folded += scaled[:, lane : lane + 128]
        out_ref[...] = jnp.sum(folded.T, axis=0, keepdims=True)


def top_layers(core, codes, one_all, own, far, out_w):
    ys, cores, row_count, width = codes.shape
    in_width, blk_width = one_all.shape[2:]
    cols = own.shape[2]
    steps = 4 if ys % 4 == 0 else 1
    per = ys // steps
    return pl.pallas_call(
        top_kernel,
        grid_spec=pltpu.PrefetchScalarGridSpec(
            num_scalar_prefetch=1,
            grid=(steps,),
            in_specs=[
                pl.BlockSpec((ys, 1, row_count, width), lambda i, c: (0, c[0], 0, 0)),
                pl.BlockSpec((per, cores, in_width, blk_width), lambda i, c: (i, 0, 0, 0)),
                pl.BlockSpec((per, blk_width, cols), lambda i, c: (i, 0, 0)),
                pl.BlockSpec((per, blk_width, cols), lambda i, c: (i, 0, 0)),
                pl.BlockSpec((1, cols), lambda i, c: (0, 0)),
            ],
            out_specs=pl.BlockSpec((1, 2 * ys * row_count), lambda i, c: (0, 0)),
            scratch_shapes=[pltpu.VMEM((2 * ys * row_count, cols), jnp.float32)],
        ),
        out_shape=jax.ShapeDtypeStruct((1, 2 * ys * row_count), jnp.float32),
    )(core, codes, one_all, own, far, out_w)


def local(
    dense_feats,
    sparse_ids,
    lengths,
    table_map,
    row_perm,
    tables,
    bottom_one,
    bottom_two,
    bottom_three,
    top_one,
    top_two,
    top_out,
):
    groups = lax.axis_size("grp")
    owners = lax.axis_size("tbl")
    cores = 2
    ys = groups // cores
    grp_idx = lax.axis_index("grp")
    core = grp_idx % cores
    y_idx = grp_idx // cores
    same_core = [[cores * y + c for y in range(ys)] for c in range(cores)]
    swap_core = [(cores * y + c, cores * y + 1 - c) for y in range(ys) for c in range(cores)]
    slot_count = tables.shape[0]
    row_count = dense_feats.shape[0]
    feats = sparse_ids.shape[0]
    dim = tables.shape[2]

    cols, fixed_width = code_order(feats, dim, top_one.shape[0])
    in_width = cols.shape[0]
    moved_width = in_width - fixed_width
    pick_col = (jnp.asarray(cols)[:, None] == jnp.arange(top_one.shape[0])[None, :]).astype(
        jnp.bfloat16
    )
    one_local = jnp.dot(pick_col, top_one, preferred_element_type=jnp.float32).astype(jnp.bfloat16)
    one_all = lax.all_gather(one_local, "grp", axis=0, tiled=False)
    one_all = one_all.reshape(ys, cores, in_width, top_one.shape[1])

    out_cols = top_two.shape[1] // ys
    two_split = top_two.reshape(top_two.shape[0], ys, out_cols).transpose(1, 0, 2)
    own = lax.all_to_all(
        two_split, "grp", split_axis=0, concat_axis=0, tiled=True, axis_index_groups=same_core
    )
    far = lax.ppermute(own, "grp", swap_core)

    first_slot = (lax.axis_index("tbl") * slot_count).astype(jnp.int32).reshape(1)
    pooled = pool_slots(
        table_map, first_slot, sparse_ids.transpose(0, 2, 1), lengths, tables, owners, row_count
    )
    arrived = lax.all_to_all(pooled, "tbl", split_axis=0, concat_axis=0, tiled=True)
    arrived = arrived.reshape(owners * slot_count, row_count, dim)
    pick_slot = (
        table_map[:, None] == jnp.arange(owners * slot_count, dtype=jnp.int32)[None, :]
    ).astype(jnp.bfloat16)
    embedded = jnp.einsum(
        "fs,srd->frd", pick_slot, arrived, preferred_element_type=jnp.float32
    ).astype(jnp.bfloat16)

    bottom_out = dense_layer(
        dense_layer(dense_layer(dense_feats, bottom_one), bottom_two), bottom_three
    )
    gathered = lax.all_gather(embedded[:NPERM], "grp", axis=1, tiled=True)
    fixed = jnp.concatenate([bottom_out[None], embedded[NPERM:]], axis=0)
    code_fixed = fixed_codes(fixed, bottom_out, fixed_width)
    code_base = moved_codes(embedded[:NPERM], fixed, moved_width)
    source = row_perm // (owners * row_count) * row_count + row_perm % row_count
    pick_row = (source[:, None] == jnp.arange(gathered.shape[1], dtype=jnp.int32)[None, :]).astype(
        jnp.bfloat16
    )
    shuffled = jnp.einsum(
        "rs,psd->prd", pick_row, gathered, preferred_element_type=jnp.float32
    ).astype(jnp.bfloat16)
    code_perm = moved_codes(shuffled, fixed, moved_width)
    codes = jnp.concatenate([code_fixed, code_base, code_perm], axis=1)
    codes_all = lax.all_gather(codes, "grp", axis=0, tiled=False)
    codes_all = codes_all.reshape(ys, cores, row_count, codes.shape[1])

    out_w = lax.dynamic_slice(top_out, (y_idx * out_cols,), (out_cols,)).reshape(1, out_cols)
    out_w = out_w.astype(jnp.float32)
    part = top_layers(core.reshape(1), codes_all, one_all, own, far, out_w)
    part = part.reshape(2, ys, row_count).transpose(1, 0, 2)
    pieces = lax.all_to_all(
        part, "grp", split_axis=0, concat_axis=0, tiled=True, axis_index_groups=same_core
    )
    return jax.nn.sigmoid(jnp.sum(pieces, axis=0))


def solution(mesh):
    placed = (
        P(("grp", "tbl"), None),
        P(None, "grp", None),
        P(None, "grp"),
        P(),
        P(("grp", "tbl")),
        P("tbl", None, None),
        P(),
        P(),
        P(),
        P(None, "grp"),
        P("grp", None),
        P(),
    )
    return jax.shard_map(
        local, mesh=mesh, in_specs=placed, out_specs=P(None, ("grp", "tbl")), check_vma=False
    )
```

time: 211 us -> 157 us (0.74)
  waiting for transfers between devices: 71.5 us -> 8.53 us
  other arithmetic: 54 us -> 3.36 us
  blocking collectives: 40.5 us -> 80.8 us
  Pallas kernels: 0 us -> 18.2 us
  matrix products: 12.8 us -> 3.71 us
  starting transfers between devices: 13.8 us -> 22.8 us
    reduce_scatter x1 -> x0, waiting for transfers between devices: 57.7 us -> none  [local(): lax.psum_scatter(second_layer(hidden, top_two).astype(jnp.bfloat16), 'grp...]
    reduce_sum x4 -> x1, other arithmetic: 51 us -> 0.02 us  [local(): return jax.nn.sigmoid(jnp.sum(pieces, axis=0))]
    all_gather x1, blocking collectives: 22.4 us -> 52.2 us  [local(): gathered = lax.all_gather(embedded[:NPERM], 'grp', axis=1, tiled=True)]
    pallas_call x0 -> x2, Pallas kernels: none -> 18.2 us  [the longest x1 11 us: pool_slots(): pl.pallas_call(pool_kernel, grid_spec=pltpu.PrefetchScalarGridSpec(num_sc...]
    all_to_all x0 -> x1, blocking collectives: none -> 10.8 us  [local(): lax.all_to_all(part, 'grp', split_axis=0, concat_axis=0, tiled=True, axis...]
    dot_general x7 -> x4, matrix products: 11.9 us -> 2.79 us  [the longest x1 2.03 us: local(): jnp.dot(pick_col, top_one, preferred_element_type=jnp.float32)]
    all_to_all x1 -> x2, starting transfers between devices: 13.7 us -> 20.7 us  [the longest x1 13.8 us: local(): lax.all_to_all(pooled, 'tbl', split_axis=0, concat_axis=0, tiled=True)]
    all_to_all x1 -> x2, waiting for transfers between devices: 13.7 us -> 8.5 us  [the longest x1 8.5 us: local(): lax.all_to_all(pooled, 'tbl', split_axis=0, concat_axis=0, tiled=True)]
  transfers between devices with their start and end apart: 2 -> 4, of which waited for: 2 -> 1; matrix products, arithmetic and copies ran while one was open for 0% -> 5% of each run, Pallas kernels for 0% -> 0%
where the time goes in v1:
time: 157 us; the launch traced here: 155 us
  blocking collectives  80.8 us (51%)
  starting transfers between devices  22.8 us (15%)
  Pallas kernels  18.2 us (12%)
  between operations  13.9 us (9%)
  waiting for transfers between devices  8.53 us (5%)
  local copies, waits for them, and re-layouts  3.82 us (2%)
  matrix products  3.71 us (2%)
  other arithmetic  3.36 us (2%)
    all_gather x1, blocking collectives, local(): gathered = lax.all_gather(embedded[:NPERM], 'grp', axis=1, tiled=True)  52.2 us
    all_gather x1, blocking collectives, local(): codes_all = lax.all_gather(codes, 'grp', axis=0, tiled=False)  17.8 us
    all_to_all x1, starting transfers between devices, local(): lax.all_to_all(pooled, 'tbl', split_axis=0, concat_axis=0, tiled=True)  13.8 us
    pallas_call x1, Pallas kernels, pool_slots(): pl.pallas_call(pool_kernel, grid_spec=pltpu.PrefetchScalarGridSpec(num_sc...  11 us
    all_to_all x1, blocking collectives, local(): lax.all_to_all(part, 'grp', split_axis=0, concat_axis=0, tiled=True, axis...  10.8 us
    all_to_all x1, waiting for transfers between devices, local(): lax.all_to_all(pooled, 'tbl', split_axis=0, concat_axis=0, tiled=True)  8.5 us
    pallas_call x1, Pallas kernels, top_layers(): pl.pallas_call(top_kernel, grid_spec=pltpu.PrefetchScalarGridSpec(num_sca...  7.19 us
    all_to_all x1, starting transfers between devices, local(): lax.all_to_all(two_split, 'grp', split_axis=0, concat_axis=0, tiled=True,...  6.83 us
  transfers between devices with their start and end apart: 4, of which 1 were waited for; matrix products, arithmetic and copies ran while one was open for 5% of the time, Pallas kernels for 0%

profile of v1, /device:TPU:1, one launch (start us, length us, event | category | flops | bytes accessed | tf_op | source)
XLA Modules:
  0.0 155.0 jit_solution(8322366114403896731)
XLA Ops:
  6.5 0.0 copy-start
  6.5 0.0 copy-start.5
  6.5 0.0 copy-start.6
  6.5 0.0 copy-start.4
  6.5 0.0 copy-start.2
  6.6 0.0 copy-start.8
  6.6 11.0 %shard_map.127 = bf16[32,2,32,128]{3,2,1,0:T(8,128)(2,1)} custom-call(s32[26]{0:T(128)} %map_ref.1, s32[1]{0:T(128)} %bitcast.3.owner_ref, s32[26,8,1024]{2,1,0:T(8,128)} %bitcast.94, s32[26,1024]{1,0:T(8,128)} %len_ref.1, bf16[2,2048,128]{2,1,0:T(8,128)(2,1)} %table_ref.1), custom_call_target="tpu_custom_call" | custom-call | tf_op jit(solution)/shard_map/pallas_call | solution.py:90
  17.5 0.0 copy-start.7
  17.5 13.8 %all-to-all-start = ((bf16[32,2,32,128]{3,2,1,0:T(8,128)(2,1)}), bf16[32,2,32,128]{3,2,1,0:T(8,128)(2,1)S(1)}, u32[]{:S(2)}, u32[]{:S(2)}) async-start(bf16[32,2,32,128]{3,2,1,0:T(8,128)(2,1)} %shard_map.127), calls=%async_computation | async-start | bytes 1048576 | tf_op jit(solution)/shard_map/all_to_all | solution.py:254
  31.4 0.0 all-gather.4.cloned.1.call-start
  31.4 2.0 %convolution_convert_fusion = bf16[512,256]{1,0:T(8,128)(2,1)} fusion(bf16[480,256]{1,0:T(8,128)(2,1)} %param.22, s32[512]{0:T(512)} %constant.78.clone), kind=kOutput, calls=%fused_computation | convolution fusion | flops 126205952 | bytes 509952 | tf_op jit(solution)/shard_map/dot_general | solution.py:239
  33.5 0.0 all-gather.4.cloned.1.call-update
  33.5 0.0 copy-done
  33.5 0.0 copy-done.5
  33.5 0.0 copy-done.6
  33.5 0.3 fusion.3
  33.8 0.0 copy-done.4
  33.8 0.1 fusion.4
  34.0 0.0 copy-done.2
  34.0 0.5 copy.64
  34.5 1.3 copy.65
  35.8 1.3 dynamic-slice_convert_fusion
  37.2 0.0 copy-done.8
  37.2 8.5 %all-to-all-done = bf16[32,2,32,128]{3,2,1,0:T(8,128)(2,1)S(1)} async-done(((bf16[32,2,32,128]{3,2,1,0:T(8,128)(2,1)}), bf16[32,2,32,128]{3,2,1,0:T(8,128)(2,1)S(1)}, u32[]{:S(2)}, u32[]{:S(2)}) %all-to-all-start) | async-done | bytes 524320 | tf_op jit(solution)/shard_map/all_to_all | solution.py:254
  45.7 6.8 %all-to-all-start.1 = ((bf16[8,256,256]{2,1,0:T(8,128)(2,1)}), bf16[8,256,256]{2,1,0:T(8,128)(2,1)S(1)}, u32[]{:S(2)}, u32[]{:S(2)}) async-start(bf16[8,256,256]{2,1,0:T(8,128)(2,1)} %bitcast.41), calls=%async_computation.1 | async-start | bytes 2097152 | tf_op jit(solution)/shard_map/all_to_all | solution.py:245
  52.5 0.0 copy-done.7
  52.5 0.3 convolution_convert_fusion.1
  52.8 0.1 slice.159
  52.9 0.2 fusion.14
  53.2 0.3 fusion.8
  53.5 52.2 %all_gather.15 = bf16[4,512,128]{2,0,1:T(4,128)(2,1)S(1)} all-gather(bf16[4,32,128]{2,0,1:T(4,128)(2,1)S(1)} %slice.182), channel_id=1, replica_groups=mesh['grp'=16,'tbl'=32] {'grp'}, dimensions={1}, use_global_device_ids=true | all-gather | bytes 557056 | tf_op jit(solution)/shard_map/all_gather | solution.py:266
  105.7 0.2 convolution_convert_fusion.2
  106.1 0.3 fusion.11
  106.5 0.0 all-to-all-done.1.own_ref
  106.5 0.0 copy-start.1
  106.5 2.1 %collective-permute-start = (bf16[8,256,256]{2,1,0:T(8,128)(2,1)S(1)}, bf16[8,256,256]{2,1,0:T(8,128)(2,1)S(1)}, u32[]{:S(2)}, u32[]{:S(2)}) collective-permute-start(bf16[8,256,256]{2,1,0:T(8,128)(2,1)S(1)} %all-to-all-done.1.own_ref), channel_id=1, source_target_pairs={{0,32},{32,0},{64,96},{96,64},{128,160},{160,128},{192,224},{224,1... | collective-permute-start | bytes 3145736 | tf_op jit(solution)/shard_map/ppermute | solution.py:248
  108.6 0.1 concatenate.27
  108.8 0.1 fusion.37
  108.9 17.8 %all-gather = bf16[512,640]{1,0:T(8,128)(2,1)} all-gather(bf16[32,640]{1,0:T(8,128)(2,1)S(1)} %fusion.22), channel_id=2, replica_groups=mesh['grp'=16,'tbl'=32] {'grp'}, dimensions={0}, use_global_device_ids=true | all-gather | bytes 696320 | tf_op jit(solution)/shard_map/all_gather | solution.py:279
  126.6 0.0 collective-permute-done.far_ref
  126.6 0.0 copy-start.3
  126.6 0.0 all-gather.4.cloned.1.call-done
  126.7 0.0 copy-done.1
  126.7 1.0 copy-done.3
  127.6 7.2 %shard_map.128 = f32[1,512]{1,0:T(1,128)} custom-call(s32[1]{0:T(128)} %bitcast.core_ref, bf16[8,2,32,640]{3,2,1,0:T(8,128)(2,1)} %bitcast.92, bf16[8,2,512,256]{3,2,1,0:T(8,128)(2,1)} %bitcast.90, bf16[8,256,256]{2,1,0:T(8,128)(2,1)} %copy-done.1, bf16[8,256,256]{2,1,0:T(8,128)(2,1)} %copy-done.3, f32[1,256]{1,0:T(1,128)} %bitcast.98), custom_call_target="tpu_custom_call" | custom-call | tf_op jit(solution)/shard_map/pallas_call | solution.py:186
  134.8 0.5 broadcast.56
  135.3 1.3 reduce.3
  136.7 0.1 reshape.33
  136.8 10.8 %all_to_all.15 = f32[8,2,32]{2,1,0:T(2,128)S(1)} all-to-all(f32[8,2,32]{2,1,0:T(2,128)S(1)} %bitcast.97), channel_id=1, replica_groups={{0,64,128,192,256,320,384,448},{32,96,160,224,288,352,416,480},{1,65,12..., dimensions={0} | all-to-all | bytes 4096 | tf_op jit(solution)/shard_map/all_to_all | solution.py:286
  147.6 0.6 add_divide_fusion
  (40 shorter events, 0.2 us)
Async XLA Ops:
  6.5 27.0 %copy-start = (bf16[512,256]{1,0:T(8,128)(2,1)S(1)}, bf16[512,256]{1,0:T(8,128)(2,1)}, u32[]{:S(2)}) copy-start(bf16[512,256]{1,0:T(8,128)(2,1)} %param.20) | copy-start | bytes 786436
  6.5 27.0 %copy-start.5 = (bf16[13,512]{1,0:T(8,128)(2,1)S(1)}, bf16[13,512]{1,0:T(8,128)(2,1)}, u32[]{:S(2)}) copy-start(bf16[13,512]{1,0:T(8,128)(2,1)} %param.19) | copy-start | bytes 39940
  6.5 27.0 %copy-start.6 = (bf16[32,13]{0,1:T(8,128)(2,1)S(1)}, bf16[32,13]{0,1:T(8,128)(2,1)}, u32[]{:S(2)}) copy-start(bf16[32,13]{0,1:T(8,128)(2,1)} %param.13) | copy-start | bytes 2500
  6.5 27.3 %copy-start.4 = (bf16[256,128]{1,0:T(8,128)(2,1)S(1)}, bf16[256,128]{1,0:T(8,128)(2,1)}, u32[]{:S(2)}) copy-start(bf16[256,128]{1,0:T(8,128)(2,1)} %param.21) | copy-start | bytes 196612
  6.5 27.5 %copy-start.2 = (bf16[256,2048]{1,0:T(8,128)(2,1)S(1)}, bf16[256,2048]{1,0:T(8,128)(2,1)}, u32[]{:S(2)}) copy-start(bf16[256,2048]{1,0:T(8,128)(2,1)} %param.23) | copy-start | bytes 3145732
  6.6 30.6 %copy-start.8 = (s32[32]{0:T(128)S(1)}, s32[32]{0:T(128)}, u32[]{:S(2)}) copy-start(s32[32]{0:T(128)} %param.17) | copy-start | bytes 388
  17.5 35.0 %copy-start.7 = (s32[26]{0:T(128)S(1)}, s32[26]{0:T(128)}, u32[]{:S(2)}) copy-start(s32[26]{0:T(128)} %map_ref.1) | copy-start | bytes 316
  17.5 28.1 %all-to-all-start = ((bf16[32,2,32,128]{3,2,1,0:T(8,128)(2,1)}), bf16[32,2,32,128]{3,2,1,0:T(8,128)(2,1)S(1)}, u32[]{:S(2)}, u32[]{:S(2)}) async-start(bf16[32,2,32,128]{3,2,1,0:T(8,128)(2,1)} %shard_map.127), calls=%async_computation | async-start | bytes 1048576 | tf_op jit(solution)/shard_map/all_to_all | solution.py:254
  31.4 95.3 %all-gather.4.cloned.1.call-start = ((), (), s32[]{:S(2)}) async-start(), calls=%async_computation.3 | async-start | bytes 4456448 | tf_op jit(solution)/shard_map/all_gather | solution.py:240
  45.7 60.8 %all-to-all-start.1 = ((bf16[8,256,256]{2,1,0:T(8,128)(2,1)}), bf16[8,256,256]{2,1,0:T(8,128)(2,1)S(1)}, u32[]{:S(2)}, u32[]{:S(2)}) async-start(bf16[8,256,256]{2,1,0:T(8,128)(2,1)} %bitcast.41), calls=%async_computation.1 | async-start | bytes 2097152 | tf_op jit(solution)/shard_map/all_to_all | solution.py:245
  106.5 20.2 %copy-start.1 = (bf16[8,256,256]{2,1,0:T(8,128)(2,1)}, bf16[8,256,256]{2,1,0:T(8,128)(2,1)S(1)}, u32[]{:S(2)}) copy-start(bf16[8,256,256]{2,1,0:T(8,128)(2,1)S(1)} %all-to-all-done.1.own_ref) | copy-start | bytes 3145732
  106.5 20.1 %collective-permute-start = (bf16[8,256,256]{2,1,0:T(8,128)(2,1)S(1)}, bf16[8,256,256]{2,1,0:T(8,128)(2,1)S(1)}, u32[]{:S(2)}, u32[]{:S(2)}) collective-permute-start(bf16[8,256,256]{2,1,0:T(8,128)(2,1)S(1)} %all-to-all-done.1.own_ref), channel_id=1, source_target_pairs={{0,32},{32,0},{64,96},{96,64},{128,160},{160,128},{192,224},{224,1... | collective-permute-start | bytes 3145736 | tf_op jit(solution)/shard_map/ppermute | solution.py:248
  126.6 1.0 copy-start.3
Sparse Core Ops, SparseCore 0:
  34.3 65.5 all-gather.3

commit v2 on v1

--- a/solution.py
+++ b/solution.py
@@ -141,11 +141,10 @@
     return jnp.pad(out, ((0, 0), (0, moved_width - out.shape[1]))).astype(jnp.bfloat16)
 
 
-def top_kernel(core_ref, codes_ref, one_ref, own_ref, far_ref, out_w_ref, out_ref, acc_ref):
+def top_kernel(pos_ref, codes_ref, one_ref, own_ref, far_ref, keep_ref, send_ref, acc_ref):
     step = pl.program_id(0)
-    core = core_ref[0]
+    core = pos_ref[0]
     width = codes_ref.shape[3]
-    rows = codes_ref.shape[0] * codes_ref.shape[2]
     in_width = one_ref.shape[2]
     moved_width = width - in_width
     fixed_width = in_width - moved_width
@@ -158,48 +157,66 @@
         acc_ref[...] = jnp.zeros_like(acc_ref)
 
     total = acc_ref[...]
-    for blk in range(own_ref.shape[0]):
-        for side, second in ((core, own_ref), (1 - core, far_ref)):
-            first = one_ref[blk, side]
-            base = jnp.dot(fixed, first[:fixed_width], preferred_element_type=jnp.float32)
-            delta = jnp.dot(moved, first[fixed_width:], preferred_element_type=jnp.float32)
-            hidden = jnp.concatenate([base, base], axis=0) + delta
-            hidden = jnp.maximum(hidden, 0.0).astype(jnp.bfloat16)
-            total += jnp.dot(hidden, second[blk], preferred_element_type=jnp.float32)
+    for side, second in ((core, own_ref), (1 - core, far_ref)):
+        first = one_ref[0, side]
+        base = jnp.dot(fixed, first[:fixed_width], preferred_element_type=jnp.float32)
+        delta = jnp.dot(moved, first[fixed_width:], preferred_element_type=jnp.float32)
+        hidden = jnp.concatenate([base, base], axis=0) + delta
+        hidden = jnp.maximum(hidden, 0.0).astype(jnp.bfloat16)
+        total += jnp.dot(hidden, second[0], preferred_element_type=jnp.float32)
     acc_ref[...] = total
 
     @pl.when(step == pl.num_programs(0) - 1)
     def _():
-        scaled = jnp.maximum(total, 0.0) * out_w_ref[...]
-        folded = scaled[:, :128]
-        for lane in range(128, scaled.shape[1], 128):
-            folded += scaled[:, lane : lane + 128]
-        out_ref[...] = jnp.sum(folded.T, axis=0, keepdims=True)
-
-
-def top_layers(core, codes, one_all, own, far, out_w):
+        half = total.shape[1] // 2
+        low, high = total[:, :half], total[:, half:]
+        is_low = pos_ref[2] == 0
+        keep_ref[...] = jnp.where(is_low, low, high)
+        send_ref[...] = jnp.where(is_low, high, low).astype(jnp.bfloat16)
+
+
+def top_layers(pos, codes, one_all, own, far):
     ys, cores, row_count, width = codes.shape
     in_width, blk_width = one_all.shape[2:]
-    cols = own.shape[2]
-    steps = 4 if ys % 4 == 0 else 1
-    per = ys // steps
+    quad, _, cols = own.shape
+    rows = 2 * ys * row_count
+    weights = pl.BlockSpec((1, blk_width, cols), lambda i, p: (i, 0, 0))
+    result = pl.BlockSpec((rows, cols // 2), lambda i, p: (0, 0))
     return pl.pallas_call(
         top_kernel,
         grid_spec=pltpu.PrefetchScalarGridSpec(
             num_scalar_prefetch=1,
-            grid=(steps,),
+            grid=(quad,),
             in_specs=[
-                pl.BlockSpec((ys, 1, row_count, width), lambda i, c: (0, c[0], 0, 0)),
-                pl.BlockSpec((per, cores, in_width, blk_width), lambda i, c: (i, 0, 0, 0)),
-                pl.BlockSpec((per, blk_width, cols), lambda i, c: (i, 0, 0)),
-                pl.BlockSpec((per, blk_width, cols), lambda i, c: (i, 0, 0)),
-                pl.BlockSpec((1, cols), lambda i, c: (0, 0)),
+                pl.BlockSpec((ys, 1, row_count, width), lambda i, p: (0, p[0], 0, 0)),
+                pl.BlockSpec(
+                    (1, cores, in_width, blk_width), lambda i, p: ((p[1] + quad - i) % quad, 0, 0, 0)
+                ),
+                weights,
+                weights,
             ],
-            out_specs=pl.BlockSpec((1, 2 * ys * row_count), lambda i, c: (0, 0)),
-            scratch_shapes=[pltpu.VMEM((2 * ys * row_count, cols), jnp.float32)],
+            out_specs=[result, result],
+            scratch_shapes=[pltpu.VMEM((rows, cols), jnp.float32)],
         ),
-        out_shape=jax.ShapeDtypeStruct((1, 2 * ys * row_count), jnp.float32),
-    )(core, codes, one_all, own, far, out_w)
+        out_shape=[
+            jax.ShapeDtypeStruct((rows, cols // 2), jnp.float32),
+            jax.ShapeDtypeStruct((rows, cols // 2), jnp.bfloat16),
+        ],
+    )(pos, codes, one_all, own, far)
+
+
+def logit_kernel(keep_ref, came_ref, out_w_ref, out_ref):
+    ys, variants, row_count = out_ref.shape
+    total = keep_ref[...] + came_ref[...].astype(jnp.float32)
+    scaled = jnp.maximum(total, 0.0) * out_w_ref[...]
+    folded = scaled[:, :128]
+    for lane in range(128, scaled.shape[1], 128):
+        folded += scaled[:, lane : lane + 128]
+    sums = jnp.sum(folded.T, axis=0, keepdims=True)
+    for variant in range(variants):
+        for y in range(ys):
+            start = (variant * ys + y) * row_count
+            out_ref[y, variant : variant + 1] = sums[:, start : start + row_count]
 
 
 def local(
@@ -223,8 +240,14 @@
     grp_idx = lax.axis_index("grp")
     core = grp_idx % cores
     y_idx = grp_idx // cores
+    pairs = 2
+    quad = ys // pairs
     same_core = [[cores * y + c for y in range(ys)] for c in range(cores)]
     swap_core = [(cores * y + c, cores * y + 1 - c) for y in range(ys) for c in range(cores)]
+    swap_pair = [(cores * y + c, cores * (y ^ 1) + c) for y in range(ys) for c in range(cores)]
+    same_parity = [
+        [cores * y + c for y in range(h, ys, pairs) for c in range(cores)] for h in range(pairs)
+    ]
     slot_count = tables.shape[0]
     row_count = dense_feats.shape[0]
     feats = sparse_ids.shape[0]
@@ -237,16 +260,24 @@
         jnp.bfloat16
     )
     one_local = jnp.dot(pick_col, top_one, preferred_element_type=jnp.float32).astype(jnp.bfloat16)
-    one_all = lax.all_gather(one_local, "grp", axis=0, tiled=False)
-    one_all = one_all.reshape(ys, cores, in_width, top_one.shape[1])
-
-    out_cols = top_two.shape[1] // ys
-    two_split = top_two.reshape(top_two.shape[0], ys, out_cols).transpose(1, 0, 2)
-    own = lax.all_to_all(
-        two_split, "grp", split_axis=0, concat_axis=0, tiled=True, axis_index_groups=same_core
-    )
-    far = lax.ppermute(own, "grp", swap_core)
-
+    one_all = lax.all_gather(
+        one_local, "grp", axis=0, tiled=False, axis_index_groups=same_parity
+    )
+    one_all = one_all.reshape(quad, cores, in_width, top_one.shape[1])
+
+    blk_cols = top_two.shape[1] // quad
+    blocks = []
+    for hop in range(quad):
+        start = (y_idx // pairs + hop) % quad * blk_cols
+        piece = lax.dynamic_slice(top_two, (0, start), (top_two.shape[0], blk_cols))
+        if hop:
+            shift = [
+                (cores * y + c, cores * ((y + pairs * hop) % ys) + c)
+                for y in range(ys)
+                for c in range(cores)
+            ]
+            piece = lax.ppermute(piece, "grp", shift)
+        blocks.append(piece)
     first_slot = (lax.axis_index("tbl") * slot_count).astype(jnp.int32).reshape(1)
     pooled = pool_slots(
         table_map, first_slot, sparse_ids.transpose(0, 2, 1), lengths, tables, owners, row_count
@@ -264,6 +295,9 @@
         dense_layer(dense_layer(dense_feats, bottom_one), bottom_two), bottom_three
     )
     gathered = lax.all_gather(embedded[:NPERM], "grp", axis=1, tiled=True)
+    gathered, *blocks = lax.optimization_barrier((gathered, *blocks))
+    own = jnp.stack(blocks, axis=0)
+    far = lax.ppermute(own, "grp", swap_core)
     fixed = jnp.concatenate([bottom_out[None], embedded[NPERM:]], axis=0)
     code_fixed = fixed_codes(fixed, bottom_out, fixed_width)
     code_base = moved_codes(embedded[:NPERM], fixed, moved_width)
@@ -279,10 +313,17 @@
     codes_all = lax.all_gather(codes, "grp", axis=0, tiled=False)
     codes_all = codes_all.reshape(ys, cores, row_count, codes.shape[1])
 
-    out_w = lax.dynamic_slice(top_out, (y_idx * out_cols,), (out_cols,)).reshape(1, out_cols)
+    half = blk_cols // pairs
+    parity = y_idx % pairs
+    out_start = y_idx // pairs * blk_cols + parity * half
+    out_w = lax.dynamic_slice(top_out, (out_start,), (half,)).reshape(1, half)
     out_w = out_w.astype(jnp.float32)
-    part = top_layers(core.reshape(1), codes_all, one_all, own, far, out_w)
-    part = part.reshape(2, ys, row_count).transpose(1, 0, 2)
+    pos = jnp.stack([core, y_idx // pairs, parity]).astype(jnp.int32)
+    keep, send = top_layers(pos, codes_all, one_all, own, far)
+    came = lax.ppermute(send, "grp", swap_pair)
+    part = pl.pallas_call(
+        logit_kernel, out_shape=jax.ShapeDtypeStruct((ys, 2, row_count), jnp.float32)
+    )(keep, came, out_w)
     pieces = lax.all_to_all(
         part, "grp", split_axis=0, concat_axis=0, tiled=True, axis_index_groups=same_core
     )

time: 157 us -> 155 us (0.987)
  starting transfers between devices: 22.8 us -> 33 us
  blocking collectives: 80.8 us -> 73.3 us
  waiting for transfers between devices: 8.53 us -> 5.24 us
  Pallas kernels: 18.2 us -> 20 us
  local copies, waits for them, and re-layouts: 3.82 us -> 2.2 us
    ppermute x0 -> x4, starting transfers between devices: none -> 17 us  [the longest x3 13.6 us: local(): piece = lax.ppermute(piece, 'grp', shift)]
    all_to_all x1, waiting for transfers between devices: 8.5 us -> 0.01 us  [local(): lax.all_to_all(pooled, 'tbl', split_axis=0, concat_axis=0, tiled=True)]
    all_gather x1, blocking collectives: 52.2 us -> 44.5 us  [local(): gathered = lax.all_gather(embedded[:NPERM], 'grp', axis=1, tiled=True)]
    all_to_all x1 -> x0, starting transfers between devices: 6.83 us -> none  [local(): lax.all_to_all(two_split, 'grp', split_axis=0, concat_axis=0, tiled=True,...]
    ppermute x0 -> x4, waiting for transfers between devices: none -> 5.2 us  [the longest x1 5.2 us: local(): came = lax.ppermute(send, 'grp', swap_pair)]
    pallas_call x0 -> x1, Pallas kernels: none -> 1.95 us  [local(): pl.pallas_call(logit_kernel, out_shape=jax.ShapeDtypeStruct((ys, 2, row_c...]
  transfers between devices with their start and end apart: 4 -> 7, of which waited for: 1 -> 1; matrix products, arithmetic and copies ran while one was open for 5% -> 4% of each run, Pallas kernels for 0% -> 0%
where the time goes in v2:
time: 155 us; the launch traced here: 153 us
  blocking collectives  73.3 us (47%)
  starting transfers between devices  33 us (21%)
  Pallas kernels  20 us (13%)
  between operations  14.1 us (9%)
  waiting for transfers between devices  5.24 us (3%)
  other arithmetic  2.76 us (2%)
  matrix products  2.75 us (2%)
  local copies, waits for them, and re-layouts  2.2 us (1%)
    all_gather x1, blocking collectives, local(): gathered = lax.all_gather(embedded[:NPERM], 'grp', axis=1, tiled=True)  44.5 us
    all_gather x1, blocking collectives, local(): codes_all = lax.all_gather(codes, 'grp', axis=0, tiled=False)  17.8 us
    all_to_all x1, starting transfers between devices, local(): lax.all_to_all(pooled, 'tbl', split_axis=0, concat_axis=0, tiled=True)  13.8 us
    ppermute x3, starting transfers between devices, local(): piece = lax.ppermute(piece, 'grp', shift)  13.6 us
    all_to_all x1, blocking collectives, local(): lax.all_to_all(part, 'grp', split_axis=0, concat_axis=0, tiled=True, axis...  11 us
    pallas_call x1, Pallas kernels, pool_slots(): pl.pallas_call(pool_kernel, grid_spec=pltpu.PrefetchScalarGridSpec(num_sc...  10.9 us
    pallas_call x1, Pallas kernels, top_layers(): pl.pallas_call(top_kernel, grid_spec=pltpu.PrefetchScalarGridSpec(num_sca...  7.07 us
    ppermute x1, waiting for transfers between devices, local(): came = lax.ppermute(send, 'grp', swap_pair)  5.2 us
  transfers between devices with their start and end apart: 7, of which 1 were waited for; matrix products, arithmetic and copies ran while one was open for 4% of the time, Pallas kernels for 0%

profile of v2, /device:TPU:1, one launch (start us, length us, event | category | flops | bytes accessed | tf_op | source)
XLA Modules:
  0.0 153.3 jit_solution(17285344113414478347)
XLA Ops:
  6.5 0.0 copy-start
  6.5 0.0 copy-start.11
  6.5 0.0 copy-start.9
  6.5 0.0 copy-start.3
  6.5 10.9 %shard_map.127 = bf16[32,2,32,128]{3,2,1,0:T(8,128)(2,1)} custom-call(s32[26]{0:T(128)} %map_ref.1, s32[1]{0:T(128)} %bitcast.5.owner_ref, s32[26,8,1024]{2,1,0:T(8,128)} %bitcast.95, s32[26,1024]{1,0:T(8,128)} %len_ref.1, bf16[2,2048,128]{2,1,0:T(8,128)(2,1)} %table_ref.1), custom_call_target="tpu_custom_call" | custom-call | tf_op jit(solution)/shard_map/pallas_call | solution.py:90
  17.5 0.0 copy-start.6
  17.5 0.0 copy-start.7
  17.5 13.8 %all-to-all-start = ((bf16[32,2,32,128]{3,2,1,0:T(8,128)(2,1)}), bf16[32,2,32,128]{3,2,1,0:T(8,128)(2,1)S(1)}, u32[]{:S(2)}, u32[]{:S(2)}) async-start(bf16[32,2,32,128]{3,2,1,0:T(8,128)(2,1)} %shard_map.127), calls=%async_computation | async-start | bytes 1048576 | tf_op jit(solution)/shard_map/all_to_all | solution.py:285
  31.4 0.0 copy-start.5
  31.4 0.0 copy-start.10
  31.4 0.0 copy-start.8
  31.4 0.0 all-gather.4.cloned.1.call-start
  31.4 0.0 copy-done.11
  31.4 0.0 copy-done.9
  31.5 1.1 convolution_convert_fusion
  32.5 0.0 all-gather.4.cloned.1.call-update
  32.7 0.0 copy-done.3
  32.7 0.1 constant_dynamic-slice_fusion
  32.8 5.9 %collective-permute-start.2 = (bf16[256,512]{1,0:T(8,128)(2,1)S(1)}, bf16[256,512]{1,0:T(8,128)(2,1)S(1)}, u32[]{:S(2)}, u32[]{:S(2)}) collective-permute-start(bf16[256,512]{1,0:T(8,128)(2,1)S(1)} %get-tuple-element.19), channel_id=1, source_target_pairs={{0,384},{32,416},{64,448},{96,480},{128,0},{160,32},{192,64},{224,... | collective-permute-start | bytes 786440 | tf_op jit(solution)/shard_map/ppermute | solution.py:279
  38.7 1.9 %collective-permute-start = (bf16[256,512]{1,0:T(8,128)(2,1)S(1)}, bf16[256,512]{1,0:T(8,128)(2,1)S(1)}, u32[]{:S(2)}, u32[]{:S(2)}) collective-permute-start(bf16[256,512]{1,0:T(8,128)(2,1)S(1)} %get-tuple-element.20), channel_id=1, source_target_pairs={{0,128},{32,160},{64,192},{96,224},{128,256},{160,288},{192,320},{... | collective-permute-start | bytes 786440 | tf_op jit(solution)/shard_map/ppermute | solution.py:279
  40.6 5.8 %collective-permute-start.1 = (bf16[256,512]{1,0:T(8,128)(2,1)S(1)}, bf16[256,512]{1,0:T(8,128)(2,1)S(1)}, u32[]{:S(2)}, u32[]{:S(2)}) collective-permute-start(bf16[256,512]{1,0:T(8,128)(2,1)S(1)} %get-tuple-element.22), channel_id=1, source_target_pairs={{0,256},{32,288},{64,320},{96,352},{128,384},{160,416},{192,448},{... | collective-permute-start | bytes 786440 | tf_op jit(solution)/shard_map/ppermute | solution.py:279
  46.5 0.0 copy-done
  46.5 0.0 copy-done.6
  46.5 0.0 copy-done.7
  46.5 0.3 fusion.3
  46.8 0.0 copy-done.5
  46.8 0.1 fusion.4
  47.0 0.6 pad_add_fusion.pos_ref
  47.6 0.0 copy-done.10
  47.6 0.0 all-to-all-done
  47.6 0.0 copy-done.8
  47.6 0.3 convolution_convert_fusion.1
  47.9 0.1 slice.159
  48.0 0.3 fusion.8
  48.3 0.2 fusion.14
  48.7 44.5 %all_gather.15 = bf16[4,512,128]{2,0,1:T(4,128)(2,1)S(1)} all-gather(bf16[4,32,128]{2,0,1:T(4,128)(2,1)S(1)} %slice.182), channel_id=1, replica_groups=mesh['grp'=16,'tbl'=32] {'grp'}, dimensions={1}, use_global_device_ids=true | all-gather | bytes 557056 | tf_op jit(solution)/shard_map/all_gather | solution.py:297
  93.3 0.0 collective-permute-done.2
  93.3 0.0 collective-permute-done
  93.3 0.0 collective-permute-done.1
  93.3 0.2 convolution_convert_fusion.2
  93.5 0.3 fusion.11
  93.8 0.1 pad_maximum_fusion.own_ref
  93.9 0.0 copy-start.1
  93.9 2.1 %collective-permute-start.3 = (bf16[4,256,512]{2,1,0:T(8,128)(2,1)S(1)}, bf16[4,256,512]{2,1,0:T(8,128)(2,1)S(1)}, u32[]{:S(2)}, u32[]{:S(2)}) collective-permute-start(bf16[4,256,512]{2,1,0:T(8,128)(2,1)S(1)} %pad_maximum_fusion.own_ref), channel_id=1, source_target_pairs={{0,32},{32,0},{64,96},{96,64},{128,160},{160,128},{192,224},{224,1... | collective-permute-start | bytes 3145736 | tf_op jit(solution)/shard_map/ppermute | solution.py:300
  96.1 0.1 concatenate.27
  96.3 0.1 fusion.37
  96.4 17.8 %all-gather = bf16[512,640]{1,0:T(8,128)(2,1)} all-gather(bf16[32,640]{1,0:T(8,128)(2,1)S(1)} %fusion.22), channel_id=2, replica_groups=mesh['grp'=16,'tbl'=32] {'grp'}, dimensions={0}, use_global_device_ids=true | all-gather | bytes 696320 | tf_op jit(solution)/shard_map/all_gather | solution.py:313
  114.2 0.0 collective-permute-done.3.far_ref
  114.2 0.0 copy-start.2
  114.2 0.0 all-gather.4.cloned.1.call-done
  114.2 0.0 copy-done.1
  114.2 0.9 copy-done.2
  115.2 7.1 %shard_map.128 = (f32[512,256]{1,0:T(8,128)}, bf16[512,256]{1,0:T(8,128)(2,1)}) custom-call(s32[3]{0:T(128)} %pad_add_fusion.pos_ref, bf16[8,2,32,640]{3,2,1,0:T(8,128)(2,1)} %bitcast.91, bf16[4,2,512,256]{3,2,1,0:T(8,128)(2,1)} %bitcast.92, bf16[4,256,512]{2,1,0:T(8,128)(2,1)} %copy-done.1, bf16[4,256,512]{2,1,0:T(8,128)(2,1)} %copy-done.2), custom_call_target="tpu_custom_call" | custom-call | tf_op jit(solution)/shard_map/pallas_call | solution.py:185
  122.2 3.4 %collective-permute-start.4 = (bf16[512,256]{1,0:T(8,128)(2,1)}, bf16[512,256]{1,0:T(8,128)(2,1)S(1)}, u32[]{:S(2)}, u32[]{:S(2)}) collective-permute-start(bf16[512,256]{1,0:T(8,128)(2,1)} %get-tuple-element.18), channel_id=1, source_target_pairs={{0,64},{32,96},{64,0},{96,32},{128,192},{160,224},{192,128},{224,1... | collective-permute-start | bytes 786440 | tf_op jit(solution)/shard_map/ppermute | solution.py:323
  125.6 1.3 dynamic-slice_convert_fusion
  127.0 5.2 %collective-permute-done.4.came_ref = bf16[512,256]{1,0:T(8,128)(2,1)S(1)} collective-permute-done((bf16[512,256]{1,0:T(8,128)(2,1)}, bf16[512,256]{1,0:T(8,128)(2,1)S(1)}, u32[]{:S(2)}, u32[]{:S(2)}) %collective-permute-start.4) | collective-permute-done | bytes 262176 | tf_op jit(solution)/shard_map/ppermute | solution.py:323
  132.2 0.0 copy-start.4
  132.2 0.7 copy-done.4
  132.8 1.9 %shard_map.129 = f32[8,2,32]{2,1,0:T(2,128)} custom-call(f32[512,256]{1,0:T(8,128)} %get-tuple-element.17.keep_ref, bf16[512,256]{1,0:T(8,128)(2,1)} %copy-done.4, f32[1,256]{1,0:T(1,128)} %bitcast.101), custom_call_target="tpu_custom_call" | custom-call | tf_op jit(solution)/shard_map/pallas_call | solution.py:324
  134.8 11.0 %all_to_all.10 = f32[8,2,32]{2,1,0:T(2,128)S(1)} all-to-all(f32[8,2,32]{2,1,0:T(2,128)} %shard_map.129), channel_id=1, replica_groups={{0,64,128,192,256,320,384,448},{32,96,160,224,288,352,416,480},{1,65,12..., dimensions={0} | all-to-all | bytes 4096 | tf_op jit(solution)/shard_map/all_to_all | solution.py:327
  145.9 0.6 add_divide_fusion
  (39 shorter events, 0.2 us)
Async XLA Ops:
  6.5 39.9 %copy-start = (bf16[512,256]{1,0:T(8,128)(2,1)S(1)}, bf16[512,256]{1,0:T(8,128)(2,1)}, u32[]{:S(2)}) copy-start(bf16[512,256]{1,0:T(8,128)(2,1)} %param.20) | copy-start | bytes 786436
  6.5 24.9 %copy-start.11 = (s32[512]{0:T(512)S(1)}, s32[512]{0:T(512)}, u32[]{:S(2)}) copy-start(s32[512]{0:T(512)} %constant.125.clone) | copy-start | bytes 6148
  6.5 24.9 %copy-start.9 = (bf16[480,256]{1,0:T(8,128)(2,1)S(1)}, bf16[480,256]{1,0:T(8,128)(2,1)}, u32[]{:S(2)}) copy-start(bf16[480,256]{1,0:T(8,128)(2,1)} %param.22) | copy-start | bytes 737284
  6.5 26.1 %copy-start.3 = (bf16[256,2048]{1,0:T(8,128)(2,1)S(1)}, bf16[256,2048]{1,0:T(8,128)(2,1)}, u32[]{:S(2)}) copy-start(bf16[256,2048]{1,0:T(8,128)(2,1)} %param.23) | copy-start | bytes 3145732
  17.5 29.0 %copy-start.6 = (bf16[13,512]{1,0:T(8,128)(2,1)S(1)}, bf16[13,512]{1,0:T(8,128)(2,1)}, u32[]{:S(2)}) copy-start(bf16[13,512]{1,0:T(8,128)(2,1)} %param.19) | copy-start | bytes 39940
  17.5 29.0 %copy-start.7 = (bf16[32,13]{0,1:T(8,128)(2,1)S(1)}, bf16[32,13]{0,1:T(8,128)(2,1)}, u32[]{:S(2)}) copy-start(bf16[32,13]{0,1:T(8,128)(2,1)} %param.13) | copy-start | bytes 2500
  17.5 30.1 %all-to-all-start = ((bf16[32,2,32,128]{3,2,1,0:T(8,128)(2,1)}), bf16[32,2,32,128]{3,2,1,0:T(8,128)(2,1)S(1)}, u32[]{:S(2)}, u32[]{:S(2)}) async-start(bf16[32,2,32,128]{3,2,1,0:T(8,128)(2,1)} %shard_map.127), calls=%async_computation | async-start | bytes 1048576 | tf_op jit(solution)/shard_map/all_to_all | solution.py:285
  31.4 15.4 %copy-start.5 = (bf16[256,128]{1,0:T(8,128)(2,1)S(1)}, bf16[256,128]{1,0:T(8,128)(2,1)}, u32[]{:S(2)}) copy-start(bf16[256,128]{1,0:T(8,128)(2,1)} %param.21) | copy-start | bytes 196612
  31.4 16.2 %copy-start.10 = (s32[32]{0:T(128)S(1)}, s32[32]{0:T(128)}, u32[]{:S(2)}) copy-start(s32[32]{0:T(128)} %param.17) | copy-start | bytes 388
  31.4 16.2 %copy-start.8 = (s32[26]{0:T(128)S(1)}, s32[26]{0:T(128)}, u32[]{:S(2)}) copy-start(s32[26]{0:T(128)} %map_ref.1) | copy-start | bytes 316
  31.4 82.8 %all-gather.4.cloned.1.call-start = ((), (), s32[]{:S(2)}) async-start(), calls=%async_computation.2 | async-start | bytes 2359296 | tf_op jit(solution)/shard_map/all_gather | solution.py:263
  32.8 60.5 %collective-permute-start.2 = (bf16[256,512]{1,0:T(8,128)(2,1)S(1)}, bf16[256,512]{1,0:T(8,128)(2,1)S(1)}, u32[]{:S(2)}, u32[]{:S(2)}) collective-permute-start(bf16[256,512]{1,0:T(8,128)(2,1)S(1)} %get-tuple-element.19), channel_id=1, source_target_pairs={{0,384},{32,416},{64,448},{96,480},{128,0},{160,32},{192,64},{224,... | collective-permute-start | bytes 786440 | tf_op jit(solution)/shard_map/ppermute | solution.py:279
  38.7 54.6 %collective-permute-start = (bf16[256,512]{1,0:T(8,128)(2,1)S(1)}, bf16[256,512]{1,0:T(8,128)(2,1)S(1)}, u32[]{:S(2)}, u32[]{:S(2)}) collective-permute-start(bf16[256,512]{1,0:T(8,128)(2,1)S(1)} %get-tuple-element.20), channel_id=1, source_target_pairs={{0,128},{32,160},{64,192},{96,224},{128,256},{160,288},{192,320},{... | collective-permute-start | bytes 786440 | tf_op jit(solution)/shard_map/ppermute | solution.py:279
  40.6 52.6 %collective-permute-start.1 = (bf16[256,512]{1,0:T(8,128)(2,1)S(1)}, bf16[256,512]{1,0:T(8,128)(2,1)S(1)}, u32[]{:S(2)}, u32[]{:S(2)}) collective-permute-start(bf16[256,512]{1,0:T(8,128)(2,1)S(1)} %get-tuple-element.22), channel_id=1, source_target_pairs={{0,256},{32,288},{64,320},{96,352},{128,384},{160,416},{192,448},{... | collective-permute-start | bytes 786440 | tf_op jit(solution)/shard_map/ppermute | solution.py:279
  93.9 20.3 %copy-start.1 = (bf16[4,256,512]{2,1,0:T(8,128)(2,1)}, bf16[4,256,512]{2,1,0:T(8,128)(2,1)S(1)}, u32[]{:S(2)}) copy-start(bf16[4,256,512]{2,1,0:T(8,128)(2,1)S(1)} %pad_maximum_fusion.own_ref) | copy-start | bytes 3145732
  93.9 20.2 %collective-permute-start.3 = (bf16[4,256,512]{2,1,0:T(8,128)(2,1)S(1)}, bf16[4,256,512]{2,1,0:T(8,128)(2,1)S(1)}, u32[]{:S(2)}, u32[]{:S(2)}) collective-permute-start(bf16[4,256,512]{2,1,0:T(8,128)(2,1)S(1)} %pad_maximum_fusion.own_ref), channel_id=1, source_target_pairs={{0,32},{32,0},{64,96},{96,64},{128,160},{160,128},{192,224},{224,1... | collective-permute-start | bytes 3145736 | tf_op jit(solution)/shard_map/ppermute | solution.py:300
  114.2 1.0 copy-start.2
  122.2 9.9 %collective-permute-start.4 = (bf16[512,256]{1,0:T(8,128)(2,1)}, bf16[512,256]{1,0:T(8,128)(2,1)S(1)}, u32[]{:S(2)}, u32[]{:S(2)}) collective-permute-start(bf16[512,256]{1,0:T(8,128)(2,1)} %get-tuple-element.18), channel_id=1, source_target_pairs={{0,64},{32,96},{64,0},{96,32},{128,192},{160,224},{192,128},{224,1... | collective-permute-start | bytes 786440 | tf_op jit(solution)/shard_map/ppermute | solution.py:323
  132.2 0.7 copy-start.4
Sparse Core Ops, SparseCore 0:
  34.4 53.3 all-gather.3

commit v3 on v1

--- a/solution.py
+++ b/solution.py
@@ -141,15 +141,14 @@
     return jnp.pad(out, ((0, 0), (0, moved_width - out.shape[1]))).astype(jnp.bfloat16)
 
 
-def top_kernel(core_ref, codes_ref, one_ref, own_ref, far_ref, out_w_ref, out_ref, acc_ref):
+def top_kernel(codes_ref, weights_ref, out_w_ref, out_ref, acc_ref):
     step = pl.program_id(0)
-    core = core_ref[0]
-    width = codes_ref.shape[3]
-    rows = codes_ref.shape[0] * codes_ref.shape[2]
-    in_width = one_ref.shape[2]
+    width = codes_ref.shape[2]
+    blk_width = weights_ref.shape[2]
+    in_width = weights_ref.shape[1] - blk_width
     moved_width = width - in_width
     fixed_width = in_width - moved_width
-    codes = jnp.concatenate([codes_ref[y, 0] for y in range(codes_ref.shape[0])], axis=0)
+    codes = jnp.concatenate([codes_ref[z] for z in range(codes_ref.shape[0])], axis=0)
     fixed = codes[:, :fixed_width]
     moved = jnp.concatenate([codes[:, fixed_width:in_width], codes[:, in_width:]], axis=0)
 
@@ -158,48 +157,49 @@
         acc_ref[...] = jnp.zeros_like(acc_ref)
 
     total = acc_ref[...]
-    for blk in range(own_ref.shape[0]):
-        for side, second in ((core, own_ref), (1 - core, far_ref)):
-            first = one_ref[blk, side]
-            base = jnp.dot(fixed, first[:fixed_width], preferred_element_type=jnp.float32)
-            delta = jnp.dot(moved, first[fixed_width:], preferred_element_type=jnp.float32)
-            hidden = jnp.concatenate([base, base], axis=0) + delta
-            hidden = jnp.maximum(hidden, 0.0).astype(jnp.bfloat16)
-            total += jnp.dot(hidden, second[blk], preferred_element_type=jnp.float32)
+    for blk in range(weights_ref.shape[0]):
+        base = jnp.dot(
+            fixed, weights_ref[blk, :fixed_width], preferred_element_type=jnp.float32
+        )
+        delta = jnp.dot(
+            moved, weights_ref[blk, fixed_width:in_width], preferred_element_type=jnp.float32
+        )
+        hidden = jnp.concatenate([base, base], axis=0) + delta
+        hidden = jnp.maximum(hidden, 0.0).astype(jnp.bfloat16)
+        total += jnp.dot(hidden, weights_ref[blk, in_width:], preferred_element_type=jnp.float32)
     acc_ref[...] = total
 
     @pl.when(step == pl.num_programs(0) - 1)
     def _():
+        zs, variants, row_count = out_ref.shape
         scaled = jnp.maximum(total, 0.0) * out_w_ref[...]
         folded = scaled[:, :128]
         for lane in range(128, scaled.shape[1], 128):
             folded += scaled[:, lane : lane + 128]
-        out_ref[...] = jnp.sum(folded.T, axis=0, keepdims=True)
-
-
-def top_layers(core, codes, one_all, own, far, out_w):
-    ys, cores, row_count, width = codes.shape
-    in_width, blk_width = one_all.shape[2:]
-    cols = own.shape[2]
-    steps = 4 if ys % 4 == 0 else 1
-    per = ys // steps
+        sums = jnp.sum(folded.T, axis=0, keepdims=True)
+        for variant in range(variants):
+            for z in range(zs):
+                start = (variant * zs + z) * row_count
+                out_ref[z, variant : variant + 1] = sums[:, start : start + row_count]
+
+
+def top_layers(codes, weights, out_w):
+    zs, row_count, width = codes.shape
+    rows = zs * row_count
+    groups, depth, blk_width = weights.shape
+    steps = 4 if groups % 4 == 0 else 1
     return pl.pallas_call(
         top_kernel,
-        grid_spec=pltpu.PrefetchScalarGridSpec(
-            num_scalar_prefetch=1,
-            grid=(steps,),
-            in_specs=[
-                pl.BlockSpec((ys, 1, row_count, width), lambda i, c: (0, c[0], 0, 0)),
-                pl.BlockSpec((per, cores, in_width, blk_width), lambda i, c: (i, 0, 0, 0)),
-                pl.BlockSpec((per, blk_width, cols), lambda i, c: (i, 0, 0)),
-                pl.BlockSpec((per, blk_width, cols), lambda i, c: (i, 0, 0)),
-                pl.BlockSpec((1, cols), lambda i, c: (0, 0)),
-            ],
-            out_specs=pl.BlockSpec((1, 2 * ys * row_count), lambda i, c: (0, 0)),
-            scratch_shapes=[pltpu.VMEM((2 * ys * row_count, cols), jnp.float32)],
-        ),
-        out_shape=jax.ShapeDtypeStruct((1, 2 * ys * row_count), jnp.float32),
-    )(core, codes, one_all, own, far, out_w)
+        grid=(steps,),
+        in_specs=[
+            pl.BlockSpec((zs, row_count, width), lambda i: (0, 0, 0)),
+            pl.BlockSpec((groups // steps, depth, blk_width), lambda i: (i, 0, 0)),
+            pl.BlockSpec((1, blk_width), lambda i: (0, 0)),
+        ],
+        out_specs=pl.BlockSpec((zs, 2, row_count), lambda i: (0, 0, 0)),
+        scratch_shapes=[pltpu.VMEM((2 * rows, blk_width), jnp.float32)],
+        out_shape=jax.ShapeDtypeStruct((zs, 2, row_count), jnp.float32),
+    )(codes, weights, out_w)
 
 
 def local(
@@ -216,15 +216,12 @@
     top_two,
     top_out,
 ):
-    groups = lax.axis_size("grp")
     owners = lax.axis_size("tbl")
-    cores = 2
-    ys = groups // cores
-    grp_idx = lax.axis_index("grp")
-    core = grp_idx % cores
-    y_idx = grp_idx // cores
-    same_core = [[cores * y + c for y in range(ys)] for c in range(cores)]
-    swap_core = [(cores * y + c, cores * y + 1 - c) for y in range(ys) for c in range(cores)]
+    owner_idx = lax.axis_index("tbl")
+    blk_cols = top_one.shape[1]
+    zs = top_two.shape[1] // blk_cols
+    z_idx = owner_idx % zs
+    along_z = [[x * zs + z for z in range(zs)] for x in range(owners // zs)]
     slot_count = tables.shape[0]
     row_count = dense_feats.shape[0]
     feats = sparse_ids.shape[0]
@@ -237,17 +234,12 @@
         jnp.bfloat16
     )
     one_local = jnp.dot(pick_col, top_one, preferred_element_type=jnp.float32).astype(jnp.bfloat16)
-    one_all = lax.all_gather(one_local, "grp", axis=0, tiled=False)
-    one_all = one_all.reshape(ys, cores, in_width, top_one.shape[1])
-
-    out_cols = top_two.shape[1] // ys
-    two_split = top_two.reshape(top_two.shape[0], ys, out_cols).transpose(1, 0, 2)
-    own = lax.all_to_all(
-        two_split, "grp", split_axis=0, concat_axis=0, tiled=True, axis_index_groups=same_core
-    )
-    far = lax.ppermute(own, "grp", swap_core)
-
-    first_slot = (lax.axis_index("tbl") * slot_count).astype(jnp.int32).reshape(1)
+    two_local = lax.dynamic_slice(top_two, (0, z_idx * blk_cols), (top_two.shape[0], blk_cols))
+    weights = lax.all_gather(
+        jnp.concatenate([one_local, two_local], axis=0), "grp", axis=0, tiled=False
+    )
+
+    first_slot = (owner_idx * slot_count).astype(jnp.int32).reshape(1)
     pooled = pool_slots(
         table_map, first_slot, sparse_ids.transpose(0, 2, 1), lengths, tables, owners, row_count
     )
@@ -276,15 +268,13 @@
     ).astype(jnp.bfloat16)
     code_perm = moved_codes(shuffled, fixed, moved_width)
     codes = jnp.concatenate([code_fixed, code_base, code_perm], axis=1)
-    codes_all = lax.all_gather(codes, "grp", axis=0, tiled=False)
-    codes_all = codes_all.reshape(ys, cores, row_count, codes.shape[1])
-
-    out_w = lax.dynamic_slice(top_out, (y_idx * out_cols,), (out_cols,)).reshape(1, out_cols)
-    out_w = out_w.astype(jnp.float32)
-    part = top_layers(core.reshape(1), codes_all, one_all, own, far, out_w)
-    part = part.reshape(2, ys, row_count).transpose(1, 0, 2)
+    codes_all = lax.all_gather(
+        codes, "tbl", axis=0, tiled=False, axis_index_groups=along_z
+    )
+    out_w = lax.dynamic_slice(top_out, (z_idx * blk_cols,), (blk_cols,)).reshape(1, blk_cols)
+    part = top_layers(codes_all, weights, out_w.astype(jnp.float32))
     pieces = lax.all_to_all(
-        part, "grp", split_axis=0, concat_axis=0, tiled=True, axis_index_groups=same_core
+        part, "tbl", split_axis=0, concat_axis=0, tiled=True, axis_index_groups=along_z
     )
     return jax.nn.sigmoid(jnp.sum(pieces, axis=0))
 

time: 157 us -> 127 us (0.81)
  the two profiles are of different devices: /device:TPU:1 before, /device:TPU:2 now
where the time goes in v3:
time: 127 us; the launch traced here: 126 us
  blocking collectives  59.6 us (47%)
  Pallas kernels  18.1 us (14%)
  between operations  13.8 us (11%)
  starting transfers between devices  13.5 us (11%)
  waiting for transfers between devices  11.9 us (9%)
  matrix products  4.83 us (4%)
  other arithmetic  2.82 us (2%)
  local copies, waits for them, and re-layouts  1.63 us (1%)
    all_gather x1, blocking collectives, local(): lax.all_gather(codes, 'tbl', axis=0, tiled=False, axis_index_groups=along_z)  27.2 us
    all_gather x1, blocking collectives, local(): gathered = lax.all_gather(embedded[:NPERM], 'grp', axis=1, tiled=True)  20.1 us
    all_to_all x1, starting transfers between devices, local(): lax.all_to_all(pooled, 'tbl', split_axis=0, concat_axis=0, tiled=True)  13.5 us
    all_to_all x1, blocking collectives, local(): lax.all_to_all(part, 'tbl', split_axis=0, concat_axis=0, tiled=True, axis...  12.3 us
    all_to_all x1, waiting for transfers between devices, local(): lax.all_to_all(pooled, 'tbl', split_axis=0, concat_axis=0, tiled=True)  11.9 us
    pallas_call x1, Pallas kernels, pool_slots(): pl.pallas_call(pool_kernel, grid_spec=pltpu.PrefetchScalarGridSpec(num_sc...  10.8 us
    pallas_call x1, Pallas kernels, top_layers(): pl.pallas_call(top_kernel, grid=(steps,), in_specs=[pl.BlockSpec((zs, row...  7.3 us
  transfers between devices with their start and end apart: 2, of which 1 were waited for; matrix products, arithmetic and copies ran while one was open for 4% of the time, Pallas kernels for 9%

profile of v3, /device:TPU:2, one launch (start us, length us, event | category | flops | bytes accessed | tf_op | source)
XLA Modules:
  0.0 126.2 jit_solution(3979407732960763546)
XLA Ops:
  6.5 0.0 copy-start
  6.5 0.0 copy-start.1
  6.5 0.0 copy-start.2
  6.5 0.0 all-gather.4.cloned.1.call-start
  6.6 1.2 copy-done
  7.8 1.3 %convolution_convert_fusion = bf16[512,256]{1,0:T(8,128)(2,1)S(1)} fusion(bf16[480,256]{1,0:T(8,128)(2,1)} %param.22, s32[512]{0:T(512)} %constant.66.clone), kind=kOutput, calls=%fused_computation | convolution fusion | flops 126205952 | bytes 509952 | tf_op jit(solution)/shard_map/dot_general | solution.py:236
  9.1 0.8 pad_maximum_fusion
  9.9 0.0 all-gather.4.cloned.1.call-update
  9.9 10.8 %shard_map.127 = bf16[32,2,32,128]{3,2,1,0:T(8,128)(2,1)} custom-call(s32[26]{0:T(128)} %map_ref.1, s32[1]{0:T(128)} %bitcast.2.owner_ref, s32[26,8,1024]{2,1,0:T(8,128)} %bitcast.87, s32[26,1024]{1,0:T(8,128)} %len_ref.1, bf16[2,2048,128]{2,1,0:T(8,128)(2,1)} %table_ref.1), custom_call_target="tpu_custom_call" | custom-call | tf_op jit(solution)/shard_map/pallas_call | solution.py:90
  20.8 13.5 %all-to-all-start = ((bf16[32,2,32,128]{3,2,1,0:T(8,128)(2,1)}), bf16[32,2,32,128]{3,2,1,0:T(8,128)(2,1)S(1)}, u32[]{:S(2)}, u32[]{:S(2)}) async-start(bf16[32,2,32,128]{3,2,1,0:T(8,128)(2,1)} %shard_map.127), calls=%async_computation | async-start | bytes 1048576 | tf_op jit(solution)/shard_map/all_to_all | solution.py:246
  34.2 1.3 %fusion.3 = bf16[32,256]{1,0:T(8,128)(2,1)S(1)} fusion(bf16[512,256]{1,0:T(8,128)(2,1)} %param.20, bf16[32,13]{0,1:T(8,128)(2,1)} %param.13, bf16[13,512]{1,0:T(8,128)(2,1)} %param.19), kind=kOutput, calls=%fused_computation.7 | convolution fusion | flops 8863744 | bytes 292672 | tf_op jit(solution)/shard_map/dot_general | solution.py:16
  35.5 1.0 fusion.4
  36.5 1.3 %dynamic-slice_convert_fusion = f32[256]{0:T(256)} fusion(bf16[2048]{0:T(1024)(128)(2,1)} %param.24, s32[]{:T(128)S(6)} %select_n.25), kind=kLoop, calls=%fused_computation.94 | loop fusion | flops 256 | bytes 1540 | tf_op jit(solution)/shard_map/convert_element_type | solution.py:275
  37.8 0.0 copy-done.2
  37.8 11.9 %all-to-all-done = bf16[32,2,32,128]{3,2,1,0:T(8,128)(2,1)S(1)} async-done(((bf16[32,2,32,128]{3,2,1,0:T(8,128)(2,1)}), bf16[32,2,32,128]{3,2,1,0:T(8,128)(2,1)S(1)}, u32[]{:S(2)}, u32[]{:S(2)}) %all-to-all-start) | async-done | bytes 524320 | tf_op jit(solution)/shard_map/all_to_all | solution.py:246
  49.8 0.0 copy-done.1
  49.8 0.3 convolution_convert_fusion.1
  50.1 0.1 slice.159
  50.1 20.1 %all_gather.15 = bf16[4,512,128]{2,0,1:T(4,128)(2,1)S(1)} all-gather(bf16[4,32,128]{2,0,1:T(4,128)(2,1)S(1)} %slice.182), channel_id=1, replica_groups=mesh['grp'=16,'tbl'=32] {'grp'}, dimensions={1}, use_global_device_ids=true | all-gather | bytes 557056 | tf_op jit(solution)/shard_map/all_gather | solution.py:258
  70.3 0.2 convolution_convert_fusion.2
  70.5 0.3 fusion.11
  70.8 0.3 fusion.8
  71.1 0.2 fusion.14
  71.6 0.1 concatenate.30
  71.8 0.1 fusion.37
  71.9 27.2 %all-gather = bf16[256,640]{1,0:T(8,128)(2,1)} all-gather(bf16[32,640]{1,0:T(8,128)(2,1)S(1)} %fusion.22), channel_id=2, replica_groups={{0,1,2,3,4,5,6,7},{8,9,10,11,12,13,14,15},{16,17,18,19,20,21,22,23},{24..., dimensions={0}, use_global_device_ids=true | all-gather | bytes 368640 | tf_op jit(solution)/shard_map/all_gather | solution.py:271
  99.1 0.0 all-gather.4.cloned.1.call-done
  99.1 7.3 %shard_map.128 = f32[8,2,32]{2,1,0:T(2,128)} custom-call(bf16[8,32,640]{2,1,0:T(8,128)(2,1)} %bitcast.86, bf16[16,768,256]{2,1,0:T(8,128)(2,1)} %bitcast.84, f32[1,256]{1,0:T(1,128)} %bitcast.90), custom_call_target="tpu_custom_call" | custom-call | tf_op jit(solution)/shard_map/pallas_call | solution.py:191
  106.4 12.3 %all_to_all.10 = f32[8,2,32]{2,1,0:T(2,128)S(1)} all-to-all(f32[8,2,32]{2,1,0:T(2,128)} %shard_map.128), channel_id=1, replica_groups={{0,1,2,3,4,5,6,7},{8,9,10,11,12,13,14,15},{16,17,18,19,20,21,22,23},{24..., dimensions={0} | all-to-all | bytes 4096 | tf_op jit(solution)/shard_map/all_to_all | solution.py:276
  118.7 0.6 add_divide_fusion
  (40 shorter events, 0.2 us)
Async XLA Ops:
  6.5 1.2 copy-start
  6.5 43.2 %copy-start.1 = (s32[26]{0:T(128)S(1)}, s32[26]{0:T(128)}, u32[]{:S(2)}) copy-start(s32[26]{0:T(128)} %map_ref.1) | copy-start | bytes 316
  6.5 31.3 %copy-start.2 = (s32[32]{0:T(128)S(1)}, s32[32]{0:T(128)}, u32[]{:S(2)}) copy-start(s32[32]{0:T(128)} %param.17) | copy-start | bytes 388
  6.5 92.6 %all-gather.4.cloned.1.call-start = ((), (), s32[]{:S(2)}) async-start(), calls=%async_computation.2 | async-start | bytes 6684672 | tf_op jit(solution)/shard_map/all_gather | solution.py:238
  20.8 29.0 %all-to-all-start = ((bf16[32,2,32,128]{3,2,1,0:T(8,128)(2,1)}), bf16[32,2,32,128]{3,2,1,0:T(8,128)(2,1)S(1)}, u32[]{:S(2)}, u32[]{:S(2)}) async-start(bf16[32,2,32,128]{3,2,1,0:T(8,128)(2,1)} %shard_map.127), calls=%async_computation | async-start | bytes 1048576 | tf_op jit(solution)/shard_map/all_to_all | solution.py:246
Sparse Core Ops, SparseCore 0:
  10.1 54.3 all-gather.3

commit v4 on v3

--- a/solution.py
+++ b/solution.py
@@ -1,3 +1,5 @@
+import functools
+
 import jax
 import jax.numpy as jnp
 import numpy as np
@@ -10,6 +12,7 @@
 LO = 256
 ROWBLK = 16
 TILE = 256
+XS = 4
 
 
 def dense_layer(inputs, weights):
@@ -141,11 +144,10 @@
     return jnp.pad(out, ((0, 0), (0, moved_width - out.shape[1]))).astype(jnp.bfloat16)
 
 
-def top_kernel(codes_ref, weights_ref, out_w_ref, out_ref, acc_ref):
+def top_kernel(in_width, codes_ref, weights_ref, out_w_ref, out_ref, acc_ref):
     step = pl.program_id(0)
     width = codes_ref.shape[2]
     blk_width = weights_ref.shape[2]
-    in_width = weights_ref.shape[1] - blk_width
     moved_width = width - in_width
     fixed_width = in_width - moved_width
     codes = jnp.concatenate([codes_ref[z] for z in range(codes_ref.shape[0])], axis=0)
@@ -166,7 +168,17 @@
         )
         hidden = jnp.concatenate([base, base], axis=0) + delta
         hidden = jnp.maximum(hidden, 0.0).astype(jnp.bfloat16)
-        total += jnp.dot(hidden, weights_ref[blk, in_width:], preferred_element_type=jnp.float32)
+        total += jnp.concatenate(
+            [
+                jnp.dot(
+                    hidden,
+                    weights_ref[blk, start : start + blk_width],
+                    preferred_element_type=jnp.float32,
+                )
+                for start in range(in_width, weights_ref.shape[1], blk_width)
+            ],
+            axis=1,
+        )
     acc_ref[...] = total
 
     @pl.when(step == pl.num_programs(0) - 1)
@@ -183,21 +195,21 @@
                 out_ref[z, variant : variant + 1] = sums[:, start : start + row_count]
 
 
-def top_layers(codes, weights, out_w):
+def top_layers(codes, weights, out_w, in_width):
     zs, row_count, width = codes.shape
     rows = zs * row_count
     groups, depth, blk_width = weights.shape
     steps = 4 if groups % 4 == 0 else 1
     return pl.pallas_call(
-        top_kernel,
+        functools.partial(top_kernel, in_width),
         grid=(steps,),
         in_specs=[
             pl.BlockSpec((zs, row_count, width), lambda i: (0, 0, 0)),
             pl.BlockSpec((groups // steps, depth, blk_width), lambda i: (i, 0, 0)),
-            pl.BlockSpec((1, blk_width), lambda i: (0, 0)),
+            pl.BlockSpec(out_w.shape, lambda i: (0, 0)),
         ],
         out_specs=pl.BlockSpec((zs, 2, row_count), lambda i: (0, 0, 0)),
-        scratch_shapes=[pltpu.VMEM((2 * rows, blk_width), jnp.float32)],
+        scratch_shapes=[pltpu.VMEM((2 * rows, out_w.shape[1]), jnp.float32)],
         out_shape=jax.ShapeDtypeStruct((zs, 2, row_count), jnp.float32),
     )(codes, weights, out_w)
 
@@ -219,9 +231,11 @@
     owners = lax.axis_size("tbl")
     owner_idx = lax.axis_index("tbl")
     blk_cols = top_one.shape[1]
-    zs = top_two.shape[1] // blk_cols
-    z_idx = owner_idx % zs
-    along_z = [[x * zs + z for z in range(zs)] for x in range(owners // zs)]
+    xs = XS
+    zs = owners // xs
+    x_idx = owner_idx // zs
+    along_x = [[x * zs + z for x in range(xs)] for z in range(zs)]
+    out_cols = top_two.shape[1] // xs
     slot_count = tables.shape[0]
     row_count = dense_feats.shape[0]
     feats = sparse_ids.shape[0]
@@ -234,9 +248,14 @@
         jnp.bfloat16
     )
     one_local = jnp.dot(pick_col, top_one, preferred_element_type=jnp.float32).astype(jnp.bfloat16)
-    two_local = lax.dynamic_slice(top_two, (0, z_idx * blk_cols), (top_two.shape[0], blk_cols))
+    two_local = [
+        lax.dynamic_slice(
+            top_two, (0, x_idx * out_cols + start), (top_two.shape[0], blk_cols)
+        )
+        for start in range(0, out_cols, blk_cols)
+    ]
     weights = lax.all_gather(
-        jnp.concatenate([one_local, two_local], axis=0), "grp", axis=0, tiled=False
+        jnp.concatenate([one_local, *two_local], axis=0), "grp", axis=0, tiled=False
     )
 
     first_slot = (owner_idx * slot_count).astype(jnp.int32).reshape(1)
@@ -268,13 +287,18 @@
     ).astype(jnp.bfloat16)
     code_perm = moved_codes(shuffled, fixed, moved_width)
     codes = jnp.concatenate([code_fixed, code_base, code_perm], axis=1)
-    codes_all = lax.all_gather(
-        codes, "tbl", axis=0, tiled=False, axis_index_groups=along_z
-    )
-    out_w = lax.dynamic_slice(top_out, (z_idx * blk_cols,), (blk_cols,)).reshape(1, blk_cols)
-    part = top_layers(codes_all, weights, out_w.astype(jnp.float32))
+    codes_all = lax.all_to_all(
+        jnp.broadcast_to(codes[None], (xs, *codes.shape)),
+        "tbl",
+        split_axis=0,
+        concat_axis=0,
+        tiled=True,
+        axis_index_groups=along_x,
+    )
+    out_w = lax.dynamic_slice(top_out, (x_idx * out_cols,), (out_cols,)).reshape(1, out_cols)
+    part = top_layers(codes_all, weights, out_w.astype(jnp.float32), in_width)
     pieces = lax.all_to_all(
-        part, "tbl", split_axis=0, concat_axis=0, tiled=True, axis_index_groups=along_z
+        part, "tbl", split_axis=0, concat_axis=0, tiled=True, axis_index_groups=along_x
     )
     return jax.nn.sigmoid(jnp.sum(pieces, axis=0))
 

time: 127 us -> 110 us (0.87)
  the two profiles are of different devices: /device:TPU:2 before, /device:TPU:1 now
where the time goes in v4:
time: 110 us; the launch traced here: 108 us
  blocking collectives  31.9 us (29%)
  Pallas kernels  18.4 us (17%)
  starting transfers between devices  17.1 us (16%)
  waiting for transfers between devices  15.6 us (14%)
  between operations  13.8 us (13%)
  matrix products  5.27 us (5%)
  other arithmetic  3.52 us (3%)
  local copies, waits for them, and re-layouts  2.76 us (3%)
    all_gather x1, blocking collectives, local(): gathered = lax.all_gather(embedded[:NPERM], 'grp', axis=1, tiled=True)  24.6 us
    all_to_all x1, starting transfers between devices, local(): lax.all_to_all(pooled, 'tbl', split_axis=0, concat_axis=0, tiled=True)  13.7 us
    all_to_all x1, waiting for transfers between devices, local(): lax.all_to_all(pooled, 'tbl', split_axis=0, concat_axis=0, tiled=True)  11.6 us
    pallas_call x1, Pallas kernels, pool_slots(): pl.pallas_call(pool_kernel, grid_spec=pltpu.PrefetchScalarGridSpec(num_sc...  10.8 us
    pallas_call x1, Pallas kernels, top_layers(): pl.pallas_call(functools.partial(top_kernel, in_width), grid=(steps,), in...  7.57 us
    all_to_all x1, blocking collectives, local(): lax.all_to_all(part, 'tbl', split_axis=0, concat_axis=0, tiled=True, axis...  7.33 us
    all_to_all x1, waiting for transfers between devices, local(): lax.all_to_all(jnp.broadcast_to(codes[None], (xs, *codes.shape)), 'tbl',...  3.98 us
    all_to_all x1, starting transfers between devices, local(): lax.all_to_all(jnp.broadcast_to(codes[None], (xs, *codes.shape)), 'tbl',...  3.34 us
  transfers between devices with their start and end apart: 3, of which 2 were waited for; matrix products, arithmetic and copies ran while one was open for 7% of the time, Pallas kernels for 10%

profile of v4, /device:TPU:1, one launch (start us, length us, event | category | flops | bytes accessed | tf_op | source)
XLA Modules:
  0.0 108.3 jit_solution(2149950510324539897)
XLA Ops:
  6.5 0.0 copy-start
  6.5 0.0 all-gather.3.cloned.1.call-start
  6.5 1.4 %convolution_convert_fusion = bf16[512,256]{1,0:T(8,128)(2,1)S(1)} fusion(bf16[480,256]{1,0:T(8,128)(2,1)} %param.22, s32[512]{0:T(512)} %constant.71.clone), kind=kOutput, calls=%fused_computation | convolution fusion | flops 126205952 | bytes 509952 | tf_op jit(solution)/shard_map/dot_general | solution.py:250
  7.9 1.0 constant_dynamic-slice_fusion.1
  8.9 0.9 pad_maximum_fusion
  9.8 0.0 all-gather.3.cloned.1.call-update
  9.8 10.8 %shard_map.127 = bf16[32,2,32,128]{3,2,1,0:T(8,128)(2,1)} custom-call(s32[26]{0:T(128)} %map_ref.1, s32[1]{0:T(128)} %bitcast.2.owner_ref, s32[26,8,1024]{2,1,0:T(8,128)} %bitcast.85, s32[26,1024]{1,0:T(8,128)} %len_ref.1, bf16[2,2048,128]{2,1,0:T(8,128)(2,1)} %table_ref.1), custom_call_target="tpu_custom_call" | custom-call | tf_op jit(solution)/shard_map/pallas_call | solution.py:93
  20.6 13.7 %all-to-all-start = ((bf16[32,2,32,128]{3,2,1,0:T(8,128)(2,1)}), bf16[32,2,32,128]{3,2,1,0:T(8,128)(2,1)S(1)}, u32[]{:S(2)}, u32[]{:S(2)}) async-start(bf16[32,2,32,128]{3,2,1,0:T(8,128)(2,1)} %shard_map.127), calls=%async_computation | async-start | bytes 1048576 | tf_op jit(solution)/shard_map/all_to_all | solution.py:265
  34.3 0.0 copy-done
  34.4 1.0 fusion.3
  35.4 1.0 fusion.4
  36.4 0.7 fusion.42
  37.1 11.6 %all-to-all-done = bf16[32,2,32,128]{3,2,1,0:T(8,128)(2,1)S(1)} async-done(((bf16[32,2,32,128]{3,2,1,0:T(8,128)(2,1)}), bf16[32,2,32,128]{3,2,1,0:T(8,128)(2,1)S(1)}, u32[]{:S(2)}, u32[]{:S(2)}) %all-to-all-start) | async-done | bytes 524320 | tf_op jit(solution)/shard_map/all_to_all | solution.py:265
  48.7 0.9 convolution_convert_fusion.1
  49.6 0.1 slice.159
  49.7 24.6 %all_gather.9 = bf16[4,512,128]{2,0,1:T(4,128)(2,1)S(1)} all-gather(bf16[4,32,128]{2,0,1:T(4,128)(2,1)S(1)} %slice.182), channel_id=1, replica_groups=mesh['grp'=16,'tbl'=32] {'grp'}, dimensions={1}, use_global_device_ids=true | all-gather | bytes 557056 | tf_op jit(solution)/shard_map/all_gather | solution.py:277
  74.3 0.2 convolution_convert_fusion.2
  74.5 0.3 fusion.11
  74.8 0.3 fusion.8
  75.1 0.2 fusion.14
  75.6 0.1 concatenate.30
  75.8 0.1 fusion.37
  75.9 0.7 broadcast_in_dim.5
  76.6 3.3 %all-to-all-start.1 = ((bf16[4,32,640]{2,1,0:T(8,128)(2,1)}), bf16[4,32,640]{2,1,0:T(8,128)(2,1)S(1)}, u32[]{:S(2)}, u32[]{:S(2)}) async-start(bf16[4,32,640]{2,1,0:T(8,128)(2,1)} %broadcast_in_dim.5), calls=%async_computation.1 | async-start | bytes 327680 | tf_op jit(solution)/shard_map/all_to_all | solution.py:290
  80.0 1.3 %dynamic-slice_convert_fusion = f32[512]{0:T(512)} fusion(bf16[2048]{0:T(1024)(128)(2,1)} %param.24, s32[]{:T(128)S(6)} %select_n.26), kind=kLoop, calls=%fused_computation.89 | loop fusion | flops 512 | bytes 3076 | tf_op jit(solution)/shard_map/convert_element_type | solution.py:299
  81.3 4.0 %all-to-all-done.1.codes_ref = bf16[4,32,640]{2,1,0:T(8,128)(2,1)S(1)} async-done(((bf16[4,32,640]{2,1,0:T(8,128)(2,1)}), bf16[4,32,640]{2,1,0:T(8,128)(2,1)S(1)}, u32[]{:S(2)}, u32[]{:S(2)}) %all-to-all-start.1) | async-done | bytes 163872 | tf_op jit(solution)/shard_map/all_to_all | solution.py:290
  85.3 0.0 copy-start.1
  85.3 0.0 all-gather.3.cloned.1.call-done
  85.3 0.7 copy-done.1
  85.9 7.6 %shard_map.128 = f32[4,2,32]{2,1,0:T(2,128)} custom-call(bf16[4,32,640]{2,1,0:T(8,128)(2,1)} %copy-done.1, bf16[16,1024,256]{2,1,0:T(8,128)(2,1)} %bitcast.83, f32[1,512]{1,0:T(1,128)} %bitcast.88), custom_call_target="tpu_custom_call" | custom-call | tf_op jit(solution)/shard_map/pallas_call | solution.py:203
  93.5 7.3 %all_to_all.15 = f32[4,2,32]{2,1,0:T(2,128)S(1)} all-to-all(f32[4,2,32]{2,1,0:T(2,128)} %shard_map.128), channel_id=1, replica_groups={{0,8,16,24},{1,9,17,25},{2,10,18,26},{3,11,19,27},{4,12,20,28},{5,13,21..., dimensions={0} | all-to-all | bytes 2048 | tf_op jit(solution)/shard_map/all_to_all | solution.py:300
  100.9 0.6 add_divide_fusion
  (38 shorter events, 0.2 us)
Async XLA Ops:
  6.5 27.8 %copy-start = (bf16[512,256]{1,0:T(8,128)(2,1)S(1)}, bf16[512,256]{1,0:T(8,128)(2,1)}, u32[]{:S(2)}) copy-start(bf16[512,256]{1,0:T(8,128)(2,1)} %param.20) | copy-start | bytes 786436
  6.5 78.7 %all-gather.3.cloned.1.call-start = ((), (), s32[]{:S(2)}) async-start(), calls=%async_computation.3 | async-start | bytes 8912896 | tf_op jit(solution)/shard_map/all_gather | solution.py:257
  20.6 28.0 %all-to-all-start = ((bf16[32,2,32,128]{3,2,1,0:T(8,128)(2,1)}), bf16[32,2,32,128]{3,2,1,0:T(8,128)(2,1)S(1)}, u32[]{:S(2)}, u32[]{:S(2)}) async-start(bf16[32,2,32,128]{3,2,1,0:T(8,128)(2,1)} %shard_map.127), calls=%async_computation | async-start | bytes 1048576 | tf_op jit(solution)/shard_map/all_to_all | solution.py:265
  76.6 8.6 %all-to-all-start.1 = ((bf16[4,32,640]{2,1,0:T(8,128)(2,1)}), bf16[4,32,640]{2,1,0:T(8,128)(2,1)S(1)}, u32[]{:S(2)}, u32[]{:S(2)}) async-start(bf16[4,32,640]{2,1,0:T(8,128)(2,1)} %broadcast_in_dim.5), calls=%async_computation.1 | async-start | bytes 327680 | tf_op jit(solution)/shard_map/all_to_all | solution.py:290
  85.3 0.7 copy-start.1
Sparse Core Ops, SparseCore 0:
  9.9 66.9 all-gather.2

commit v5 on v4

v5 whole, which is shorter than its diff:
```python
import functools

import jax
import jax.numpy as jnp
import numpy as np
from jax import lax
from jax.experimental import pallas as pl
from jax.experimental.pallas import tpu as pltpu
from jax.sharding import PartitionSpec as P

NPERM = 4
LO = 256
ROWBLK = 16
TILE = 512
XS = 4


def dense_layer(inputs, weights):
    return jnp.maximum(jnp.dot(inputs, weights, preferred_element_type=jnp.float32), 0.0).astype(
        jnp.bfloat16
    )


def spread_bags(ids):
    sub = lax.broadcasted_iota(jnp.int32, ids.shape, 0)
    grp = lax.broadcasted_iota(jnp.int32, ids.shape, 1) // ROWBLK
    for step in (1, 2, 4):
        down = pltpu.roll(pltpu.roll(ids, 8 - step, 0), ROWBLK * step, 1)
        up = pltpu.roll(pltpu.roll(ids, step, 0), 128 - ROWBLK * step, 1)
        sub_bit = (sub & step) != 0
        grp_bit = (grp & step) != 0
        ids = jnp.where(sub_bit == grp_bit, ids, jnp.where(sub_bit, up, down))
    return ids


def pool_kernel(map_ref, owner_ref, *refs):
    slot_count = len(refs) - 6
    ids_refs = refs[:slot_count]
    len_ref, table_ref, out_ref, cnt_ref, local_ref, sem = refs[slot_count:]
    vocab = table_ref.shape[1]
    hi_count = vocab // LO
    height = hi_count * ROWBLK
    span = len_ref.shape[1]
    fetch = pltpu.make_async_copy(table_ref, local_ref, sem)
    fetch.start()
    row_id = lax.broadcasted_iota(jnp.int32, (height, 128), 0)
    col_id = lax.broadcasted_iota(jnp.int32, (height, 128), 1)
    target = jnp.where(row_id % ROWBLK == col_id % ROWBLK, row_id // ROWBLK, -1)
    target = target.astype(jnp.float32).astype(jnp.bfloat16).reshape(-1, 16, 128)
    lo_id = lax.broadcasted_iota(jnp.int32, (LO, 128), 0)
    lo_id = lo_id.astype(jnp.float32).astype(jnp.bfloat16).reshape(-1, 16, 128)
    one = jnp.ones((), jnp.bfloat16)
    zero = jnp.zeros((), jnp.bfloat16)
    blank = jnp.zeros((height, 128), jnp.bfloat16)
    feat_pos = lax.broadcasted_iota(jnp.int32, len_ref.shape, 0)

    def one_hot(row, wanted):
        row = jnp.broadcast_to(row, (16, 128)).astype(jnp.bfloat16)
        return jnp.where(row[None] == wanted, one, zero).reshape(-1, 128)

    for slot in range(slot_count):
        feat = find_feature(slot, map_ref, owner_ref)
        lens = jnp.sum(jnp.where(feat_pos == feat, len_ref[...], 0), axis=0, keepdims=True)
        for start in range(0, span, 128):
            ids = ids_refs[slot][0, :, start : start + 128]
            bag_pos = lax.broadcasted_iota(jnp.int32, ids.shape, 0)
            ids = spread_bags(jnp.where(bag_pos < lens[:, start : start + 128], ids, vocab))
            high = (ids // LO).astype(jnp.float32)
            low = (ids % LO).astype(jnp.float32)
            for blk in range(0, 8, 2):
                lhs = [one_hot(high[i : i + 1], target) for i in (blk, blk + 1)]
                rhs = [one_hot(low[i : i + 1], lo_id) for i in (blk, blk + 1)]
                lhs = jnp.concatenate(
                    [
                        jnp.concatenate([lhs[0], blank], axis=1),
                        jnp.concatenate([blank, lhs[1]], axis=1),
                    ],
                    axis=0,
                )
                counts = lax.dot_general(
                    lhs,
                    jnp.concatenate(rhs, axis=1),
                    (((1,), (1,)), ((), ())),
                    preferred_element_type=jnp.float32,
                ).astype(jnp.bfloat16)
                for part in range(2 * hi_count):
                    row = start + (blk + part // hi_count) * ROWBLK
                    col = part % hi_count * LO
                    cnt_ref[slot, row : row + ROWBLK, col : col + LO] = counts[
                        part * ROWBLK : (part + 1) * ROWBLK
                    ]
        if slot == 0:
            fetch.wait()
        row_count = out_ref.shape[2]
        for start in range(0, span, TILE):
            pooled = jnp.dot(
                cnt_ref[slot, start : start + TILE],
                local_ref[slot],
                preferred_element_type=jnp.float32,
            ).astype(jnp.bfloat16)
            out_ref[start // row_count : (start + TILE) // row_count, slot] = pooled.reshape(
                TILE // row_count, row_count, out_ref.shape[3]
            )


def find_feature(slot, map_ref, owner_ref):
    wanted = owner_ref[0] + slot
    feat = jnp.int32(0)
    for idx in range(map_ref.shape[0]):
        feat = jnp.where(map_ref[idx] == wanted, idx, feat)
    return feat


def pool_slots(table_map, first_slot, ids_t, lengths, tables, owners, row_count):
    slot_count, vocab, dim = tables.shape
    feats, bag, span = ids_t.shape

    def ids_spec(slot):
        return pl.BlockSpec((1, bag, span), lambda i, m, o: (find_feature(slot, m, o), 0, 0))

    return pl.pallas_call(
        pool_kernel,
        grid_spec=pltpu.PrefetchScalarGridSpec(
            num_scalar_prefetch=2,
            grid=(1,),
            in_specs=[
                *[ids_spec(slot) for slot in range(slot_count)],
                pl.BlockSpec((feats, span), lambda i, m, o: (0, 0)),
                pl.BlockSpec(memory_space=pl.ANY),
            ],
            out_specs=pl.BlockSpec(
                (owners, slot_count, row_count, dim), lambda i, m, o: (0, 0, 0, 0)
            ),
            scratch_shapes=[
                pltpu.VMEM((slot_count, span, vocab), jnp.bfloat16),
                pltpu.VMEM(tables.shape, jnp.bfloat16),
                pltpu.SemaphoreType.DMA(()),
            ],
        ),
        out_shape=jax.ShapeDtypeStruct((owners, slot_count, row_count, dim), jnp.bfloat16),
    )(table_map, first_slot, *[ids_t] * slot_count, lengths, tables)


def pack_kernel(part_ref, cols_ref, one_ref, two_ref, out_ref, sems):
    blk_width = out_ref.shape[1]
    in_width = cols_ref.shape[1]
    count = (out_ref.shape[0] - in_width) // two_ref.shape[0]
    copies = []
    for blk in range(count):
        start = pl.multiple_of((part_ref[0] * count + blk) * blk_width, blk_width)
        copies.append(
            pltpu.make_async_copy(
                two_ref.at[:, pl.ds(start, blk_width)],
                out_ref.at[pl.ds(in_width + blk * two_ref.shape[0], two_ref.shape[0])],
                sems.at[blk],
            )
        )
        copies[-1].start()
    row = lax.broadcasted_iota(jnp.int32, (one_ref.shape[0], in_width), 0)
    pick = jnp.where(row == cols_ref[...], 1.0, 0.0).astype(jnp.bfloat16)
    out_ref[:in_width] = lax.dot_general(
        pick, one_ref[...], (((0,), (0,)), ((), ())), preferred_element_type=jnp.float32
    ).astype(jnp.bfloat16)
    for copy in copies:
        copy.wait()


def pack_weights(part, cols, top_one, top_two, out_cols):
    blk_width = top_one.shape[1]
    count = out_cols // blk_width
    whole = pl.BlockSpec(memory_space=pltpu.VMEM)
    rows = cols.shape[0] + count * top_two.shape[0]
    return pl.pallas_call(
        pack_kernel,
        in_specs=[
            pl.BlockSpec(memory_space=pltpu.SMEM),
            whole,
            whole,
            pl.BlockSpec(memory_space=pl.ANY),
        ],
        out_specs=whole,
        scratch_shapes=[pltpu.SemaphoreType.DMA((count,))],
        out_shape=jax.ShapeDtypeStruct((rows, blk_width), jnp.bfloat16),
    )(part.reshape(1), jnp.asarray(cols)[None], top_one, top_two)


def code_order(feats, dim, width):
    order = [0, *range(NPERM + 1, feats + 1), *range(1, NPERM + 1)]
    fixed = feats + 1 - NPERM

    def column(i, j):
        a, b = max(order[i], order[j]), min(order[i], order[j])
        return dim + a * (a - 1) // 2 + b

    cols = list(range(dim))
    cols += [column(i, j) for i in range(1, fixed) for j in range(i)]
    cols += [width - 1]
    cols += [-1] * (-len(cols) % 128)
    fixed_width = len(cols)
    cols += [column(i, j) for i in range(fixed, feats + 1) for j in range(i)]
    cols += [-1] * (-len(cols) % 128)
    return np.array(cols, np.int32), fixed_width


def fixed_codes(vectors, lead, fixed_width):
    gram = jnp.einsum("ird,jrd->rij", vectors, vectors, preferred_element_type=jnp.float32)
    pairs = [gram[:, level, :level] for level in range(1, vectors.shape[0])]
    out = jnp.concatenate([lead.astype(jnp.float32), *pairs], axis=1)
    return jnp.pad(out, ((0, 0), (0, fixed_width - out.shape[1]))).astype(jnp.bfloat16)


def moved_codes(moved, fixed, moved_width):
    every = jnp.concatenate([fixed, moved], axis=0)
    gram = jnp.einsum("ird,jrd->rij", moved, every, preferred_element_type=jnp.float32)
    pairs = [gram[:, i, : fixed.shape[0] + i] for i in range(moved.shape[0])]
    out = jnp.concatenate(pairs, axis=1)
    return jnp.pad(out, ((0, 0), (0, moved_width - out.shape[1]))).astype(jnp.bfloat16)


def top_kernel(in_width, codes_ref, weights_ref, out_w_ref, out_ref, acc_ref, codes_all_ref):
    step = pl.program_id(0)
    blk_width = weights_ref.shape[2]
    fixed_width = 2 * in_width - codes_ref.shape[2]

    @pl.when(step == 0)
    def _():
        codes = jnp.concatenate([codes_ref[x] for x in range(codes_ref.shape[0])], axis=0)
        rows = codes.shape[0]
        codes_all_ref[:rows] = codes[:, :in_width]
        codes_all_ref[rows:, :fixed_width] = codes[:, :fixed_width]
        codes_all_ref[rows:, fixed_width:] = codes[:, in_width:]
        acc_ref[...] = jnp.zeros_like(acc_ref)

    codes = codes_all_ref[...]
    hidden = []
    for blk in range(weights_ref.shape[0]):
        pre = jnp.dot(codes, weights_ref[blk, :in_width], preferred_element_type=jnp.float32)
        hidden.append(jnp.maximum(pre, 0.0).astype(jnp.bfloat16))
    for col in range(0, acc_ref.shape[1], blk_width):
        total = acc_ref[:, col : col + blk_width]
        row = in_width + col // blk_width * blk_width
        for blk in range(weights_ref.shape[0]):
            total += jnp.dot(
                hidden[blk],
                weights_ref[blk, row : row + blk_width],
                preferred_element_type=jnp.float32,
            )
        acc_ref[:, col : col + blk_width] = total

    @pl.when(step == pl.num_programs(0) - 1)
    def _():
        xs, variants, row_count = out_ref.shape
        scaled = jnp.maximum(acc_ref[...], 0.0) * out_w_ref[...]
        folded = scaled[:, :128]
        for lane in range(128, scaled.shape[1], 128):
            folded += scaled[:, lane : lane + 128]
        sums = jnp.sum(folded.T, axis=0, keepdims=True)
        for variant in range(variants):
            for x in range(xs):
                start = (variant * xs + x) * row_count
                out_ref[x, variant : variant + 1] = sums[:, start : start + row_count]


def top_layers(codes, weights, out_w, in_width):
    xs, row_count, _ = codes.shape
    groups, depth, blk_width = weights.shape
    steps = 2
    rows = 2 * xs * row_count
    return pl.pallas_call(
        functools.partial(top_kernel, in_width),
        grid=(steps,),
        in_specs=[
            pl.BlockSpec(memory_space=pltpu.VMEM),
            pl.BlockSpec((groups // steps, depth, blk_width), lambda i: (i, 0, 0)),
            pl.BlockSpec(memory_space=pltpu.VMEM),
        ],
        out_specs=pl.BlockSpec((xs, 2, row_count), lambda i: (0, 0, 0)),
        scratch_shapes=[
            pltpu.VMEM((rows, out_w.shape[1]), jnp.float32),
            pltpu.VMEM((rows, in_width), jnp.bfloat16),
        ],
        out_shape=jax.ShapeDtypeStruct((xs, 2, row_count), jnp.float32),
    )(codes, weights, out_w)


def local(
    dense_feats,
    sparse_ids,
    lengths,
    table_map,
    row_perm,
    tables,
    bottom_one,
    bottom_two,
    bottom_three,
    top_one,
    top_two,
    top_out,
):
    owners = lax.axis_size("tbl")
    owner_idx = lax.axis_index("tbl")
    xs = XS
    zs = owners // xs
    x_idx = owner_idx // zs
    along_x = [[x * zs + z for x in range(xs)] for z in range(zs)]
    out_cols = top_two.shape[1] // xs
    slot_count = tables.shape[0]
    row_count = dense_feats.shape[0]
    feats = sparse_ids.shape[0]
    dim = tables.shape[2]

    cols, fixed_width = code_order(feats, dim, top_one.shape[0])
    in_width = cols.shape[0]
    moved_width = in_width - fixed_width
    packed = pack_weights(x_idx.astype(jnp.int32), cols, top_one, top_two, out_cols)
    weights = lax.all_gather(packed, "grp", axis=0, tiled=False)

    first_slot = (owner_idx * slot_count).astype(jnp.int32).reshape(1)
    pooled = pool_slots(
        table_map, first_slot, sparse_ids.transpose(0, 2, 1), lengths, tables, owners, row_count
    )
    arrived = lax.all_to_all(pooled, "tbl", split_axis=0, concat_axis=0, tiled=True)
    arrived = arrived.reshape(owners * slot_count, row_count, dim)
    pick_slot = (
        table_map[:, None] == jnp.arange(owners * slot_count, dtype=jnp.int32)[None, :]
    ).astype(jnp.bfloat16)
    embedded = jnp.einsum(
        "fs,srd->frd", pick_slot, arrived, preferred_element_type=jnp.float32
    ).astype(jnp.bfloat16)

    bottom_out = dense_layer(
        dense_layer(dense_layer(dense_feats, bottom_one), bottom_two), bottom_three
    )
    gathered = lax.all_gather(embedded[:NPERM], "grp", axis=1, tiled=True)
    fixed = jnp.concatenate([bottom_out[None], embedded[NPERM:]], axis=0)
    code_fixed = fixed_codes(fixed, bottom_out, fixed_width)
    code_base = moved_codes(embedded[:NPERM], fixed, moved_width)
    source = row_perm // (owners * row_count) * row_count + row_perm % row_count
    pick_row = (source[:, None] == jnp.arange(gathered.shape[1], dtype=jnp.int32)[None, :]).astype(
        jnp.bfloat16
    )
    shuffled = jnp.einsum(
        "rs,psd->prd", pick_row, gathered, preferred_element_type=jnp.float32
    ).astype(jnp.bfloat16)
    code_perm = moved_codes(shuffled, fixed, moved_width)
    codes = jnp.concatenate([code_fixed, code_base, code_perm], axis=1)
    codes_all = lax.all_to_all(
        jnp.broadcast_to(codes[None], (xs, *codes.shape)),
        "tbl",
        split_axis=0,
        concat_axis=0,
        tiled=True,
        axis_index_groups=along_x,
    )
    out_w = lax.dynamic_slice(top_out, (x_idx * out_cols,), (out_cols,)).reshape(1, out_cols)
    part = top_layers(codes_all, weights, out_w.astype(jnp.float32), in_width)
    pieces = lax.all_to_all(
        part, "tbl", split_axis=0, concat_axis=0, tiled=True, axis_index_groups=along_x
    )
    return jax.nn.sigmoid(jnp.sum(pieces, axis=0))


def solution(mesh):
    placed = (
        P(("grp", "tbl"), None),
        P(None, "grp", None),
        P(None, "grp"),
        P(),
        P(("grp", "tbl")),
        P("tbl", None, None),
        P(),
        P(),
        P(),
        P(None, "grp"),
        P("grp", None),
        P(),
    )
    return jax.shard_map(
        local, mesh=mesh, in_specs=placed, out_specs=P(None, ("grp", "tbl")), check_vma=False
    )
```

time: 110 us -> 105 us (0.955)
  Pallas kernels: 18.4 us -> 15.9 us
  matrix products: 5.27 us -> 3.91 us
    pallas_call x1, Pallas kernels: 10.8 us -> 7.5 us  [pool_slots(): pl.pallas_call(pool_kernel, grid_spec=pltpu.PrefetchScalarGridSpec(num_sc...]
    pallas_call x0 -> x1, Pallas kernels: none -> 2.83 us  [pack_weights(): pl.pallas_call(pack_kernel, in_specs=[pl.BlockSpec(memory_space=pltpu.SME...]
    pallas_call x1, Pallas kernels: 7.57 us -> 5.56 us  [top_layers(): pl.pallas_call(functools.partial(top_kernel, in_width), grid=(steps,), in...]
    dot_general x1 -> x0, matrix products: 1.35 us -> none  [local(): jnp.dot(pick_col, top_one, preferred_element_type=jnp.float32)]
  transfers between devices with their start and end apart: 3 -> 3, of which waited for: 2 -> 2; matrix products, arithmetic and copies ran while one was open for 7% -> 7% of each run, Pallas kernels for 10% -> 7%
where the time goes in v5:
time: 105 us; the launch traced here: 103 us
  blocking collectives  32.4 us (31%)
  starting transfers between devices  17.1 us (16%)
  Pallas kernels  15.9 us (15%)
  waiting for transfers between devices  15.5 us (15%)
  between operations  13.8 us (13%)
  matrix products  3.91 us (4%)
  other arithmetic  2.71 us (3%)
  local copies, waits for them, and re-layouts  1.74 us (2%)
    all_gather x1, blocking collectives, local(): gathered = lax.all_gather(embedded[:NPERM], 'grp', axis=1, tiled=True)  25.1 us
    all_to_all x1, starting transfers between devices, local(): lax.all_to_all(pooled, 'tbl', split_axis=0, concat_axis=0, tiled=True)  13.7 us
    all_to_all x1, waiting for transfers between devices, local(): lax.all_to_all(pooled, 'tbl', split_axis=0, concat_axis=0, tiled=True)  11.6 us
    pallas_call x1, Pallas kernels, pool_slots(): pl.pallas_call(pool_kernel, grid_spec=pltpu.PrefetchScalarGridSpec(num_sc...  7.5 us
    all_to_all x1, blocking collectives, local(): lax.all_to_all(part, 'tbl', split_axis=0, concat_axis=0, tiled=True, axis...  7.33 us
    pallas_call x1, Pallas kernels, top_layers(): pl.pallas_call(functools.partial(top_kernel, in_width), grid=(steps,), in...  5.56 us
    all_to_all x1, waiting for transfers between devices, local(): lax.all_to_all(jnp.broadcast_to(codes[None], (xs, *codes.shape)), 'tbl',...  3.91 us
    all_to_all x1, starting transfers between devices, local(): lax.all_to_all(jnp.broadcast_to(codes[None], (xs, *codes.shape)), 'tbl',...  3.34 us
  transfers between devices with their start and end apart: 3, of which 2 were waited for; matrix products, arithmetic and copies ran while one was open for 7% of the time, Pallas kernels for 7%

profile of v5, /device:TPU:1, one launch (start us, length us, event | category | flops | bytes accessed | tf_op | source)
XLA Modules:
  0.0 103.0 jit_solution(206790080992502921)
XLA Ops:
  6.5 0.0 copy-start
  6.5 0.0 all-gather.3.cloned.1.call-start
  6.5 2.8 %shard_map.128 = bf16[1024,256]{1,0:T(8,128)(2,1)} custom-call(s32[1]{0:T(128)} %bitcast.37.part_ref, s32[1,512]{1,0:T(1,128)} %constant.77.cols_ref, bf16[480,256]{1,0:T(8,128)(2,1)} %one_ref.1, bf16[256,2048]{1,0:T(8,128)(2,1)} %two_ref.1), custom_call_target="tpu_custom_call" | custom-call | tf_op jit(solution)/shard_map/pallas_call | solution.py:173
  9.4 0.0 all-gather.3.cloned.1.call-update
  9.4 7.5 %shard_map.127 = bf16[32,2,32,128]{3,2,1,0:T(8,128)(2,1)} custom-call(s32[26]{0:T(128)} %map_ref.1, s32[1]{0:T(128)} %bitcast.2.owner_ref, s32[26,8,1024]{2,1,0:T(8,128)} %bitcast.84, s32[26,8,1024]{2,1,0:T(8,128)} %bitcast.85, s32[26,1024]{1,0:T(8,128)} %refs_2_.1, bf16[2,2048,128]{2,1,0:T(8,128)(2,1)} %refs_3_.1), custom_call_target="tpu_custom_call" | custom-call | tf_op jit(solution)/shard_map/pallas_call | solution.py:121
  16.9 13.7 %all-to-all-start = ((bf16[32,2,32,128]{3,2,1,0:T(8,128)(2,1)}), bf16[32,2,32,128]{3,2,1,0:T(8,128)(2,1)S(1)}, u32[]{:S(2)}, u32[]{:S(2)}) async-start(bf16[32,2,32,128]{3,2,1,0:T(8,128)(2,1)} %shard_map.127), calls=%async_computation | async-start | bytes 1048576 | tf_op jit(solution)/shard_map/all_to_all | solution.py:322
  30.7 0.0 copy-done
  30.7 1.0 fusion.3
  31.7 1.0 fusion.4
  32.7 0.7 fusion.41
  33.4 11.6 %all-to-all-done = bf16[32,2,32,128]{3,2,1,0:T(8,128)(2,1)S(1)} async-done(((bf16[32,2,32,128]{3,2,1,0:T(8,128)(2,1)}), bf16[32,2,32,128]{3,2,1,0:T(8,128)(2,1)S(1)}, u32[]{:S(2)}, u32[]{:S(2)}) %all-to-all-start) | async-done | bytes 524320 | tf_op jit(solution)/shard_map/all_to_all | solution.py:322
  45.0 0.9 convolution_convert_fusion
  45.9 0.1 slice.159
  46.0 25.1 %all_gather.9 = bf16[4,512,128]{2,0,1:T(4,128)(2,1)S(1)} all-gather(bf16[4,32,128]{2,0,1:T(4,128)(2,1)S(1)} %slice.182), channel_id=1, replica_groups=mesh['grp'=16,'tbl'=32] {'grp'}, dimensions={1}, use_global_device_ids=true | all-gather | bytes 557056 | tf_op jit(solution)/shard_map/all_gather | solution.py:334
  71.1 0.2 convolution_convert_fusion.1
  71.3 0.3 fusion.10
  71.6 0.3 fusion.7
  71.9 0.2 fusion.13
  72.4 0.1 concatenate.27
  72.6 0.1 fusion.36
  72.7 0.7 broadcast_in_dim.7
  73.4 3.3 %all-to-all-start.1 = ((bf16[4,32,640]{2,1,0:T(8,128)(2,1)}), bf16[4,32,640]{2,1,0:T(8,128)(2,1)S(1)}, u32[]{:S(2)}, u32[]{:S(2)}) async-start(bf16[4,32,640]{2,1,0:T(8,128)(2,1)} %broadcast_in_dim.7), calls=%async_computation.1 | async-start | bytes 327680 | tf_op jit(solution)/shard_map/all_to_all | solution.py:347
  76.8 1.3 %dynamic-slice_convert_fusion = f32[512]{0:T(512)} fusion(bf16[2048]{0:T(1024)(128)(2,1)} %param.24, s32[]{:T(128)S(6)} %select_n.22), kind=kLoop, calls=%fused_computation.85 | loop fusion | flops 512 | bytes 3076 | tf_op jit(solution)/shard_map/convert_element_type | solution.py:356
  78.1 3.9 %all-to-all-done.1.codes_ref = bf16[4,32,640]{2,1,0:T(8,128)(2,1)S(1)} async-done(((bf16[4,32,640]{2,1,0:T(8,128)(2,1)}), bf16[4,32,640]{2,1,0:T(8,128)(2,1)S(1)}, u32[]{:S(2)}, u32[]{:S(2)}) %all-to-all-start.1) | async-done | bytes 163872 | tf_op jit(solution)/shard_map/all_to_all | solution.py:347
  82.0 0.0 copy-start.1
  82.0 0.0 all-gather.3.cloned.1.call-done
  82.0 0.7 copy-done.1
  82.7 5.6 %shard_map.129 = f32[4,2,32]{2,1,0:T(2,128)} custom-call(bf16[4,32,640]{2,1,0:T(8,128)(2,1)} %copy-done.1, bf16[16,1024,256]{2,1,0:T(8,128)(2,1)} %bitcast.83, f32[1,512]{1,0:T(1,128)} %bitcast.89), custom_call_target="tpu_custom_call" | custom-call | tf_op jit(solution)/shard_map/pallas_call | solution.py:269
  88.3 7.3 %all_to_all.15 = f32[4,2,32]{2,1,0:T(2,128)S(1)} all-to-all(f32[4,2,32]{2,1,0:T(2,128)} %shard_map.129), channel_id=1, replica_groups={{0,8,16,24},{1,9,17,25},{2,10,18,26},{3,11,19,27},{4,12,20,28},{5,13,21..., dimensions={0} | all-to-all | bytes 2048 | tf_op jit(solution)/shard_map/all_to_all | solution.py:357
  95.6 0.6 add_divide_fusion
  (38 shorter events, 0.2 us)
Async XLA Ops:
  6.5 24.1 %copy-start = (bf16[512,256]{1,0:T(8,128)(2,1)S(1)}, bf16[512,256]{1,0:T(8,128)(2,1)}, u32[]{:S(2)}) copy-start(bf16[512,256]{1,0:T(8,128)(2,1)} %param.20) | copy-start | bytes 786436
  6.5 75.5 %all-gather.3.cloned.1.call-start = ((), (), s32[]{:S(2)}) async-start(), calls=%async_computation.3 | async-start | bytes 8912896 | tf_op jit(solution)/shard_map/all_gather | solution.py:316
  16.9 28.1 %all-to-all-start = ((bf16[32,2,32,128]{3,2,1,0:T(8,128)(2,1)}), bf16[32,2,32,128]{3,2,1,0:T(8,128)(2,1)S(1)}, u32[]{:S(2)}, u32[]{:S(2)}) async-start(bf16[32,2,32,128]{3,2,1,0:T(8,128)(2,1)} %shard_map.127), calls=%async_computation | async-start | bytes 1048576 | tf_op jit(solution)/shard_map/all_to_all | solution.py:322
  73.4 8.6 %all-to-all-start.1 = ((bf16[4,32,640]{2,1,0:T(8,128)(2,1)}), bf16[4,32,640]{2,1,0:T(8,128)(2,1)S(1)}, u32[]{:S(2)}, u32[]{:S(2)}) async-start(bf16[4,32,640]{2,1,0:T(8,128)(2,1)} %broadcast_in_dim.7), calls=%async_computation.1 | async-start | bytes 327680 | tf_op jit(solution)/shard_map/all_to_all | solution.py:347
  82.0 0.7 copy-start.1
Sparse Core Ops, SparseCore 0:
  9.5 66.9 all-gather.2

commit v6 on v5

--- a/solution.py
+++ b/solution.py
@@ -33,16 +33,33 @@
     return ids
 
 
-def pool_kernel(map_ref, owner_ref, *refs):
-    slot_count = len(refs) - 6
+def pool_kernel(map_ref, owner_ref, part_ref, *refs):
+    slot_count = len(refs) - 13
     ids_refs = refs[:slot_count]
-    len_ref, table_ref, out_ref, cnt_ref, local_ref, sem = refs[slot_count:]
+    len_ref, cols_ref, table_ref, one_ref, two_ref, out_ref, packed_ref = refs[slot_count:-6]
+    cnt_ref, local_ref, first_ref, pack_ref, sem, sems = refs[-6:]
     vocab = table_ref.shape[1]
     hi_count = vocab // LO
     height = hi_count * ROWBLK
     span = len_ref.shape[1]
     fetch = pltpu.make_async_copy(table_ref, local_ref, sem)
     fetch.start()
+    in_width = cols_ref.shape[1]
+    depth, blk_width = two_ref.shape[0], one_ref.shape[1]
+    count = (pack_ref.shape[0] - in_width) // depth
+    loads = [pltpu.make_async_copy(one_ref, first_ref, sems.at[0])]
+    for blk in range(count):
+        start = pl.multiple_of((part_ref[0] * count + blk) * blk_width, blk_width)
+        loads.append(
+            pltpu.make_async_copy(
+                two_ref.at[:, pl.ds(start, blk_width)],
+                pack_ref.at[pl.ds(in_width + blk * depth, depth)],
+                sems.at[1 + blk],
+            )
+        )
+    for load in loads:
+        load.start()
+    send = pltpu.make_async_copy(pack_ref, packed_ref, sems.at[1 + count])
     row_id = lax.broadcasted_iota(jnp.int32, (height, 128), 0)
     col_id = lax.broadcasted_iota(jnp.int32, (height, 128), 1)
     target = jnp.where(row_id % ROWBLK == col_id % ROWBLK, row_id // ROWBLK, -1)
@@ -90,6 +107,14 @@
                         part * ROWBLK : (part + 1) * ROWBLK
                     ]
         if slot == 0:
+            for load in loads:
+                load.wait()
+            row = lax.broadcasted_iota(jnp.int32, (first_ref.shape[0], in_width), 0)
+            pick = jnp.where(row == cols_ref[...], 1.0, 0.0).astype(jnp.bfloat16)
+            pack_ref[:in_width] = lax.dot_general(
+                pick, first_ref[...], (((0,), (0,)), ((), ())), preferred_element_type=jnp.float32
+            ).astype(jnp.bfloat16)
+            send.start()
             fetch.wait()
         row_count = out_ref.shape[2]
         for start in range(0, span, TILE):
@@ -101,6 +126,7 @@
             out_ref[start // row_count : (start + TILE) // row_count, slot] = pooled.reshape(
                 TILE // row_count, row_count, out_ref.shape[3]
             )
+    send.wait()
 
 
 def find_feature(slot, map_ref, owner_ref):
@@ -111,77 +137,59 @@
     return feat
 
 
-def pool_slots(table_map, first_slot, ids_t, lengths, tables, owners, row_count):
+def pool_slots(
+    table_map, first_slot, part, ids_t, lengths, tables, cols, top_one, top_two, dims
+):
+    owners, row_count, out_cols = dims
     slot_count, vocab, dim = tables.shape
     feats, bag, span = ids_t.shape
+    blk_width = top_one.shape[1]
+    count = out_cols // blk_width
+    packed = (cols.shape[0] + count * top_two.shape[0], blk_width)
+    pooled = (owners, slot_count, row_count, dim)
+    away = pl.BlockSpec(memory_space=pl.ANY)
 
     def ids_spec(slot):
-        return pl.BlockSpec((1, bag, span), lambda i, m, o: (find_feature(slot, m, o), 0, 0))
+        return pl.BlockSpec((1, bag, span), lambda i, m, o, p: (find_feature(slot, m, o), 0, 0))
 
     return pl.pallas_call(
         pool_kernel,
         grid_spec=pltpu.PrefetchScalarGridSpec(
-            num_scalar_prefetch=2,
+            num_scalar_prefetch=3,
             grid=(1,),
             in_specs=[
                 *[ids_spec(slot) for slot in range(slot_count)],
-                pl.BlockSpec((feats, span), lambda i, m, o: (0, 0)),
-                pl.BlockSpec(memory_space=pl.ANY),
+                pl.BlockSpec((feats, span), lambda i, m, o, p: (0, 0)),
+                pl.BlockSpec((1, cols.shape[0]), lambda i, m, o, p: (0, 0)),
+                away,
+                away,
+                away,
             ],
-            out_specs=pl.BlockSpec(
-                (owners, slot_count, row_count, dim), lambda i, m, o: (0, 0, 0, 0)
-            ),
+            out_specs=[pl.BlockSpec(pooled, lambda i, m, o, p: (0, 0, 0, 0)), away],
             scratch_shapes=[
                 pltpu.VMEM((slot_count, span, vocab), jnp.bfloat16),
                 pltpu.VMEM(tables.shape, jnp.bfloat16),
+                pltpu.VMEM(top_one.shape, jnp.bfloat16),
+                pltpu.VMEM(packed, jnp.bfloat16),
                 pltpu.SemaphoreType.DMA(()),
+                pltpu.SemaphoreType.DMA((count + 2,)),
             ],
         ),
-        out_shape=jax.ShapeDtypeStruct((owners, slot_count, row_count, dim), jnp.bfloat16),
-    )(table_map, first_slot, *[ids_t] * slot_count, lengths, tables)
-
-
-def pack_kernel(part_ref, cols_ref, one_ref, two_ref, out_ref, sems):
-    blk_width = out_ref.shape[1]
-    in_width = cols_ref.shape[1]
-    count = (out_ref.shape[0] - in_width) // two_ref.shape[0]
-    copies = []
-    for blk in range(count):
-        start = pl.multiple_of((part_ref[0] * count + blk) * blk_width, blk_width)
-        copies.append(
-            pltpu.make_async_copy(
-                two_ref.at[:, pl.ds(start, blk_width)],
-                out_ref.at[pl.ds(in_width + blk * two_ref.shape[0], two_ref.shape[0])],
-                sems.at[blk],
-            )
-        )
-        copies[-1].start()
-    row = lax.broadcasted_iota(jnp.int32, (one_ref.shape[0], in_width), 0)
-    pick = jnp.where(row == cols_ref[...], 1.0, 0.0).astype(jnp.bfloat16)
-    out_ref[:in_width] = lax.dot_general(
-        pick, one_ref[...], (((0,), (0,)), ((), ())), preferred_element_type=jnp.float32
-    ).astype(jnp.bfloat16)
-    for copy in copies:
-        copy.wait()
-
-
-def pack_weights(part, cols, top_one, top_two, out_cols):
-    blk_width = top_one.shape[1]
-    count = out_cols // blk_width
-    whole = pl.BlockSpec(memory_space=pltpu.VMEM)
-    rows = cols.shape[0] + count * top_two.shape[0]
-    return pl.pallas_call(
-        pack_kernel,
-        in_specs=[
-            pl.BlockSpec(memory_space=pltpu.SMEM),
-            whole,
-            whole,
-            pl.BlockSpec(memory_space=pl.ANY),
+        out_shape=[
+            jax.ShapeDtypeStruct(pooled, jnp.bfloat16),
+            jax.ShapeDtypeStruct(packed, jnp.bfloat16),
         ],
-        out_specs=whole,
-        scratch_shapes=[pltpu.SemaphoreType.DMA((count,))],
-        out_shape=jax.ShapeDtypeStruct((rows, blk_width), jnp.bfloat16),
-    )(part.reshape(1), jnp.asarray(cols)[None], top_one, top_two)
+    )(
+        table_map,
+        first_slot,
+        part,
+        *[ids_t] * slot_count,
+        lengths,
+        jnp.asarray(cols)[None],
+        tables,
+        top_one,
+        top_two,
+    )
 
 
 def code_order(feats, dim, width):
@@ -312,13 +320,20 @@
     cols, fixed_width = code_order(feats, dim, top_one.shape[0])
     in_width = cols.shape[0]
     moved_width = in_width - fixed_width
-    packed = pack_weights(x_idx.astype(jnp.int32), cols, top_one, top_two, out_cols)
+    first_slot = (owner_idx * slot_count).astype(jnp.int32).reshape(1)
+    pooled, packed = pool_slots(
+        table_map,
+        first_slot,
+        x_idx.astype(jnp.int32).reshape(1),
+        sparse_ids.transpose(0, 2, 1),
+        lengths,
+        tables,
+        cols,
+        top_one,
+        top_two,
+        (owners, row_count, out_cols),
+    )
     weights = lax.all_gather(packed, "grp", axis=0, tiled=False)
-
-    first_slot = (owner_idx * slot_count).astype(jnp.int32).reshape(1)
-    pooled = pool_slots(
-        table_map, first_slot, sparse_ids.transpose(0, 2, 1), lengths, tables, owners, row_count
-    )
     arrived = lax.all_to_all(pooled, "tbl", split_axis=0, concat_axis=0, tiled=True)
     arrived = arrived.reshape(owners * slot_count, row_count, dim)
     pick_slot = (

time: 105 us -> 104 us (level)
  waiting for transfers between devices: 15.5 us -> 17.6 us
  Pallas kernels: 15.9 us -> 13.8 us
    pallas_call x1 -> x0, Pallas kernels: 2.83 us -> none  [pack_weights(): pl.pallas_call(pack_kernel, in_specs=[pl.BlockSpec(memory_space=pltpu.SME...]
    all_gather x1, waiting for transfers between devices: 0.01 us -> 1.93 us  [local(): weights = lax.all_gather(packed, 'grp', axis=0, tiled=False)]
  transfers between devices with their start and end apart: 3 -> 3, of which waited for: 2 -> 3; matrix products, arithmetic and copies ran while one was open for 7% -> 7% of each run, Pallas kernels for 7% -> 0%
where the time goes in v6:
time: 104 us; the launch traced here: 103 us
  blocking collectives  33.1 us (32%)
  waiting for transfers between devices  17.6 us (17%)
  starting transfers between devices  17.1 us (16%)
  Pallas kernels  13.8 us (13%)
  between operations  13.8 us (13%)
  matrix products  3.92 us (4%)
  other arithmetic  2.67 us (3%)
  local copies, waits for them, and re-layouts  1.09 us (1%)
    all_gather x1, blocking collectives, local(): gathered = lax.all_gather(embedded[:NPERM], 'grp', axis=1, tiled=True)  25 us
    all_to_all x1, starting transfers between devices, local(): lax.all_to_all(pooled, 'tbl', split_axis=0, concat_axis=0, tiled=True)  13.7 us
    all_to_all x1, waiting for transfers between devices, local(): lax.all_to_all(pooled, 'tbl', split_axis=0, concat_axis=0, tiled=True)  11.6 us
    pallas_call x1, Pallas kernels, pool_slots(): pl.pallas_call(pool_kernel, grid_spec=pltpu.PrefetchScalarGridSpec(num_sc...  8.27 us
    all_to_all x1, blocking collectives, local(): lax.all_to_all(part, 'tbl', split_axis=0, concat_axis=0, tiled=True, axis...  8.1 us
    pallas_call x1, Pallas kernels, top_layers(): pl.pallas_call(functools.partial(top_kernel, in_width), grid=(steps,), in...  5.56 us
    all_to_all x1, waiting for transfers between devices, local(): lax.all_to_all(jnp.broadcast_to(codes[None], (xs, *codes.shape)), 'tbl',...  4.01 us
    all_to_all x1, starting transfers between devices, local(): lax.all_to_all(jnp.broadcast_to(codes[None], (xs, *codes.shape)), 'tbl',...  3.35 us
  transfers between devices with their start and end apart: 3, of which 3 were waited for; matrix products, arithmetic and copies ran while one was open for 7% of the time, Pallas kernels for 0%

profile of v6, /device:TPU:1, one launch (start us, length us, event | category | flops | bytes accessed | tf_op | source)
XLA Modules:
  0.0 103.0 jit_solution(3168501557587209772)
XLA Ops:
  6.5 0.0 copy-start
  6.5 0.0 all-gather.3.cloned.1.call-start
  6.5 8.3 %shard_map.127 = (bf16[32,2,32,128]{3,2,1,0:T(8,128)(2,1)}, bf16[1024,256]{1,0:T(8,128)(2,1)}) custom-call(s32[26]{0:T(128)} %map_ref.1, s32[1]{0:T(128)} %bitcast.2.owner_ref, s32[1]{0:T(128)} %bitcast.3.part_ref, s32[26,8,1024]{2,1,0:T(8,128)} %bitcast.84, s32[26,8,1024]{2,1,0:T(8,128)} %bitcast.85, s32[26,1024]{1,0:T(8,128)} %refs_2_.1, ...), custom_call_target="tpu_custom_call" | custom-call | tf_op jit(solution)/shard_map/pallas_call | solution.py:155
  14.8 0.0 all-gather.3.cloned.1.call-update
  14.8 13.7 %all-to-all-start = ((bf16[32,2,32,128]{3,2,1,0:T(8,128)(2,1)}), bf16[32,2,32,128]{3,2,1,0:T(8,128)(2,1)S(1)}, u32[]{:S(2)}, u32[]{:S(2)}) async-start(bf16[32,2,32,128]{3,2,1,0:T(8,128)(2,1)} %get-tuple-element.7), calls=%async_computation | async-start | bytes 1048576 | tf_op jit(solution)/shard_map/all_to_all | solution.py:337
  28.6 0.0 copy-done
  28.6 1.0 fusion.3
  29.6 1.0 fusion.4
  30.6 0.7 fusion.41
  31.3 11.6 %all-to-all-done = bf16[32,2,32,128]{3,2,1,0:T(8,128)(2,1)S(1)} async-done(((bf16[32,2,32,128]{3,2,1,0:T(8,128)(2,1)}), bf16[32,2,32,128]{3,2,1,0:T(8,128)(2,1)S(1)}, u32[]{:S(2)}, u32[]{:S(2)}) %all-to-all-start) | async-done | bytes 524320 | tf_op jit(solution)/shard_map/all_to_all | solution.py:337
  42.9 0.9 convolution_convert_fusion
  43.9 0.1 slice.159
  43.9 25.0 %all_gather.9 = bf16[4,512,128]{2,0,1:T(4,128)(2,1)S(1)} all-gather(bf16[4,32,128]{2,0,1:T(4,128)(2,1)S(1)} %slice.182), channel_id=1, replica_groups=mesh['grp'=16,'tbl'=32] {'grp'}, dimensions={1}, use_global_device_ids=true | all-gather | bytes 557056 | tf_op jit(solution)/shard_map/all_gather | solution.py:349
  69.0 0.2 convolution_convert_fusion.1
  69.2 0.3 fusion.10
  69.5 0.3 fusion.7
  69.8 0.2 fusion.13
  70.3 0.1 concatenate.27
  70.5 0.1 fusion.36
  70.6 0.7 broadcast_in_dim.8
  71.3 3.3 %all-to-all-start.1 = ((bf16[4,32,640]{2,1,0:T(8,128)(2,1)}), bf16[4,32,640]{2,1,0:T(8,128)(2,1)S(1)}, u32[]{:S(2)}, u32[]{:S(2)}) async-start(bf16[4,32,640]{2,1,0:T(8,128)(2,1)} %broadcast_in_dim.8), calls=%async_computation.1 | async-start | bytes 327680 | tf_op jit(solution)/shard_map/all_to_all | solution.py:362
  74.7 1.3 %dynamic-slice_convert_fusion = f32[512]{0:T(512)} fusion(bf16[2048]{0:T(1024)(128)(2,1)} %param.24, s32[]{:T(128)S(6)} %select_n.22), kind=kLoop, calls=%fused_computation.85 | loop fusion | flops 512 | bytes 3076 | tf_op jit(solution)/shard_map/convert_element_type | solution.py:371
  76.0 4.0 %all-to-all-done.1.codes_ref = bf16[4,32,640]{2,1,0:T(8,128)(2,1)S(1)} async-done(((bf16[4,32,640]{2,1,0:T(8,128)(2,1)}), bf16[4,32,640]{2,1,0:T(8,128)(2,1)S(1)}, u32[]{:S(2)}, u32[]{:S(2)}) %all-to-all-start.1) | async-done | bytes 163872 | tf_op jit(solution)/shard_map/all_to_all | solution.py:362
  80.0 0.0 copy-start.1
  80.0 1.9 %all-gather.3.cloned.1.call-done = bf16[16384,256]{1,0:T(8,128)(2,1)} async-done(((bf16[1024,256]{1,0:T(8,128)(2,1)}), bf16[16384,256]{1,0:T(8,128)(2,1)}) %all-gather.3.cloned.1.call-update) | async-done | bytes 8388624 | tf_op jit(solution)/shard_map/all_gather | solution.py:336
  81.9 0.0 copy-done.1
  81.9 5.6 %shard_map.128 = f32[4,2,32]{2,1,0:T(2,128)} custom-call(bf16[4,32,640]{2,1,0:T(8,128)(2,1)} %copy-done.1, bf16[16,1024,256]{2,1,0:T(8,128)(2,1)} %bitcast.83, f32[1,512]{1,0:T(1,128)} %bitcast.89), custom_call_target="tpu_custom_call" | custom-call | tf_op jit(solution)/shard_map/pallas_call | solution.py:277
  87.5 8.1 %all_to_all.15 = f32[4,2,32]{2,1,0:T(2,128)S(1)} all-to-all(f32[4,2,32]{2,1,0:T(2,128)} %shard_map.128), channel_id=1, replica_groups={{0,8,16,24},{1,9,17,25},{2,10,18,26},{3,11,19,27},{4,12,20,28},{5,13,21..., dimensions={0} | all-to-all | bytes 2048 | tf_op jit(solution)/shard_map/all_to_all | solution.py:372
  95.6 0.6 add_divide_fusion
  (38 shorter events, 0.2 us)
Async XLA Ops:
  6.5 22.0 %copy-start = (bf16[512,256]{1,0:T(8,128)(2,1)S(1)}, bf16[512,256]{1,0:T(8,128)(2,1)}, u32[]{:S(2)}) copy-start(bf16[512,256]{1,0:T(8,128)(2,1)} %param.20) | copy-start | bytes 786436
  6.5 75.4 %all-gather.3.cloned.1.call-start = ((), (), s32[]{:S(2)}) async-start(), calls=%async_computation.3 | async-start | bytes 8912896 | tf_op jit(solution)/shard_map/all_gather | solution.py:336
  14.8 28.1 %all-to-all-start = ((bf16[32,2,32,128]{3,2,1,0:T(8,128)(2,1)}), bf16[32,2,32,128]{3,2,1,0:T(8,128)(2,1)S(1)}, u32[]{:S(2)}, u32[]{:S(2)}) async-start(bf16[32,2,32,128]{3,2,1,0:T(8,128)(2,1)} %get-tuple-element.7), calls=%async_computation | async-start | bytes 1048576 | tf_op jit(solution)/shard_map/all_to_all | solution.py:337
  71.3 8.7 %all-to-all-start.1 = ((bf16[4,32,640]{2,1,0:T(8,128)(2,1)}), bf16[4,32,640]{2,1,0:T(8,128)(2,1)S(1)}, u32[]{:S(2)}, u32[]{:S(2)}) async-start(bf16[4,32,640]{2,1,0:T(8,128)(2,1)} %broadcast_in_dim.8), calls=%async_computation.1 | async-start | bytes 327680 | tf_op jit(solution)/shard_map/all_to_all | solution.py:362
  80.0 1.9 %copy-start.1 = (bf16[4,32,640]{2,1,0:T(8,128)(2,1)}, bf16[4,32,640]{2,1,0:T(8,128)(2,1)S(1)}, u32[]{:S(2)}) copy-start(bf16[4,32,640]{2,1,0:T(8,128)(2,1)S(1)} %all-to-all-done.1.codes_ref) | copy-start | bytes 491524
Sparse Core Ops, SparseCore 0:
  15.0 66.9 all-gather.2

commit v7 on v6

--- a/solution.py
+++ b/solution.py
@@ -33,33 +33,40 @@
     return ids
 
 
-def pool_kernel(map_ref, owner_ref, part_ref, *refs):
-    slot_count = len(refs) - 13
-    ids_refs = refs[:slot_count]
-    len_ref, cols_ref, table_ref, one_ref, two_ref, out_ref, packed_ref = refs[slot_count:-6]
-    cnt_ref, local_ref, first_ref, pack_ref, sem, sems = refs[-6:]
-    vocab = table_ref.shape[1]
-    hi_count = vocab // LO
-    height = hi_count * ROWBLK
-    span = len_ref.shape[1]
-    fetch = pltpu.make_async_copy(table_ref, local_ref, sem)
-    fetch.start()
-    in_width = cols_ref.shape[1]
+def pack_loads(part_ref, one_ref, two_ref, first_ref, pack_ref, sems):
     depth, blk_width = two_ref.shape[0], one_ref.shape[1]
-    count = (pack_ref.shape[0] - in_width) // depth
+    count = sems.shape[0] - 2
+    in_rows = pack_ref.shape[0] - count * depth
     loads = [pltpu.make_async_copy(one_ref, first_ref, sems.at[0])]
     for blk in range(count):
         start = pl.multiple_of((part_ref[0] * count + blk) * blk_width, blk_width)
         loads.append(
             pltpu.make_async_copy(
                 two_ref.at[:, pl.ds(start, blk_width)],
-                pack_ref.at[pl.ds(in_width + blk * depth, depth)],
+                pack_ref.at[pl.ds(in_rows + blk * depth, depth)],
                 sems.at[1 + blk],
             )
         )
-    for load in loads:
-        load.start()
-    send = pltpu.make_async_copy(pack_ref, packed_ref, sems.at[1 + count])
+    return loads
+
+
+def pool_kernel(slot, map_ref, owner_ref, part_ref, ids_ref, len_ref, table_ref, *refs):
+    packs = slot == 0
+    cnt_ref, local_ref, sem = refs[-3:]
+    if packs:
+        cols_ref, one_ref, two_ref, out_ref, packed_ref, first_ref, pack_ref, sems = refs[:-3]
+        loads = pack_loads(part_ref, one_ref, two_ref, first_ref, pack_ref, sems)
+        for load in loads:
+            load.start()
+        send = pltpu.make_async_copy(pack_ref, packed_ref, sems.at[sems.shape[0] - 1])
+    else:
+        out_ref = refs[1]
+    fetch = pltpu.make_async_copy(table_ref.at[slot], local_ref, sem)
+    fetch.start()
+    vocab = local_ref.shape[0]
+    hi_count = vocab // LO
+    height = hi_count * ROWBLK
+    span = len_ref.shape[1]
     row_id = lax.broadcasted_iota(jnp.int32, (height, 128), 0)
     col_id = lax.broadcasted_iota(jnp.int32, (height, 128), 1)
     target = jnp.where(row_id % ROWBLK == col_id % ROWBLK, row_id // ROWBLK, -1)
@@ -69,64 +76,63 @@
     one = jnp.ones((), jnp.bfloat16)
     zero = jnp.zeros((), jnp.bfloat16)
     blank = jnp.zeros((height, 128), jnp.bfloat16)
-    feat_pos = lax.broadcasted_iota(jnp.int32, len_ref.shape, 0)
 
     def one_hot(row, wanted):
         row = jnp.broadcast_to(row, (16, 128)).astype(jnp.bfloat16)
         return jnp.where(row[None] == wanted, one, zero).reshape(-1, 128)
 
-    for slot in range(slot_count):
-        feat = find_feature(slot, map_ref, owner_ref)
-        lens = jnp.sum(jnp.where(feat_pos == feat, len_ref[...], 0), axis=0, keepdims=True)
-        for start in range(0, span, 128):
-            ids = ids_refs[slot][0, :, start : start + 128]
-            bag_pos = lax.broadcasted_iota(jnp.int32, ids.shape, 0)
-            ids = spread_bags(jnp.where(bag_pos < lens[:, start : start + 128], ids, vocab))
-            high = (ids // LO).astype(jnp.float32)
-            low = (ids % LO).astype(jnp.float32)
-            for blk in range(0, 8, 2):
-                lhs = [one_hot(high[i : i + 1], target) for i in (blk, blk + 1)]
-                rhs = [one_hot(low[i : i + 1], lo_id) for i in (blk, blk + 1)]
-                lhs = jnp.concatenate(
-                    [
-                        jnp.concatenate([lhs[0], blank], axis=1),
-                        jnp.concatenate([blank, lhs[1]], axis=1),
-                    ],
-                    axis=0,
-                )
-                counts = lax.dot_general(
-                    lhs,
-                    jnp.concatenate(rhs, axis=1),
-                    (((1,), (1,)), ((), ())),
-                    preferred_element_type=jnp.float32,
-                ).astype(jnp.bfloat16)
-                for part in range(2 * hi_count):
-                    row = start + (blk + part // hi_count) * ROWBLK
-                    col = part % hi_count * LO
-                    cnt_ref[slot, row : row + ROWBLK, col : col + LO] = counts[
-                        part * ROWBLK : (part + 1) * ROWBLK
-                    ]
-        if slot == 0:
+    feat_pos = lax.broadcasted_iota(jnp.int32, len_ref.shape, 0)
+    feat = find_feature(slot, map_ref, owner_ref)
+    lens = jnp.sum(jnp.where(feat_pos == feat, len_ref[...], 0), axis=0, keepdims=True)
+    for start in range(0, span, 128):
+        ids = ids_ref[0, :, start : start + 128]
+        bag_pos = lax.broadcasted_iota(jnp.int32, ids.shape, 0)
+        ids = spread_bags(jnp.where(bag_pos < lens[:, start : start + 128], ids, vocab))
+        high = (ids // LO).astype(jnp.float32)
+        low = (ids % LO).astype(jnp.float32)
+        for blk in range(0, 8, 2):
+            lhs = [one_hot(high[i : i + 1], target) for i in (blk, blk + 1)]
+            rhs = [one_hot(low[i : i + 1], lo_id) for i in (blk, blk + 1)]
+            lhs = jnp.concatenate(
+                [
+                    jnp.concatenate([lhs[0], blank], axis=1),
+                    jnp.concatenate([blank, lhs[1]], axis=1),
+                ],
+                axis=0,
+            )
+            counts = lax.dot_general(
+                lhs,
+                jnp.concatenate(rhs, axis=1),
+                (((1,), (1,)), ((), ())),
+                preferred_element_type=jnp.float32,
+            ).astype(jnp.bfloat16)
+            for part in range(2 * hi_count):
+                row = start + (blk + part // hi_count) * ROWBLK
+                col = part % hi_count * LO
+                cnt_ref[row : row + ROWBLK, col : col + LO] = counts[
+                    part * ROWBLK : (part + 1) * ROWBLK
+                ]
+        if packs and start == 0:
             for load in loads:
                 load.wait()
-            row = lax.broadcasted_iota(jnp.int32, (first_ref.shape[0], in_width), 0)
+            in_rows = cols_ref.shape[1]
+            row = lax.broadcasted_iota(jnp.int32, (first_ref.shape[0], in_rows), 0)
             pick = jnp.where(row == cols_ref[...], 1.0, 0.0).astype(jnp.bfloat16)
-            pack_ref[:in_width] = lax.dot_general(
+            pack_ref[:in_rows] = lax.dot_general(
                 pick, first_ref[...], (((0,), (0,)), ((), ())), preferred_element_type=jnp.float32
             ).astype(jnp.bfloat16)
             send.start()
-            fetch.wait()
-        row_count = out_ref.shape[2]
-        for start in range(0, span, TILE):
-            pooled = jnp.dot(
-                cnt_ref[slot, start : start + TILE],
-                local_ref[slot],
-                preferred_element_type=jnp.float32,
-            ).astype(jnp.bfloat16)
-            out_ref[start // row_count : (start + TILE) // row_count, slot] = pooled.reshape(
-                TILE // row_count, row_count, out_ref.shape[3]
-            )
-    send.wait()
+    fetch.wait()
+    row_count = out_ref.shape[2]
+    for start in range(0, span, TILE):
+        pooled = jnp.dot(
+            cnt_ref[start : start + TILE], local_ref[...], preferred_element_type=jnp.float32
+        ).astype(jnp.bfloat16)
+        out_ref[start // row_count : (start + TILE) // row_count, 0] = pooled.reshape(
+            TILE // row_count, row_count, out_ref.shape[3]
+        )
+    if packs:
+        send.wait()
 
 
 def find_feature(slot, map_ref, owner_ref):
@@ -145,51 +151,63 @@
     feats, bag, span = ids_t.shape
     blk_width = top_one.shape[1]
     count = out_cols // blk_width
-    packed = (cols.shape[0] + count * top_two.shape[0], blk_width)
-    pooled = (owners, slot_count, row_count, dim)
+    in_rows = cols.shape[0]
+    packed_shape = (in_rows + count * top_two.shape[0], blk_width)
+    pooled_shape = (owners, slot_count, row_count, dim)
+    pooled_type = jax.ShapeDtypeStruct(pooled_shape, jnp.bfloat16)
     away = pl.BlockSpec(memory_space=pl.ANY)
-
-    def ids_spec(slot):
-        return pl.BlockSpec((1, bag, span), lambda i, m, o, p: (find_feature(slot, m, o), 0, 0))
-
-    return pl.pallas_call(
-        pool_kernel,
-        grid_spec=pltpu.PrefetchScalarGridSpec(
-            num_scalar_prefetch=3,
-            grid=(1,),
-            in_specs=[
-                *[ids_spec(slot) for slot in range(slot_count)],
-                pl.BlockSpec((feats, span), lambda i, m, o, p: (0, 0)),
-                pl.BlockSpec((1, cols.shape[0]), lambda i, m, o, p: (0, 0)),
-                away,
-                away,
-                away,
-            ],
-            out_specs=[pl.BlockSpec(pooled, lambda i, m, o, p: (0, 0, 0, 0)), away],
-            scratch_shapes=[
-                pltpu.VMEM((slot_count, span, vocab), jnp.bfloat16),
-                pltpu.VMEM(tables.shape, jnp.bfloat16),
+    pooled = packed = None
+    for slot in range(slot_count):
+        in_specs = [
+            pl.BlockSpec(
+                (1, bag, span), lambda i, m, o, p, s=slot: (find_feature(s, m, o), 0, 0)
+            ),
+            pl.BlockSpec((feats, span), lambda i, m, o, p: (0, 0)),
+            away,
+        ]
+        args = [table_map, first_slot, part, ids_t, lengths, tables]
+        out_specs = [
+            pl.BlockSpec(
+                (owners, 1, row_count, dim), lambda i, m, o, p, s=slot: (0, s, 0, 0)
+            )
+        ]
+        out_shape = [pooled_type]
+        scratch = [
+            pltpu.VMEM((span, vocab), jnp.bfloat16),
+            pltpu.VMEM((vocab, dim), jnp.bfloat16),
+            pltpu.SemaphoreType.DMA(()),
+        ]
+        aliases = {}
+        if slot == 0:
+            in_specs += [pl.BlockSpec((1, in_rows), lambda i, m, o, p: (0, 0)), away, away]
+            args += [jnp.asarray(cols)[None], top_one, top_two]
+            out_specs.append(away)
+            out_shape.append(jax.ShapeDtypeStruct(packed_shape, jnp.bfloat16))
+            scratch = [
                 pltpu.VMEM(top_one.shape, jnp.bfloat16),
-                pltpu.VMEM(packed, jnp.bfloat16),
-                pltpu.SemaphoreType.DMA(()),
+                pltpu.VMEM(packed_shape, jnp.bfloat16),
                 pltpu.SemaphoreType.DMA((count + 2,)),
-            ],
-        ),
-        out_shape=[
-            jax.ShapeDtypeStruct(pooled, jnp.bfloat16),
-            jax.ShapeDtypeStruct(packed, jnp.bfloat16),
-        ],
-    )(
-        table_map,
-        first_slot,
-        part,
-        *[ids_t] * slot_count,
-        lengths,
-        jnp.asarray(cols)[None],
-        tables,
-        top_one,
-        top_two,
-    )
+            ] + scratch
+        else:
+            in_specs.append(away)
+            aliases = {len(args): 0}
+            args.append(pooled)
+        result = pl.pallas_call(
+            functools.partial(pool_kernel, slot),
+            grid_spec=pltpu.PrefetchScalarGridSpec(
+                num_scalar_prefetch=3,
+                grid=(1,),
+                in_specs=in_specs,
+                out_specs=out_specs,
+                scratch_shapes=scratch,
+            ),
+            out_shape=out_shape,
+            input_output_aliases=aliases,
+        )(*args)
+        pooled = result[0]
+        if slot == 0:
+            packed = result[1]
+    return pooled, packed
 
 
 def code_order(feats, dim, width):
@@ -246,7 +264,7 @@
         hidden.append(jnp.maximum(pre, 0.0).astype(jnp.bfloat16))
     for col in range(0, acc_ref.shape[1], blk_width):
         total = acc_ref[:, col : col + blk_width]
-        row = in_width + col // blk_width * blk_width
+        row = weights_ref.shape[1] - acc_ref.shape[1] + col
         for blk in range(weights_ref.shape[0]):
             total += jnp.dot(
                 hidden[blk],
@@ -328,7 +346,7 @@
         sparse_ids.transpose(0, 2, 1),
         lengths,
         tables,
-        cols,
+        cols[: int(np.flatnonzero(cols >= 0)[-1]) // ROWBLK * ROWBLK + ROWBLK],
         top_one,
         top_two,
         (owners, row_count, out_cols),

time: 104 us -> 105 us (level)
  Pallas kernels: 13.8 us -> 17.1 us
  matrix products: 3.92 us -> 2.42 us
    pallas_call x1 -> x2, Pallas kernels: 8.27 us -> 11.6 us  [pool_slots(): pl.pallas_call(functools.partial(pool_kernel, slot), grid_spec=pltpu.Pref...]
    all_gather x1, waiting for transfers between devices: 1.93 us -> 0.01 us  [local(): weights = lax.all_gather(packed, 'grp', axis=0, tiled=False)]
    all_to_all x1, waiting for transfers between devices: 11.6 us -> 13.1 us  [local(): lax.all_to_all(pooled, 'tbl', split_axis=0, concat_axis=0, tiled=True)]
  transfers between devices with their start and end apart: 3 -> 3, of which waited for: 3 -> 2; matrix products, arithmetic and copies ran while one was open for 7% -> 5% of each run, Pallas kernels for 0% -> 5%
where the time goes in v7:
time: 105 us; the launch traced here: 104 us
  blocking collectives  32.4 us (31%)
  starting transfers between devices  17.1 us (16%)
  Pallas kernels  17.1 us (16%)
  waiting for transfers between devices  17 us (16%)
  between operations  13.8 us (13%)
  matrix products  2.42 us (2%)
  other arithmetic  2.06 us (2%)
  local copies, waits for them, and re-layouts  1.72 us (2%)
    all_gather x1, blocking collectives, local(): gathered = lax.all_gather(embedded[:NPERM], 'grp', axis=1, tiled=True)  25.1 us
    all_to_all x1, starting transfers between devices, local(): lax.all_to_all(pooled, 'tbl', split_axis=0, concat_axis=0, tiled=True)  13.7 us
    all_to_all x1, waiting for transfers between devices, local(): lax.all_to_all(pooled, 'tbl', split_axis=0, concat_axis=0, tiled=True)  13.1 us
    pallas_call x2, Pallas kernels, pool_slots(): pl.pallas_call(functools.partial(pool_kernel, slot), grid_spec=pltpu.Pref...  11.6 us
    all_to_all x1, blocking collectives, local(): lax.all_to_all(part, 'tbl', split_axis=0, concat_axis=0, tiled=True, axis...  7.33 us
    pallas_call x1, Pallas kernels, top_layers(): pl.pallas_call(functools.partial(top_kernel, in_width), grid=(steps,), in...  5.53 us
    all_to_all x1, waiting for transfers between devices, local(): lax.all_to_all(jnp.broadcast_to(codes[None], (xs, *codes.shape)), 'tbl',...  3.92 us
    all_to_all x1, starting transfers between devices, local(): lax.all_to_all(jnp.broadcast_to(codes[None], (xs, *codes.shape)), 'tbl',...  3.34 us
  transfers between devices with their start and end apart: 3, of which 2 were waited for; matrix products, arithmetic and copies ran while one was open for 5% of the time, Pallas kernels for 5%

profile of v7, /device:TPU:1, one launch (start us, length us, event | category | flops | bytes accessed | tf_op | source)
XLA Modules:
  0.0 103.6 jit_solution(10880932140319270249)
XLA Ops:
  6.5 0.0 copy-start
  6.5 0.0 copy-start.3
  6.5 0.0 copy-start.2
  6.5 0.0 copy-start.4
  6.5 0.0 all-gather.3.cloned.1.call-start
  6.6 6.4 %shard_map.127 = (bf16[32,2,32,128]{3,2,1,0:T(8,128)(2,1)}, bf16[1008,256]{1,0:T(8,128)(2,1)}) custom-call(s32[26]{0:T(128)} %map_ref.3, s32[1]{0:T(128)} %bitcast.2.owner_ref, s32[1]{0:T(128)} %bitcast.3.part_ref, s32[26,8,1024]{2,1,0:T(8,128)} %bitcast.84, s32[26,1024]{1,0:T(8,128)} %len_ref.3, bf16[2,2048,128]{2,1,0:T(8,128)(2,1)} %table_ref.3, ...), custom_call_target="tpu_custom_call" | custom-call | tf_op jit(solution)/shard_map/pallas_call | solution.py:195
  13.0 0.0 all-gather.3.cloned.1.call-update
  13.0 5.2 %shard_map.128 = bf16[32,2,32,128]{3,2,1,0:T(8,128)(2,1)} custom-call(s32[26]{0:T(128)} %map_ref.3, s32[1]{0:T(128)} %bitcast.2.owner_ref, s32[1]{0:T(128)} %bitcast.3.part_ref, s32[26,8,1024]{2,1,0:T(8,128)} %bitcast.85, s32[26,1024]{1,0:T(8,128)} %len_ref.3, bf16[2,2048,128]{2,1,0:T(8,128)(2,1)} %table_ref.3, ...), custom_call_target="tpu_custom_call", output_to_operand_aliasing={{}: (6, {})} | custom-call | tf_op jit(solution)/shard_map/pallas_call | solution.py:195
  18.2 13.7 %all-to-all-start = ((bf16[32,2,32,128]{3,2,1,0:T(8,128)(2,1)}), bf16[32,2,32,128]{3,2,1,0:T(8,128)(2,1)S(1)}, u32[]{:S(2)}, u32[]{:S(2)}) async-start(bf16[32,2,32,128]{3,2,1,0:T(8,128)(2,1)} %shard_map.128), calls=%async_computation | async-start | bytes 1048576 | tf_op jit(solution)/shard_map/all_to_all | solution.py:355
  32.0 0.0 copy-done
  32.0 1.0 fusion.3
  33.0 0.0 copy-done.2
  33.0 0.1 fusion.4
  33.2 0.0 copy-done.4
  33.2 13.1 %all-to-all-done = bf16[32,2,32,128]{3,2,1,0:T(8,128)(2,1)S(1)} async-done(((bf16[32,2,32,128]{3,2,1,0:T(8,128)(2,1)}), bf16[32,2,32,128]{3,2,1,0:T(8,128)(2,1)S(1)}, u32[]{:S(2)}, u32[]{:S(2)}) %all-to-all-start) | async-done | bytes 524320 | tf_op jit(solution)/shard_map/all_to_all | solution.py:355
  46.3 0.0 copy-done.3
  46.3 0.3 convolution_convert_fusion
  46.6 0.1 slice.159
  46.7 25.1 %all_gather.9 = bf16[4,512,128]{2,0,1:T(4,128)(2,1)S(1)} all-gather(bf16[4,32,128]{2,0,1:T(4,128)(2,1)S(1)} %slice.182), channel_id=1, replica_groups=mesh['grp'=16,'tbl'=32] {'grp'}, dimensions={1}, use_global_device_ids=true | all-gather | bytes 557056 | tf_op jit(solution)/shard_map/all_gather | solution.py:367
  71.7 0.2 convolution_convert_fusion.1
  72.0 0.3 fusion.10
  72.2 0.3 fusion.7
  72.5 0.2 fusion.13
  73.0 0.1 concatenate.27
  73.3 0.1 fusion.36
  73.4 0.7 broadcast_in_dim.8
  74.0 3.3 %all-to-all-start.1 = ((bf16[4,32,640]{2,1,0:T(8,128)(2,1)}), bf16[4,32,640]{2,1,0:T(8,128)(2,1)S(1)}, u32[]{:S(2)}, u32[]{:S(2)}) async-start(bf16[4,32,640]{2,1,0:T(8,128)(2,1)} %broadcast_in_dim.8), calls=%async_computation.1 | async-start | bytes 327680 | tf_op jit(solution)/shard_map/all_to_all | solution.py:380
  77.4 1.4 %dynamic-slice_convert_fusion = f32[512]{0:T(512)} fusion(bf16[2048]{0:T(1024)(128)(2,1)} %param.24, s32[]{:T(128)S(6)} %select_n.22), kind=kLoop, calls=%fused_computation.85 | loop fusion | flops 512 | bytes 3076 | tf_op jit(solution)/shard_map/convert_element_type | solution.py:389
  78.7 3.9 %all-to-all-done.1.codes_ref = bf16[4,32,640]{2,1,0:T(8,128)(2,1)S(1)} async-done(((bf16[4,32,640]{2,1,0:T(8,128)(2,1)}), bf16[4,32,640]{2,1,0:T(8,128)(2,1)S(1)}, u32[]{:S(2)}, u32[]{:S(2)}) %all-to-all-start.1) | async-done | bytes 163872 | tf_op jit(solution)/shard_map/all_to_all | solution.py:380
  82.7 0.0 copy-start.1
  82.7 0.0 all-gather.3.cloned.1.call-done
  82.7 0.6 copy-done.1
  83.3 5.5 %shard_map.129 = f32[4,2,32]{2,1,0:T(2,128)} custom-call(bf16[4,32,640]{2,1,0:T(8,128)(2,1)} %copy-done.1, bf16[16,1008,256]{2,1,0:T(8,128)(2,1)} %bitcast.83, f32[1,512]{1,0:T(1,128)} %bitcast.89), custom_call_target="tpu_custom_call" | custom-call | tf_op jit(solution)/shard_map/pallas_call | solution.py:295
  88.8 7.3 %all_to_all.15 = f32[4,2,32]{2,1,0:T(2,128)S(1)} all-to-all(f32[4,2,32]{2,1,0:T(2,128)} %shard_map.129), channel_id=1, replica_groups={{0,8,16,24},{1,9,17,25},{2,10,18,26},{3,11,19,27},{4,12,20,28},{5,13,21..., dimensions={0} | all-to-all | bytes 2048 | tf_op jit(solution)/shard_map/all_to_all | solution.py:390
  96.2 0.6 add_divide_fusion
  (39 shorter events, 0.2 us)
Async XLA Ops:
  6.5 25.4 %copy-start = (bf16[512,256]{1,0:T(8,128)(2,1)S(1)}, bf16[512,256]{1,0:T(8,128)(2,1)}, u32[]{:S(2)}) copy-start(bf16[512,256]{1,0:T(8,128)(2,1)} %param.20) | copy-start | bytes 786436
  6.5 39.7 %copy-start.3 = (s32[26]{0:T(128)S(1)}, s32[26]{0:T(128)}, u32[]{:S(2)}) copy-start(s32[26]{0:T(128)} %map_ref.3) | copy-start | bytes 316
  6.5 26.5 %copy-start.2 = (bf16[256,128]{1,0:T(8,128)(2,1)S(1)}, bf16[256,128]{1,0:T(8,128)(2,1)}, u32[]{:S(2)}) copy-start(bf16[256,128]{1,0:T(8,128)(2,1)} %param.21) | copy-start | bytes 196612
  6.5 26.6 %copy-start.4 = (s32[32]{0:T(128)S(1)}, s32[32]{0:T(128)}, u32[]{:S(2)}) copy-start(s32[32]{0:T(128)} %param.17) | copy-start | bytes 388
  6.5 76.1 %all-gather.3.cloned.1.call-start = ((), (), s32[]{:S(2)}) async-start(), calls=%async_computation.3 | async-start | bytes 8773632 | tf_op jit(solution)/shard_map/all_gather | solution.py:354
  18.2 28.0 %all-to-all-start = ((bf16[32,2,32,128]{3,2,1,0:T(8,128)(2,1)}), bf16[32,2,32,128]{3,2,1,0:T(8,128)(2,1)S(1)}, u32[]{:S(2)}, u32[]{:S(2)}) async-start(bf16[32,2,32,128]{3,2,1,0:T(8,128)(2,1)} %shard_map.128), calls=%async_computation | async-start | bytes 1048576 | tf_op jit(solution)/shard_map/all_to_all | solution.py:355
  74.0 8.6 %all-to-all-start.1 = ((bf16[4,32,640]{2,1,0:T(8,128)(2,1)}), bf16[4,32,640]{2,1,0:T(8,128)(2,1)S(1)}, u32[]{:S(2)}, u32[]{:S(2)}) async-start(bf16[4,32,640]{2,1,0:T(8,128)(2,1)} %broadcast_in_dim.8), calls=%async_computation.1 | async-start | bytes 327680 | tf_op jit(solution)/shard_map/all_to_all | solution.py:380
  82.7 0.7 copy-start.1
Sparse Core Ops, SparseCore 0:
  13.1 66.3 all-gather.2

commit v8 on v5

--- a/solution.py
+++ b/solution.py
@@ -1,5 +1,3 @@
-import functools
-
 import jax
 import jax.numpy as jnp
 import numpy as np
@@ -141,47 +139,52 @@
     )(table_map, first_slot, *[ids_t] * slot_count, lengths, tables)
 
 
-def pack_kernel(part_ref, cols_ref, one_ref, two_ref, out_ref, sems):
-    blk_width = out_ref.shape[1]
-    in_width = cols_ref.shape[1]
-    count = (out_ref.shape[0] - in_width) // two_ref.shape[0]
-    copies = []
+def pack_kernel(part_ref, one_ref, two_ref, out_ref, one_local_ref, two_local_ref, sems):
+    in_rows, blk_width = one_ref.shape
+    count, depth = two_local_ref.shape[:2]
+    first = pltpu.make_async_copy(one_ref, one_local_ref, sems.at[0])
+    loads = []
+    sends = [pltpu.make_async_copy(one_local_ref, out_ref.at[pl.ds(0, in_rows)], sems.at[1])]
     for blk in range(count):
         start = pl.multiple_of((part_ref[0] * count + blk) * blk_width, blk_width)
-        copies.append(
+        loads.append(
             pltpu.make_async_copy(
-                two_ref.at[:, pl.ds(start, blk_width)],
-                out_ref.at[pl.ds(in_width + blk * two_ref.shape[0], two_ref.shape[0])],
-                sems.at[blk],
+                two_ref.at[:, pl.ds(start, blk_width)], two_local_ref.at[blk], sems.at[2 + 2 * blk]
             )
         )
-        copies[-1].start()
-    row = lax.broadcasted_iota(jnp.int32, (one_ref.shape[0], in_width), 0)
-    pick = jnp.where(row == cols_ref[...], 1.0, 0.0).astype(jnp.bfloat16)
-    out_ref[:in_width] = lax.dot_general(
-        pick, one_ref[...], (((0,), (0,)), ((), ())), preferred_element_type=jnp.float32
-    ).astype(jnp.bfloat16)
-    for copy in copies:
-        copy.wait()
-
-
-def pack_weights(part, cols, top_one, top_two, out_cols):
+        sends.append(
+            pltpu.make_async_copy(
+                two_local_ref.at[blk],
+                out_ref.at[pl.ds(in_rows + blk * depth, depth)],
+                sems.at[3 + 2 * blk],
+            )
+        )
+    loads.insert(0, first)
+    for load in loads:
+        load.start()
+    for load, send in zip(loads, sends):
+        load.wait()
+        send.start()
+    for send in sends:
+        send.wait()
+
+
+def pack_weights(part, top_one, top_two, out_cols):
     blk_width = top_one.shape[1]
     count = out_cols // blk_width
-    whole = pl.BlockSpec(memory_space=pltpu.VMEM)
-    rows = cols.shape[0] + count * top_two.shape[0]
+    depth = top_two.shape[0]
+    away = pl.BlockSpec(memory_space=pl.ANY)
     return pl.pallas_call(
         pack_kernel,
-        in_specs=[
-            pl.BlockSpec(memory_space=pltpu.SMEM),
-            whole,
-            whole,
-            pl.BlockSpec(memory_space=pl.ANY),
+        in_specs=[pl.BlockSpec(memory_space=pltpu.SMEM), away, away],
+        out_specs=away,
+        scratch_shapes=[
+            pltpu.VMEM(top_one.shape, jnp.bfloat16),
+            pltpu.VMEM((count, depth, blk_width), jnp.bfloat16),
+            pltpu.SemaphoreType.DMA((2 + 2 * count,)),
         ],
-        out_specs=whole,
-        scratch_shapes=[pltpu.SemaphoreType.DMA((count,))],
-        out_shape=jax.ShapeDtypeStruct((rows, blk_width), jnp.bfloat16),
-    )(part.reshape(1), jnp.asarray(cols)[None], top_one, top_two)
+        out_shape=jax.ShapeDtypeStruct((top_one.shape[0] + count * depth, blk_width), jnp.bfloat16),
+    )(part.reshape(1), top_one, top_two)
 
 
 def code_order(feats, dim, width):
@@ -217,28 +220,33 @@
     return jnp.pad(out, ((0, 0), (0, moved_width - out.shape[1]))).astype(jnp.bfloat16)
 
 
-def top_kernel(in_width, codes_ref, weights_ref, out_w_ref, out_ref, acc_ref, codes_all_ref):
+def top_kernel(codes_ref, cols_ref, weights_ref, out_w_ref, out_ref, acc_ref, codes_all_ref):
     step = pl.program_id(0)
     blk_width = weights_ref.shape[2]
+    in_width = cols_ref.shape[1]
+    in_rows = codes_all_ref.shape[1]
     fixed_width = 2 * in_width - codes_ref.shape[2]
 
     @pl.when(step == 0)
     def _():
         codes = jnp.concatenate([codes_ref[x] for x in range(codes_ref.shape[0])], axis=0)
-        rows = codes.shape[0]
-        codes_all_ref[:rows] = codes[:, :in_width]
-        codes_all_ref[rows:, :fixed_width] = codes[:, :fixed_width]
-        codes_all_ref[rows:, fixed_width:] = codes[:, in_width:]
+        moved = jnp.concatenate([codes[:, :fixed_width], codes[:, in_width:]], axis=1)
+        codes = jnp.concatenate([codes[:, :in_width], moved], axis=0)
+        row = lax.broadcasted_iota(jnp.int32, (in_rows, in_width), 0)
+        pick = jnp.where(row == cols_ref[...], 1.0, 0.0).astype(jnp.bfloat16)
+        codes_all_ref[...] = lax.dot_general(
+            codes, pick, (((1,), (1,)), ((), ())), preferred_element_type=jnp.float32
+        ).astype(jnp.bfloat16)
         acc_ref[...] = jnp.zeros_like(acc_ref)
 
     codes = codes_all_ref[...]
     hidden = []
     for blk in range(weights_ref.shape[0]):
-        pre = jnp.dot(codes, weights_ref[blk, :in_width], preferred_element_type=jnp.float32)
+        pre = jnp.dot(codes, weights_ref[blk, :in_rows], preferred_element_type=jnp.float32)
         hidden.append(jnp.maximum(pre, 0.0).astype(jnp.bfloat16))
     for col in range(0, acc_ref.shape[1], blk_width):
         total = acc_ref[:, col : col + blk_width]
-        row = in_width + col // blk_width * blk_width
+        row = in_rows + col
         for blk in range(weights_ref.shape[0]):
             total += jnp.dot(
                 hidden[blk],
@@ -261,15 +269,16 @@
                 out_ref[x, variant : variant + 1] = sums[:, start : start + row_count]
 
 
-def top_layers(codes, weights, out_w, in_width):
+def top_layers(codes, cols, weights, out_w):
     xs, row_count, _ = codes.shape
     groups, depth, blk_width = weights.shape
     steps = 2
     rows = 2 * xs * row_count
     return pl.pallas_call(
-        functools.partial(top_kernel, in_width),
+        top_kernel,
         grid=(steps,),
         in_specs=[
+            pl.BlockSpec(memory_space=pltpu.VMEM),
             pl.BlockSpec(memory_space=pltpu.VMEM),
             pl.BlockSpec((groups // steps, depth, blk_width), lambda i: (i, 0, 0)),
             pl.BlockSpec(memory_space=pltpu.VMEM),
@@ -277,10 +286,10 @@
         out_specs=pl.BlockSpec((xs, 2, row_count), lambda i: (0, 0, 0)),
         scratch_shapes=[
             pltpu.VMEM((rows, out_w.shape[1]), jnp.float32),
-            pltpu.VMEM((rows, in_width), jnp.bfloat16),
+            pltpu.VMEM((rows, depth - out_w.shape[1]), jnp.bfloat16),
         ],
         out_shape=jax.ShapeDtypeStruct((xs, 2, row_count), jnp.float32),
-    )(codes, weights, out_w)
+    )(codes, jnp.asarray(cols)[None], weights, out_w)
 
 
 def local(
@@ -312,7 +321,7 @@
     cols, fixed_width = code_order(feats, dim, top_one.shape[0])
     in_width = cols.shape[0]
     moved_width = in_width - fixed_width
-    packed = pack_weights(x_idx.astype(jnp.int32), cols, top_one, top_two, out_cols)
+    packed = pack_weights(x_idx.astype(jnp.int32), top_one, top_two, out_cols)
     weights = lax.all_gather(packed, "grp", axis=0, tiled=False)
 
     first_slot = (owner_idx * slot_count).astype(jnp.int32).reshape(1)
@@ -353,7 +362,8 @@
         axis_index_groups=along_x,
     )
     out_w = lax.dynamic_slice(top_out, (x_idx * out_cols,), (out_cols,)).reshape(1, out_cols)
-    part = top_layers(codes_all, weights, out_w.astype(jnp.float32), in_width)
+    codes_all = pltpu.with_memory_space_constraint(codes_all, pltpu.VMEM)
+    part = top_layers(codes_all, cols, weights, out_w.astype(jnp.float32))
     pieces = lax.all_to_all(
         part, "tbl", split_axis=0, concat_axis=0, tiled=True, axis_index_groups=along_x
     )

time: 105 us -> 103 us (0.981)
  no operation moved by 1% of the time
where the time goes in v8:
time: 103 us; the launch traced here: 102 us
  blocking collectives  32.3 us (31%)
  starting transfers between devices  17.1 us (17%)
  waiting for transfers between devices  15.6 us (15%)
  Pallas kernels  15.2 us (15%)
  between operations  13.8 us (13%)
  matrix products  3.92 us (4%)
  other arithmetic  2.7 us (3%)
  local copies, waits for them, and re-layouts  1.1 us (1%)
    all_gather x1, blocking collectives, local(): gathered = lax.all_gather(embedded[:NPERM], 'grp', axis=1, tiled=True)  25 us
    all_to_all x1, starting transfers between devices, local(): lax.all_to_all(pooled, 'tbl', split_axis=0, concat_axis=0, tiled=True)  13.7 us
    all_to_all x1, waiting for transfers between devices, local(): lax.all_to_all(pooled, 'tbl', split_axis=0, concat_axis=0, tiled=True)  11.6 us
    pallas_call x1, Pallas kernels, pool_slots(): pl.pallas_call(pool_kernel, grid_spec=pltpu.PrefetchScalarGridSpec(num_sc...  7.51 us
    all_to_all x1, blocking collectives, local(): lax.all_to_all(part, 'tbl', split_axis=0, concat_axis=0, tiled=True, axis...  7.28 us
    pallas_call x1, Pallas kernels, top_layers(): pl.pallas_call(top_kernel, grid=(steps,), in_specs=[pl.BlockSpec(memory_s...  5.83 us
    all_to_all x1, waiting for transfers between devices, local(): lax.all_to_all(jnp.broadcast_to(codes[None], (xs, *codes.shape)), 'tbl',...  3.93 us
    all_to_all x1, starting transfers between devices, local(): lax.all_to_all(jnp.broadcast_to(codes[None], (xs, *codes.shape)), 'tbl',...  3.34 us
  transfers between devices with their start and end apart: 3, of which 2 were waited for; matrix products, arithmetic and copies ran while one was open for 7% of the time, Pallas kernels for 7%

profile of v8, /device:TPU:1, one launch (start us, length us, event | category | flops | bytes accessed | tf_op | source)
XLA Modules:
  0.0 101.7 jit_solution(4015663639981220967)
XLA Ops:
  6.5 0.0 copy-start
  6.5 0.0 all-gather.3.cloned.1.call-start
  6.5 1.9 %shard_map.128 = bf16[992,256]{1,0:T(8,128)(2,1)} custom-call(s32[1]{0:T(128)} %bitcast.37.part_ref, bf16[480,256]{1,0:T(8,128)(2,1)} %one_ref.1, bf16[256,2048]{1,0:T(8,128)(2,1)} %two_ref.1), custom_call_target="tpu_custom_call" | custom-call | tf_op jit(solution)/shard_map/pallas_call | solution.py:177
  8.4 0.0 all-gather.3.cloned.1.call-update
  8.5 7.5 %shard_map.127 = bf16[32,2,32,128]{3,2,1,0:T(8,128)(2,1)} custom-call(s32[26]{0:T(128)} %map_ref.1, s32[1]{0:T(128)} %bitcast.2.owner_ref, s32[26,8,1024]{2,1,0:T(8,128)} %bitcast.84, s32[26,8,1024]{2,1,0:T(8,128)} %bitcast.85, s32[26,1024]{1,0:T(8,128)} %refs_2_.1, bf16[2,2048,128]{2,1,0:T(8,128)(2,1)} %refs_3_.1), custom_call_target="tpu_custom_call" | custom-call | tf_op jit(solution)/shard_map/pallas_call | solution.py:119
  16.0 13.7 %all-to-all-start = ((bf16[32,2,32,128]{3,2,1,0:T(8,128)(2,1)}), bf16[32,2,32,128]{3,2,1,0:T(8,128)(2,1)S(1)}, u32[]{:S(2)}, u32[]{:S(2)}) async-start(bf16[32,2,32,128]{3,2,1,0:T(8,128)(2,1)} %shard_map.127), calls=%async_computation | async-start | bytes 1048576 | tf_op jit(solution)/shard_map/all_to_all | solution.py:331
  29.7 0.0 copy-done
  29.7 1.0 %fusion.3 = bf16[32,256]{1,0:T(8,128)(2,1)S(1)} fusion(bf16[512,256]{1,0:T(8,128)(2,1)S(1)} %copy-done, bf16[32,13]{0,1:T(8,128)(2,1)} %param.13, bf16[13,512]{1,0:T(8,128)(2,1)} %param.19), kind=kOutput, calls=%fused_computation.6 | convolution fusion | flops 8863744 | bytes 292672 | tf_op jit(solution)/shard_map/dot_general | solution.py:17
  30.7 1.0 fusion.4
  31.7 0.7 fusion.41
  32.4 11.6 %all-to-all-done = bf16[32,2,32,128]{3,2,1,0:T(8,128)(2,1)S(1)} async-done(((bf16[32,2,32,128]{3,2,1,0:T(8,128)(2,1)}), bf16[32,2,32,128]{3,2,1,0:T(8,128)(2,1)S(1)}, u32[]{:S(2)}, u32[]{:S(2)}) %all-to-all-start) | async-done | bytes 524320 | tf_op jit(solution)/shard_map/all_to_all | solution.py:331
  44.0 0.9 convolution_convert_fusion
  45.0 0.1 slice.159
  45.1 25.0 %all_gather.9 = bf16[4,512,128]{2,0,1:T(4,128)(2,1)S(1)} all-gather(bf16[4,32,128]{2,0,1:T(4,128)(2,1)S(1)} %slice.182), channel_id=1, replica_groups=mesh['grp'=16,'tbl'=32] {'grp'}, dimensions={1}, use_global_device_ids=true | all-gather | bytes 557056 | tf_op jit(solution)/shard_map/all_gather | solution.py:343
  70.1 0.2 convolution_convert_fusion.1
  70.4 0.3 fusion.10
  70.6 0.3 fusion.7
  70.9 0.2 fusion.13
  71.4 0.1 concatenate.27
  71.7 0.1 fusion.36
  71.8 0.7 broadcast_in_dim.7
  72.5 3.3 %all-to-all-start.1 = ((bf16[4,32,640]{2,1,0:T(8,128)(2,1)}), bf16[4,32,640]{2,1,0:T(8,128)(2,1)S(1)}, u32[]{:S(2)}, u32[]{:S(2)}) async-start(bf16[4,32,640]{2,1,0:T(8,128)(2,1)} %broadcast_in_dim.7), calls=%async_computation.1 | async-start | bytes 327680 | tf_op jit(solution)/shard_map/all_to_all | solution.py:356
  75.8 1.3 %dynamic-slice_convert_fusion = f32[512]{0:T(512)} fusion(bf16[2048]{0:T(1024)(128)(2,1)} %param.24, s32[]{:T(128)S(6)} %select_n.22), kind=kLoop, calls=%fused_computation.85 | loop fusion | flops 512 | bytes 3076 | tf_op jit(solution)/shard_map/convert_element_type | solution.py:366
  77.2 3.9 %all-to-all-done.1.codes_ref = bf16[4,32,640]{2,1,0:T(8,128)(2,1)S(1)} async-done(((bf16[4,32,640]{2,1,0:T(8,128)(2,1)}), bf16[4,32,640]{2,1,0:T(8,128)(2,1)S(1)}, u32[]{:S(2)}, u32[]{:S(2)}) %all-to-all-start.1) | async-done | bytes 163872 | tf_op jit(solution)/shard_map/all_to_all | solution.py:356
  81.1 0.0 all-gather.3.cloned.1.call-done
  81.1 5.8 %shard_map.129 = f32[4,2,32]{2,1,0:T(2,128)} custom-call(bf16[4,32,640]{2,1,0:T(8,128)(2,1)S(1)} %all-to-all-done.1.codes_ref, s32[1,512]{1,0:T(1,128)} %constant.77.cols_ref, bf16[16,992,256]{2,1,0:T(8,128)(2,1)} %bitcast.83, f32[1,512]{1,0:T(1,128)} %bitcast.89), custom_call_target="tpu_custom_call" | custom-call | tf_op jit(solution)/shard_map/pallas_call | solution.py:277
  86.9 7.3 %all_to_all.15 = f32[4,2,32]{2,1,0:T(2,128)S(1)} all-to-all(f32[4,2,32]{2,1,0:T(2,128)} %shard_map.129), channel_id=1, replica_groups={{0,8,16,24},{1,9,17,25},{2,10,18,26},{3,11,19,27},{4,12,20,28},{5,13,21..., dimensions={0} | all-to-all | bytes 2048 | tf_op jit(solution)/shard_map/all_to_all | solution.py:367
  94.2 0.6 add_divide_fusion
  (38 shorter events, 0.2 us)
Async XLA Ops:
  6.5 23.2 %copy-start = (bf16[512,256]{1,0:T(8,128)(2,1)S(1)}, bf16[512,256]{1,0:T(8,128)(2,1)}, u32[]{:S(2)}) copy-start(bf16[512,256]{1,0:T(8,128)(2,1)} %param.20) | copy-start | bytes 786436
  6.5 74.6 %all-gather.3.cloned.1.call-start = ((), (), s32[]{:S(2)}) async-start(), calls=%async_computation.3 | async-start | bytes 8634368 | tf_op jit(solution)/shard_map/all_gather | solution.py:325
  16.0 28.1 %all-to-all-start = ((bf16[32,2,32,128]{3,2,1,0:T(8,128)(2,1)}), bf16[32,2,32,128]{3,2,1,0:T(8,128)(2,1)S(1)}, u32[]{:S(2)}, u32[]{:S(2)}) async-start(bf16[32,2,32,128]{3,2,1,0:T(8,128)(2,1)} %shard_map.127), calls=%async_computation | async-start | bytes 1048576 | tf_op jit(solution)/shard_map/all_to_all | solution.py:331
  72.5 8.6 %all-to-all-start.1 = ((bf16[4,32,640]{2,1,0:T(8,128)(2,1)}), bf16[4,32,640]{2,1,0:T(8,128)(2,1)S(1)}, u32[]{:S(2)}, u32[]{:S(2)}) async-start(bf16[4,32,640]{2,1,0:T(8,128)(2,1)} %broadcast_in_dim.7), calls=%async_computation.1 | async-start | bytes 327680 | tf_op jit(solution)/shard_map/all_to_all | solution.py:356
Sparse Core Ops, SparseCore 0:
  9.5 65.7 all-gather.2

commit v9 on v8

--- a/solution.py
+++ b/solution.py
@@ -32,9 +32,9 @@
 
 
 def pool_kernel(map_ref, owner_ref, *refs):
-    slot_count = len(refs) - 6
+    slot_count = len(refs) - 8
     ids_refs = refs[:slot_count]
-    len_ref, table_ref, out_ref, cnt_ref, local_ref, sem = refs[slot_count:]
+    len_ref, table_ref, out_ref, cnt_ref, local_ref, rows_ref, sem, sems = refs[slot_count:]
     vocab = table_ref.shape[1]
     hi_count = vocab // LO
     height = hi_count * ROWBLK
@@ -56,6 +56,7 @@
         row = jnp.broadcast_to(row, (16, 128)).astype(jnp.bfloat16)
         return jnp.where(row[None] == wanted, one, zero).reshape(-1, 128)
 
+    sends = []
     for slot in range(slot_count):
         feat = find_feature(slot, map_ref, owner_ref)
         lens = jnp.sum(jnp.where(feat_pos == feat, len_ref[...], 0), axis=0, keepdims=True)
@@ -96,9 +97,12 @@
                 local_ref[slot],
                 preferred_element_type=jnp.float32,
             ).astype(jnp.bfloat16)
-            out_ref[start // row_count : (start + TILE) // row_count, slot] = pooled.reshape(
-                TILE // row_count, row_count, out_ref.shape[3]
-            )
+            first, last = start // row_count, (start + TILE) // row_count
+            rows_ref[slot, first:last] = pooled.reshape(last - first, row_count, out_ref.shape[3])
+        sends.append(pltpu.make_async_copy(rows_ref.at[slot], out_ref.at[:, slot], sems.at[slot]))
+        sends[-1].start()
+    for send in sends:
+        send.wait()
 
 
 def find_feature(slot, map_ref, owner_ref):
@@ -126,13 +130,13 @@
                 pl.BlockSpec((feats, span), lambda i, m, o: (0, 0)),
                 pl.BlockSpec(memory_space=pl.ANY),
             ],
-            out_specs=pl.BlockSpec(
-                (owners, slot_count, row_count, dim), lambda i, m, o: (0, 0, 0, 0)
-            ),
+            out_specs=pl.BlockSpec(memory_space=pl.ANY),
             scratch_shapes=[
                 pltpu.VMEM((slot_count, span, vocab), jnp.bfloat16),
                 pltpu.VMEM(tables.shape, jnp.bfloat16),
+                pltpu.VMEM((slot_count, owners, row_count, dim), jnp.bfloat16),
                 pltpu.SemaphoreType.DMA(()),
+                pltpu.SemaphoreType.DMA((slot_count,)),
             ],
         ),
         out_shape=jax.ShapeDtypeStruct((owners, slot_count, row_count, dim), jnp.bfloat16),
@@ -187,6 +191,30 @@
     )(part.reshape(1), top_one, top_two)
 
 
+def select_kernel(map_ref, arrived_ref, moved_ref, kept_ref):
+    moved = moved_ref.shape[0]
+    for feat in range(map_ref.shape[0]):
+        value = arrived_ref[map_ref[feat]]
+        if feat < moved:
+            moved_ref[feat] = value
+        else:
+            kept_ref[feat - moved] = value
+
+
+def select_slots(table_map, arrived):
+    feats = table_map.shape[0]
+    whole = pl.BlockSpec(memory_space=pltpu.VMEM)
+    return pl.pallas_call(
+        select_kernel,
+        in_specs=[pl.BlockSpec(memory_space=pltpu.SMEM), whole],
+        out_specs=[whole, whole],
+        out_shape=[
+            jax.ShapeDtypeStruct((NPERM, *arrived.shape[1:]), arrived.dtype),
+            jax.ShapeDtypeStruct((feats - NPERM, *arrived.shape[1:]), arrived.dtype),
+        ],
+    )(table_map, pltpu.with_memory_space_constraint(arrived, pltpu.VMEM))
+
+
 def code_order(feats, dim, width):
     order = [0, *range(NPERM + 1, feats + 1), *range(1, NPERM + 1)]
     fixed = feats + 1 - NPERM
@@ -330,20 +358,15 @@
     )
     arrived = lax.all_to_all(pooled, "tbl", split_axis=0, concat_axis=0, tiled=True)
     arrived = arrived.reshape(owners * slot_count, row_count, dim)
-    pick_slot = (
-        table_map[:, None] == jnp.arange(owners * slot_count, dtype=jnp.int32)[None, :]
-    ).astype(jnp.bfloat16)
-    embedded = jnp.einsum(
-        "fs,srd->frd", pick_slot, arrived, preferred_element_type=jnp.float32
-    ).astype(jnp.bfloat16)
+    moved, kept = select_slots(table_map, arrived)
 
     bottom_out = dense_layer(
         dense_layer(dense_layer(dense_feats, bottom_one), bottom_two), bottom_three
     )
-    gathered = lax.all_gather(embedded[:NPERM], "grp", axis=1, tiled=True)
-    fixed = jnp.concatenate([bottom_out[None], embedded[NPERM:]], axis=0)
+    gathered = lax.all_gather(moved, "grp", axis=1, tiled=True)
+    fixed = jnp.concatenate([bottom_out[None], kept], axis=0)
     code_fixed = fixed_codes(fixed, bottom_out, fixed_width)
-    code_base = moved_codes(embedded[:NPERM], fixed, moved_width)
+    code_base = moved_codes(moved, fixed, moved_width)
     source = row_perm // (owners * row_count) * row_count + row_perm % row_count
     pick_row = (source[:, None] == jnp.arange(gathered.shape[1], dtype=jnp.int32)[None, :]).astype(
         jnp.bfloat16

time: 103 us -> 107 us (1.039)
  other arithmetic: 2.7 us -> 4.66 us
  Pallas kernels: 15.2 us -> 16.6 us
    concatenate x0 -> x2, other arithmetic: none -> 1.97 us  [the longest x1 1.02 us: moved_codes(): every = jnp.concatenate([fixed, moved], axis=0)]
    pallas_call x0 -> x1, Pallas kernels: none -> 1.42 us  [select_slots(): pl.pallas_call(select_kernel, in_specs=[pl.BlockSpec(memory_space=pltpu.S...]
  transfers between devices with their start and end apart: 3 -> 3, of which waited for: 2 -> 2; matrix products, arithmetic and copies ran while one was open for 7% -> 8% of each run, Pallas kernels for 7% -> 8%
where the time goes in v9:
time: 107 us; the launch traced here: 105 us
  blocking collectives  32.6 us (30%)
  starting transfers between devices  17.1 us (16%)
  Pallas kernels  16.6 us (16%)
  waiting for transfers between devices  15.6 us (15%)
  between operations  13.7 us (13%)
  other arithmetic  4.66 us (4%)
  matrix products  3.73 us (3%)
    all_gather x1, blocking collectives, local(): gathered = lax.all_gather(moved, 'grp', axis=1, tiled=True)  25.3 us
    all_to_all x1, starting transfers between devices, local(): lax.all_to_all(pooled, 'tbl', split_axis=0, concat_axis=0, tiled=True)  13.7 us
    all_to_all x1, waiting for transfers between devices, local(): lax.all_to_all(pooled, 'tbl', split_axis=0, concat_axis=0, tiled=True)  11.6 us
    pallas_call x1, Pallas kernels, pool_slots(): pl.pallas_call(pool_kernel, grid_spec=pltpu.PrefetchScalarGridSpec(num_sc...  7.44 us
    all_to_all x1, blocking collectives, local(): lax.all_to_all(part, 'tbl', split_axis=0, concat_axis=0, tiled=True, axis...  7.35 us
    pallas_call x1, Pallas kernels, top_layers(): pl.pallas_call(top_kernel, grid=(steps,), in_specs=[pl.BlockSpec(memory_s...  5.84 us
    all_to_all x1, waiting for transfers between devices, local(): lax.all_to_all(jnp.broadcast_to(codes[None], (xs, *codes.shape)), 'tbl',...  3.95 us
    all_to_all x1, starting transfers between devices, local(): lax.all_to_all(jnp.broadcast_to(codes[None], (xs, *codes.shape)), 'tbl',...  3.34 us
  transfers between devices with their start and end apart: 3, of which 2 were waited for; matrix products, arithmetic and copies ran while one was open for 8% of the time, Pallas kernels for 8%

profile of v9, /device:TPU:1, one launch (start us, length us, event | category | flops | bytes accessed | tf_op | source)
XLA Modules:
  0.0 105.0 jit_solution(1662933934272131303)
XLA Ops:
  6.5 0.0 copy-start
  6.5 0.0 all-gather.3.cloned.1.call-start
  6.5 1.9 %shard_map.129 = bf16[992,256]{1,0:T(8,128)(2,1)} custom-call(s32[1]{0:T(128)} %bitcast.36.part_ref, bf16[480,256]{1,0:T(8,128)(2,1)} %one_ref.1, bf16[256,2048]{1,0:T(8,128)(2,1)} %two_ref.1), custom_call_target="tpu_custom_call" | custom-call | tf_op jit(solution)/shard_map/pallas_call | solution.py:181
  8.4 0.0 all-gather.3.cloned.1.call-update
  8.5 7.4 %shard_map.127 = bf16[32,2,32,128]{3,2,1,0:T(8,128)(2,1)} custom-call(s32[26]{0:T(128)} %map_ref.3, s32[1]{0:T(128)} %bitcast.1.owner_ref, s32[26,8,1024]{2,1,0:T(8,128)} %bitcast.80, s32[26,8,1024]{2,1,0:T(8,128)} %bitcast.81, s32[26,1024]{1,0:T(8,128)} %refs_2_.1, bf16[2,2048,128]{2,1,0:T(8,128)(2,1)} %refs_3_.1), custom_call_target="tpu_custom_call" | custom-call | tf_op jit(solution)/shard_map/pallas_call | solution.py:123
  15.9 13.7 %all-to-all-start = ((bf16[32,2,32,128]{3,2,1,0:T(8,128)(2,1)}), bf16[32,2,32,128]{3,2,1,0:T(8,128)(2,1)S(1)}, u32[]{:S(2)}, u32[]{:S(2)}) async-start(bf16[32,2,32,128]{3,2,1,0:T(8,128)(2,1)} %shard_map.127), calls=%async_computation | async-start | bytes 1048576 | tf_op jit(solution)/shard_map/all_to_all | solution.py:359
  29.6 0.7 fusion.35
  30.3 0.0 copy-done
  30.3 1.0 fusion.4
  31.3 1.0 fusion.5
  32.3 11.6 %all-to-all-done = bf16[32,2,32,128]{3,2,1,0:T(8,128)(2,1)S(1)} async-done(((bf16[32,2,32,128]{3,2,1,0:T(8,128)(2,1)}), bf16[32,2,32,128]{3,2,1,0:T(8,128)(2,1)S(1)}, u32[]{:S(2)}, u32[]{:S(2)}) %all-to-all-start) | async-done | bytes 524320 | tf_op jit(solution)/shard_map/all_to_all | solution.py:359
  43.9 1.4 %shard_map.128 = (bf16[4,32,128]{2,1,0:T(8,128)(2,1)}, bf16[22,32,128]{2,1,0:T(8,128)(2,1)}) custom-call(s32[26]{0:T(128)} %map_ref.3, bf16[64,32,128]{2,1,0:T(8,128)(2,1)S(1)} %bitcast.78), custom_call_target="tpu_custom_call" | custom-call | tf_op jit(solution)/shard_map/pallas_call | solution.py:207
  45.4 25.3 %all_gather.9 = bf16[4,512,128]{2,1,0:T(8,128)(2,1)S(1)} all-gather(bf16[4,32,128]{2,1,0:T(8,128)(2,1)} %get-tuple-element.8), channel_id=1, replica_groups=mesh['grp'=16,'tbl'=32] {'grp'}, dimensions={1}, use_global_device_ids=true | all-gather | bytes 557056 | tf_op jit(solution)/shard_map/all_gather | solution.py:366
  70.7 0.2 fusion.3
  70.9 1.0 pad_maximum_fusion
  71.9 0.2 fusion.6
  72.2 1.0 fusion.8
  73.2 0.9 pad_maximum_fusion.3
  74.1 0.3 fusion.10
  74.7 0.1 concatenate.27
  74.9 0.1 fusion.31
  75.0 0.7 broadcast_in_dim.7
  75.7 3.3 %all-to-all-start.1 = ((bf16[4,32,640]{2,1,0:T(8,128)(2,1)}), bf16[4,32,640]{2,1,0:T(8,128)(2,1)S(1)}, u32[]{:S(2)}, u32[]{:S(2)}) async-start(bf16[4,32,640]{2,1,0:T(8,128)(2,1)} %broadcast_in_dim.7), calls=%async_computation.1 | async-start | bytes 327680 | tf_op jit(solution)/shard_map/all_to_all | solution.py:379
  79.1 1.3 %dynamic-slice_convert_fusion = f32[512]{0:T(512)} fusion(bf16[2048]{0:T(1024)(128)(2,1)} %param.24, s32[]{:T(128)S(6)} %select_n.22), kind=kLoop, calls=%fused_computation.80 | loop fusion | flops 512 | bytes 3076 | tf_op jit(solution)/shard_map/convert_element_type | solution.py:389
  80.4 3.9 %all-to-all-done.1.codes_ref = bf16[4,32,640]{2,1,0:T(8,128)(2,1)S(1)} async-done(((bf16[4,32,640]{2,1,0:T(8,128)(2,1)}), bf16[4,32,640]{2,1,0:T(8,128)(2,1)S(1)}, u32[]{:S(2)}, u32[]{:S(2)}) %all-to-all-start.1) | async-done | bytes 163872 | tf_op jit(solution)/shard_map/all_to_all | solution.py:379
  84.3 0.0 all-gather.3.cloned.1.call-done
  84.3 5.8 %shard_map.130 = f32[4,2,32]{2,1,0:T(2,128)} custom-call(bf16[4,32,640]{2,1,0:T(8,128)(2,1)S(1)} %all-to-all-done.1.codes_ref, s32[1,512]{1,0:T(1,128)} %constant.77.cols_ref, bf16[16,992,256]{2,1,0:T(8,128)(2,1)} %bitcast.79, f32[1,512]{1,0:T(1,128)} %bitcast.84), custom_call_target="tpu_custom_call" | custom-call | tf_op jit(solution)/shard_map/pallas_call | solution.py:305
  90.2 7.3 %all_to_all.15 = f32[4,2,32]{2,1,0:T(2,128)S(1)} all-to-all(f32[4,2,32]{2,1,0:T(2,128)} %shard_map.130), channel_id=1, replica_groups={{0,8,16,24},{1,9,17,25},{2,10,18,26},{3,11,19,27},{4,12,20,28},{5,13,21..., dimensions={0} | all-to-all | bytes 2048 | tf_op jit(solution)/shard_map/all_to_all | solution.py:390
  97.5 0.6 add_divide_fusion
  (35 shorter events, 0.1 us)
Async XLA Ops:
  6.5 23.8 %copy-start = (bf16[512,256]{1,0:T(8,128)(2,1)S(1)}, bf16[512,256]{1,0:T(8,128)(2,1)}, u32[]{:S(2)}) copy-start(bf16[512,256]{1,0:T(8,128)(2,1)} %param.20) | copy-start | bytes 786436
  6.5 77.8 %all-gather.3.cloned.1.call-start = ((), (), s32[]{:S(2)}) async-start(), calls=%async_computation.3 | async-start | bytes 8634368 | tf_op jit(solution)/shard_map/all_gather | solution.py:353
  15.9 28.0 %all-to-all-start = ((bf16[32,2,32,128]{3,2,1,0:T(8,128)(2,1)}), bf16[32,2,32,128]{3,2,1,0:T(8,128)(2,1)S(1)}, u32[]{:S(2)}, u32[]{:S(2)}) async-start(bf16[32,2,32,128]{3,2,1,0:T(8,128)(2,1)} %shard_map.127), calls=%async_computation | async-start | bytes 1048576 | tf_op jit(solution)/shard_map/all_to_all | solution.py:359
  75.7 8.6 %all-to-all-start.1 = ((bf16[4,32,640]{2,1,0:T(8,128)(2,1)}), bf16[4,32,640]{2,1,0:T(8,128)(2,1)S(1)}, u32[]{:S(2)}, u32[]{:S(2)}) async-start(bf16[4,32,640]{2,1,0:T(8,128)(2,1)} %broadcast_in_dim.7), calls=%async_computation.1 | async-start | bytes 327680 | tf_op jit(solution)/shard_map/all_to_all | solution.py:379
Sparse Core Ops, SparseCore 0:
  9.5 65.7 all-gather.2

commit v10 on v8

--- a/solution.py
+++ b/solution.py
@@ -32,9 +32,9 @@
 
 
 def pool_kernel(map_ref, owner_ref, *refs):
-    slot_count = len(refs) - 6
+    slot_count = len(refs) - 8
     ids_refs = refs[:slot_count]
-    len_ref, table_ref, out_ref, cnt_ref, local_ref, sem = refs[slot_count:]
+    len_ref, table_ref, out_ref, cnt_ref, local_ref, rows_ref, sem, sems = refs[slot_count:]
     vocab = table_ref.shape[1]
     hi_count = vocab // LO
     height = hi_count * ROWBLK
@@ -56,6 +56,7 @@
         row = jnp.broadcast_to(row, (16, 128)).astype(jnp.bfloat16)
         return jnp.where(row[None] == wanted, one, zero).reshape(-1, 128)
 
+    sends = []
     for slot in range(slot_count):
         feat = find_feature(slot, map_ref, owner_ref)
         lens = jnp.sum(jnp.where(feat_pos == feat, len_ref[...], 0), axis=0, keepdims=True)
@@ -96,9 +97,12 @@
                 local_ref[slot],
                 preferred_element_type=jnp.float32,
             ).astype(jnp.bfloat16)
-            out_ref[start // row_count : (start + TILE) // row_count, slot] = pooled.reshape(
-                TILE // row_count, row_count, out_ref.shape[3]
-            )
+            first, last = start // row_count, (start + TILE) // row_count
+            rows_ref[slot, first:last] = pooled.reshape(last - first, row_count, out_ref.shape[3])
+        sends.append(pltpu.make_async_copy(rows_ref.at[slot], out_ref.at[:, slot], sems.at[slot]))
+        sends[-1].start()
+    for send in sends:
+        send.wait()
 
 
 def find_feature(slot, map_ref, owner_ref):
@@ -126,13 +130,13 @@
                 pl.BlockSpec((feats, span), lambda i, m, o: (0, 0)),
                 pl.BlockSpec(memory_space=pl.ANY),
             ],
-            out_specs=pl.BlockSpec(
-                (owners, slot_count, row_count, dim), lambda i, m, o: (0, 0, 0, 0)
-            ),
+            out_specs=pl.BlockSpec(memory_space=pl.ANY),
             scratch_shapes=[
                 pltpu.VMEM((slot_count, span, vocab), jnp.bfloat16),
                 pltpu.VMEM(tables.shape, jnp.bfloat16),
+                pltpu.VMEM((slot_count, owners, row_count, dim), jnp.bfloat16),
                 pltpu.SemaphoreType.DMA(()),
+                pltpu.SemaphoreType.DMA((slot_count,)),
             ],
         ),
         out_shape=jax.ShapeDtypeStruct((owners, slot_count, row_count, dim), jnp.bfloat16),

time: 103 us -> 103 us (level)
  no operation moved by 1% of the time
where the time goes in v10:
time: 103 us; the launch traced here: 102 us
  blocking collectives  32.3 us (31%)
  starting transfers between devices  17.1 us (17%)
  waiting for transfers between devices  15.5 us (15%)
  Pallas kernels  15.1 us (15%)
  between operations  13.8 us (13%)
  matrix products  3.92 us (4%)
  other arithmetic  2.7 us (3%)
  local copies, waits for them, and re-layouts  1.1 us (1%)
    all_gather x1, blocking collectives, local(): gathered = lax.all_gather(embedded[:NPERM], 'grp', axis=1, tiled=True)  25.1 us
    all_to_all x1, starting transfers between devices, local(): lax.all_to_all(pooled, 'tbl', split_axis=0, concat_axis=0, tiled=True)  13.7 us
    all_to_all x1, waiting for transfers between devices, local(): lax.all_to_all(pooled, 'tbl', split_axis=0, concat_axis=0, tiled=True)  11.6 us
    pallas_call x1, Pallas kernels, pool_slots(): pl.pallas_call(pool_kernel, grid_spec=pltpu.PrefetchScalarGridSpec(num_sc...  7.43 us
    all_to_all x1, blocking collectives, local(): lax.all_to_all(part, 'tbl', split_axis=0, concat_axis=0, tiled=True, axis...  7.28 us
    pallas_call x1, Pallas kernels, top_layers(): pl.pallas_call(top_kernel, grid=(steps,), in_specs=[pl.BlockSpec(memory_s...  5.84 us
    all_to_all x1, waiting for transfers between devices, local(): lax.all_to_all(jnp.broadcast_to(codes[None], (xs, *codes.shape)), 'tbl',...  3.93 us
    all_to_all x1, starting transfers between devices, local(): lax.all_to_all(jnp.broadcast_to(codes[None], (xs, *codes.shape)), 'tbl',...  3.34 us
  transfers between devices with their start and end apart: 3, of which 2 were waited for; matrix products, arithmetic and copies ran while one was open for 7% of the time, Pallas kernels for 7%

profile of v10, /device:TPU:1, one launch (start us, length us, event | category | flops | bytes accessed | tf_op | source)
XLA Modules:
  0.0 101.6 jit_solution(12376656011954195545)
XLA Ops:
  6.5 0.0 copy-start
  6.5 0.0 all-gather.3.cloned.1.call-start
  6.5 1.9 %shard_map.128 = bf16[992,256]{1,0:T(8,128)(2,1)} custom-call(s32[1]{0:T(128)} %bitcast.37.part_ref, bf16[480,256]{1,0:T(8,128)(2,1)} %one_ref.1, bf16[256,2048]{1,0:T(8,128)(2,1)} %two_ref.1), custom_call_target="tpu_custom_call" | custom-call | tf_op jit(solution)/shard_map/pallas_call | solution.py:181
  8.4 0.0 all-gather.3.cloned.1.call-update
  8.5 7.4 %shard_map.127 = bf16[32,2,32,128]{3,2,1,0:T(8,128)(2,1)} custom-call(s32[26]{0:T(128)} %map_ref.1, s32[1]{0:T(128)} %bitcast.2.owner_ref, s32[26,8,1024]{2,1,0:T(8,128)} %bitcast.84, s32[26,8,1024]{2,1,0:T(8,128)} %bitcast.85, s32[26,1024]{1,0:T(8,128)} %refs_2_.1, bf16[2,2048,128]{2,1,0:T(8,128)(2,1)} %refs_3_.1), custom_call_target="tpu_custom_call" | custom-call | tf_op jit(solution)/shard_map/pallas_call | solution.py:123
  15.9 13.7 %all-to-all-start = ((bf16[32,2,32,128]{3,2,1,0:T(8,128)(2,1)}), bf16[32,2,32,128]{3,2,1,0:T(8,128)(2,1)S(1)}, u32[]{:S(2)}, u32[]{:S(2)}) async-start(bf16[32,2,32,128]{3,2,1,0:T(8,128)(2,1)} %shard_map.127), calls=%async_computation | async-start | bytes 1048576 | tf_op jit(solution)/shard_map/all_to_all | solution.py:335
  29.6 0.0 copy-done
  29.6 1.0 %fusion.3 = bf16[32,256]{1,0:T(8,128)(2,1)S(1)} fusion(bf16[512,256]{1,0:T(8,128)(2,1)S(1)} %copy-done, bf16[32,13]{0,1:T(8,128)(2,1)} %param.13, bf16[13,512]{1,0:T(8,128)(2,1)} %param.19), kind=kOutput, calls=%fused_computation.6 | convolution fusion | flops 8863744 | bytes 292672 | tf_op jit(solution)/shard_map/dot_general | solution.py:17
  30.7 1.0 fusion.4
  31.7 0.7 fusion.41
  32.3 11.6 %all-to-all-done = bf16[32,2,32,128]{3,2,1,0:T(8,128)(2,1)S(1)} async-done(((bf16[32,2,32,128]{3,2,1,0:T(8,128)(2,1)}), bf16[32,2,32,128]{3,2,1,0:T(8,128)(2,1)S(1)}, u32[]{:S(2)}, u32[]{:S(2)}) %all-to-all-start) | async-done | bytes 524320 | tf_op jit(solution)/shard_map/all_to_all | solution.py:335
  43.9 0.9 convolution_convert_fusion
  44.9 0.1 slice.159
  45.0 25.1 %all_gather.9 = bf16[4,512,128]{2,0,1:T(4,128)(2,1)S(1)} all-gather(bf16[4,32,128]{2,0,1:T(4,128)(2,1)S(1)} %slice.182), channel_id=1, replica_groups=mesh['grp'=16,'tbl'=32] {'grp'}, dimensions={1}, use_global_device_ids=true | all-gather | bytes 557056 | tf_op jit(solution)/shard_map/all_gather | solution.py:347
  70.0 0.2 convolution_convert_fusion.1
  70.3 0.3 fusion.10
  70.5 0.3 fusion.7
  70.8 0.2 fusion.13
  71.3 0.1 concatenate.27
  71.6 0.1 fusion.36
  71.7 0.7 broadcast_in_dim.7
  72.4 3.3 %all-to-all-start.1 = ((bf16[4,32,640]{2,1,0:T(8,128)(2,1)}), bf16[4,32,640]{2,1,0:T(8,128)(2,1)S(1)}, u32[]{:S(2)}, u32[]{:S(2)}) async-start(bf16[4,32,640]{2,1,0:T(8,128)(2,1)} %broadcast_in_dim.7), calls=%async_computation.1 | async-start | bytes 327680 | tf_op jit(solution)/shard_map/all_to_all | solution.py:360
  75.7 1.3 %dynamic-slice_convert_fusion = f32[512]{0:T(512)} fusion(bf16[2048]{0:T(1024)(128)(2,1)} %param.24, s32[]{:T(128)S(6)} %select_n.22), kind=kLoop, calls=%fused_computation.85 | loop fusion | flops 512 | bytes 3076 | tf_op jit(solution)/shard_map/convert_element_type | solution.py:370
  77.1 3.9 %all-to-all-done.1.codes_ref = bf16[4,32,640]{2,1,0:T(8,128)(2,1)S(1)} async-done(((bf16[4,32,640]{2,1,0:T(8,128)(2,1)}), bf16[4,32,640]{2,1,0:T(8,128)(2,1)S(1)}, u32[]{:S(2)}, u32[]{:S(2)}) %all-to-all-start.1) | async-done | bytes 163872 | tf_op jit(solution)/shard_map/all_to_all | solution.py:360
  81.0 0.0 all-gather.3.cloned.1.call-done
  81.0 5.8 %shard_map.129 = f32[4,2,32]{2,1,0:T(2,128)} custom-call(bf16[4,32,640]{2,1,0:T(8,128)(2,1)S(1)} %all-to-all-done.1.codes_ref, s32[1,512]{1,0:T(1,128)} %constant.77.cols_ref, bf16[16,992,256]{2,1,0:T(8,128)(2,1)} %bitcast.83, f32[1,512]{1,0:T(1,128)} %bitcast.89), custom_call_target="tpu_custom_call" | custom-call | tf_op jit(solution)/shard_map/pallas_call | solution.py:281
  86.9 7.3 %all_to_all.15 = f32[4,2,32]{2,1,0:T(2,128)S(1)} all-to-all(f32[4,2,32]{2,1,0:T(2,128)} %shard_map.129), channel_id=1, replica_groups={{0,8,16,24},{1,9,17,25},{2,10,18,26},{3,11,19,27},{4,12,20,28},{5,13,21..., dimensions={0} | all-to-all | bytes 2048 | tf_op jit(solution)/shard_map/all_to_all | solution.py:371
  94.2 0.6 add_divide_fusion
  (38 shorter events, 0.2 us)
Async XLA Ops:
  6.5 23.1 %copy-start = (bf16[512,256]{1,0:T(8,128)(2,1)S(1)}, bf16[512,256]{1,0:T(8,128)(2,1)}, u32[]{:S(2)}) copy-start(bf16[512,256]{1,0:T(8,128)(2,1)} %param.20) | copy-start | bytes 786436
  6.5 74.5 %all-gather.3.cloned.1.call-start = ((), (), s32[]{:S(2)}) async-start(), calls=%async_computation.3 | async-start | bytes 8634368 | tf_op jit(solution)/shard_map/all_gather | solution.py:329
  15.9 28.0 %all-to-all-start = ((bf16[32,2,32,128]{3,2,1,0:T(8,128)(2,1)}), bf16[32,2,32,128]{3,2,1,0:T(8,128)(2,1)S(1)}, u32[]{:S(2)}, u32[]{:S(2)}) async-start(bf16[32,2,32,128]{3,2,1,0:T(8,128)(2,1)} %shard_map.127), calls=%async_computation | async-start | bytes 1048576 | tf_op jit(solution)/shard_map/all_to_all | solution.py:335
  72.4 8.6 %all-to-all-start.1 = ((bf16[4,32,640]{2,1,0:T(8,128)(2,1)}), bf16[4,32,640]{2,1,0:T(8,128)(2,1)S(1)}, u32[]{:S(2)}, u32[]{:S(2)}) async-start(bf16[4,32,640]{2,1,0:T(8,128)(2,1)} %broadcast_in_dim.7), calls=%async_computation.1 | async-start | bytes 327680 | tf_op jit(solution)/shard_map/all_to_all | solution.py:360
Sparse Core Ops, SparseCore 0:
  9.5 65.7 all-gather.2
